TPU v7x, 128 devices: a whole 4x4x4 slice. The times are simulated.
128 devices in a mesh: head: 4 (over x_lo, core), batch: 32 (over y, z, x_hi).
Axes of the slice: x: 4 (x_hi: 2, x_lo: 2; x = x_hi * 2 + x_lo), y: 4, z: 4, core: 2. Of those that a mesh axis runs over, the one named last changes fastest.
Arguments:
- embedded: bfloat16 [4, 512, 2048], P(None, 'batch'), may hold values from -6 to 6
- states: bfloat16 [512, 32, 128, 128], P('batch', 'head'), may hold values from -6 to 6
- w_query: bfloat16 [2048, 2048], P(None, 'head'), may hold values from -0.125 to 0.125
- w_key: bfloat16 [2048, 2048], P(None, 'head'), may hold values from -0.125 to 0.125
- w_value: bfloat16 [2048, 4096], P(None, 'head'), may hold values from -0.125 to 0.125
- w_output_gate: bfloat16 [2048, 4096], P(None, 'head'), may hold values from -0.125 to 0.125
- w_beta: bfloat16 [2048, 32], P(None, 'head'), may hold values from -0.125 to 0.125
- w_decay: bfloat16 [2048, 32], P(None, 'head'), may hold values from -0.125 to 0.125
- decay_rate: float32 [32], replicated, may hold values from 0.05 to 4
- decay_bias: float32 [32], replicated, may hold values from -3 to 1
- head_gain: float32 [128], replicated, may hold values from 0.5 to 1.5
- input_gain: float32 [2048], replicated, may hold values from 0.5 to 1.5
- w_out: bfloat16 [4096, 2048], P('head'), may hold values from -0.09375 to 0.09375
- final_gain: float32 [2048], replicated, may hold values from 0.5 to 1.5
- lm_head: bfloat16 [2048, 131072], P(None, ('head', 'batch')), may hold values from -1 to 1
- targets: int32 [512, 4], replicated, may hold values from 0 to 131071
- active: int32 [512, 4], replicated, may hold values 0 or 1
Outputs:
- scores: float32 [512, 4], P('batch')
All inputs are finite; a program needn't handle non-finite values.
Results may differ from a plain program's by a relative error of at most 0.0022.
Values may be sent and summed in bfloat16 or wider, within the bound.
No kernel may reach another device: no remote copies, remote signals or barrier semaphores. Data moves between devices by JAX's collectives and lax.ppermute only.
A program may use at most 128 MiB of HBM per device.

v0:
```python
import jax
import jax.numpy as jnp
from jax import lax
from jax.sharding import Mesh
from jax.sharding import PartitionSpec as P

DK = 128
DV = 128
HEAD = ("head_0", "head_1")
BATCH = ("batch_0", "batch_1", "batch_2")
HEAD_BATCH = ("head_0", "head_1", "batch_0", "batch_1", "batch_2")


EPS = 1e-06


def from_everyone(array, axis):
    peers = lax.axis_size(axis)
    return lax.all_to_all(
        jnp.broadcast_to(array[None], (peers, *array.shape)), axis, 0, 0, tiled=True
    )


def of_everyone(array, axis):
    everything = from_everyone(array, axis)
    return jnp.sum(everything.astype(jnp.float32), axis=0)


def by_axis(array, axes):
    for axis in axes:
        array = lax.psum(array, axis)
    return array


def rms_scale(values, gain):
    values = values.astype(jnp.float32)
    return values * lax.rsqrt(jnp.mean(values * values, axis=-1, keepdims=True) + EPS) * gain


def unit_rows(values):
    return values * lax.rsqrt(jnp.sum(values * values, axis=-1, keepdims=True) + EPS)


def prepare(query_vector, key, value, beta_raw, decay_raw, rate, offset):
    rows, heads = beta_raw.shape
    query_float = unit_rows(
        query_vector.astype(jnp.float32).reshape(rows, heads // 2, DK)
    ) * DK ** (-0.5)
    key_f = unit_rows(key.astype(jnp.float32).reshape(rows, heads // 2, DK))
    value_f = value.astype(jnp.float32).reshape(rows, heads, DV)
    beta = jax.nn.sigmoid(beta_raw.astype(jnp.float32))
    decay = jnp.exp(-rate * jax.nn.softplus(decay_raw.astype(jnp.float32) + offset))
    return (jnp.repeat(query_float, 2, axis=1), jnp.repeat(key_f, 2, axis=1), value_f, beta, decay)


def recur(state, query_vector, key, value, beta, decay, marks):
    decayed_state = state * decay[:, :, None, None]
    retrieved_value = jnp.einsum(
        "rhk,rhkv->rhv", key, decayed_state, precision=lax.Precision.HIGHEST
    )
    update = beta[:, :, None] * (value - retrieved_value)
    corrected_state = decayed_state + key[:, :, :, None] * update[:, :, None, :]
    state_readout = jnp.einsum(
        "rhk,rhkv->rhv", query_vector, corrected_state, precision=lax.Precision.HIGHEST
    )
    kept = jnp.where(marks[:, None, None, None] > 0, corrected_state, state)
    return (kept, state_readout)


def gated_rms_norm(state_readout, gate, head_gain):
    rows, heads, width = state_readout.shape
    normed = (
        state_readout
        * lax.rsqrt(jnp.mean(state_readout * state_readout, axis=-1, keepdims=True) + EPS)
        * head_gain
    )
    gate_f = gate.astype(jnp.float32).reshape(rows, heads, width)
    return (normed * jax.nn.silu(gate_f)).astype(jnp.bfloat16).reshape(rows, heads * width)


def per_device(
    embedded,
    states,
    w_query,
    w_key,
    w_value,
    w_output_gate,
    w_beta,
    w_decay,
    decay_rate,
    decay_bias,
    head_gain,
    input_gain,
    w_out,
    final_gain,
    lm_head,
    targets,
    active,
):
    head_index = lax.axis_index(HEAD)
    batch_index = lax.axis_index(BATCH)
    batch_count = lax.axis_size(BATCH)
    steps, group, width = embedded.shape
    local_heads = w_beta.shape[1]
    slice_cols = lm_head.shape[1]
    vocab_start = lax.axis_index(HEAD_BATCH) * slice_cols
    group_marks = lax.dynamic_slice_in_dim(active, batch_index * group, group, 0)
    state = states.astype(jnp.float32)
    rate = lax.dynamic_slice_in_dim(decay_rate, head_index * local_heads, local_heads, 0)
    offset = lax.dynamic_slice_in_dim(decay_bias, head_index * local_heads, local_heads, 0)
    vocab_iota = lax.broadcasted_iota(jnp.int32, (1, slice_cols), 1)
    gathered_mixed = []
    collected = []
    for step in range(steps):
        tokens = embedded[step]
        normed = rms_scale(tokens, input_gain).astype(jnp.bfloat16)
        query_vector = jnp.dot(normed, w_query, preferred_element_type=jnp.float32).astype(
            jnp.bfloat16
        )
        key = jnp.dot(normed, w_key, preferred_element_type=jnp.float32).astype(jnp.bfloat16)
        value = jnp.dot(normed, w_value, preferred_element_type=jnp.float32).astype(jnp.bfloat16)
        gate = jnp.dot(normed, w_output_gate, preferred_element_type=jnp.float32).astype(
            jnp.bfloat16
        )
        beta_raw = jnp.dot(normed, w_beta, preferred_element_type=jnp.float32).astype(jnp.bfloat16)
        decay_raw = jnp.dot(normed, w_decay, preferred_element_type=jnp.float32).astype(
            jnp.bfloat16
        )
        q_f, k_f, v_f, beta, decay = prepare(
            query_vector, key, value, beta_raw, decay_raw, rate, offset
        )
        state, state_readout = recur(state, q_f, k_f, v_f, beta, decay, group_marks[:, step])
        mixed = gated_rms_norm(state_readout, gate, head_gain)
        gathered_mixed.append(mixed)
    mixed_steps = jnp.stack(gathered_mixed, 0)
    count = steps - 0
    heads_width = mixed_steps.shape[2]
    partial_value = jnp.dot(
        mixed_steps.reshape(count * group, heads_width), w_out, preferred_element_type=jnp.float32
    )
    summed = of_everyone(partial_value.astype(jnp.bfloat16), HEAD).astype(jnp.float32)
    hidden = rms_scale(
        embedded.reshape(count * group, width).astype(jnp.float32) + summed, final_gain
    ).astype(jnp.bfloat16)
    ordered = targets.reshape(batch_count, group, count).transpose(0, 2, 1).reshape(-1)
    logits = jnp.dot(
        lax.all_gather(hidden, BATCH, axis=0, tiled=True),
        lm_head,
        preferred_element_type=jnp.float32,
    )
    total = jnp.sum(jnp.exp(logits), axis=1)
    wanted = ordered - vocab_start
    picked = jnp.sum(jnp.where(vocab_iota == wanted[:, None], logits, 0.0), axis=1)
    stats = jnp.stack([total, picked], 0)
    stats = by_axis(stats, HEAD_BATCH)
    stats = lax.dynamic_slice_in_dim(
        stats.reshape(2, batch_count, count, group), batch_index, 1, 1
    ).reshape(2, count, group)
    marks = group_marks.T
    collected = [jnp.where(marks > 0, stats[1] - jnp.log(stats[0]), 0.0).T]
    return collected[0]


def solution(mesh):
    finer = Mesh(
        mesh.devices.reshape(2, 2, 4, 4, 2), ("head_0", "head_1", "batch_0", "batch_1", "batch_2")
    )
    return jax.shard_map(
        per_device,
        mesh=finer,
        in_specs=(
            P(None, BATCH, None),
            P(BATCH, HEAD, None, None),
            P(None, HEAD),
            P(None, HEAD),
            P(None, HEAD),
            P(None, HEAD),
            P(None, HEAD),
            P(None, HEAD),
            P(),
            P(),
            P(),
            P(),
            P(HEAD, None),
            P(),
            P(None, HEAD_BATCH),
            P(),
            P(),
        ),
        out_specs=P(BATCH, None),
        check_vma=False,
    )
```

profile of v0, /device:TPU:0, one launch (start us, length us, event | category | flops | bytes accessed | tf_op | source)
XLA Modules:
  0.0 318.8 jit_solution(9498516063745830640)
XLA Ops:
  6.6 0.9 dynamic-slice_negate_fusion
  7.5 1.1 dynamic_slice.14
  8.6 1.1 fusion.109
  9.7 1.3 fusion.70
  11.0 1.1 fusion.140
  12.1 1.1 fusion.142
  13.2 1.3 fusion.68
  14.4 2.9 fusion.63
  19.2 0.7 fusion.55
  20.8 0.7 fusion.51
  23.4 0.7 fusion.61
  24.1 0.7 fusion.57
  24.8 0.7 fusion.53
  28.1 8.9 %fusion.1 = f32[16,8,1,128]{3,2,1,0:T(1,128)S(1)} fusion(f32[16,8,128,1]{2,3,1,0:T(1,128)S(1)} %bitcast.264, bf16[16,8,128,128]{3,2,1,0:T(8,128)(2,1)} %param.18, f32[16,8]{1,0:T(8,128)S(1)} %copy.35), kind=kOutput, calls=%fused_computation.3 | convolution fusion | flops 29360128 | bytes 4325888 | tf_op jit(solution)/shard_map/rhk,rhkv->rhv/dot_general | solution.py:58
  37.1 10.3 %fusion.9 = f32[16,8,1,128]{3,2,1,0:T(1,128)S(1)} fusion(f32[16,8,128,1]{2,3,1,0:T(1,128)S(1)} %bitcast.269, bf16[16,8,128,128]{3,2,1,0:T(8,128)(2,1)} %param.18, f32[16,8]{1,0:T(8,128)S(1)} %copy.37, f32[16,8,128]{2,1,0:T(8,128)S(1)} %fusion.134, f32[16,8,128]{2,1,0:T(8,128)S(1)} %bitcast.265, f32[16,8]{1,0:T(8,128)S(1)} %copy.35, ...), kind=kOutput, calls=%fused_computation.16 | convolution fusion | flops 37748736 | bytes 4457488 | tf_op jit(solution)/shard_map/rhk,rhkv->rhv/dot_general | solution.py:58
  47.5 5.7 %fusion.7 = f32[16,8,128,128]{3,2,1,0:T(8,128)S(1)} fusion(bf16[16,8,128,128]{3,2,1,0:T(8,128)(2,1)S(1)} %copy-done.6, f32[16,8,128]{2,1,0:T(8,128)S(1)} %fusion.129, f32[16,8,128]{2,1,0:T(8,128)S(1)} %bitcast.270, f32[16,8]{1,0:T(8,128)S(1)} %copy.37, f32[16,8,128]{2,1,0:T(8,128)S(1)} %fusion.134, f32[16,8,128]{2,1,0:T(8,128)S(1)} %bitcast.266, ...), kind=kLoop, calls=%fused_computation.14 | loop fusion | flops 18874368 | bytes 12846112 | tf_op jit(solution)/shard_map/jit(_where)/select_n | solution.py:66
  53.3 7.1 %fusion.12 = f32[16,8,1,128]{3,2,1,0:T(1,128)S(1)} fusion(f32[16,8,128,1]{2,3,1,0:T(1,128)S(1)} %bitcast.256, f32[16,8,128,128]{3,2,1,0:T(8,128)S(1)} %fusion.7, f32[16,8]{1,0:T(8,128)S(1)} %copy.39), kind=kOutput, calls=%fused_computation.18 | convolution fusion | flops 27262976 | bytes 8520192 | tf_op jit(solution)/shard_map/rhk,rhkv->rhv/dot_general | solution.py:58
  60.5 8.5 %fusion.15 = f32[16,8,1,128]{3,2,1,0:T(1,128)S(1)} fusion(f32[16,8,128,1]{2,3,1,0:T(1,128)S(1)} %bitcast.283, f32[16,8,128,128]{3,2,1,0:T(8,128)S(1)} %fusion.7, f32[16,8]{1,0:T(8,128)S(1)} %copy.41, f32[16,8,128]{2,1,0:T(8,128)S(1)} %fusion.124, f32[16,8,128]{2,1,0:T(8,128)S(1)} %bitcast.257, f32[16,8]{1,0:T(8,128)S(1)} %copy.39, ...), kind=kOutput, calls=%fused_computation.21 | convolution fusion | flops 35651584 | bytes 8651792 | tf_op jit(solution)/shard_map/rhk,rhkv->rhv/dot_general | solution.py:58
  69.1 11.5 %fusion.2 = f32[16,8,1,128]{3,2,1,0:T(1,128)S(1)} fusion(f32[16,8,128,1]{2,3,1,0:T(1,128)S(1)} %bitcast.285, f32[16,8,128,128]{3,2,1,0:T(8,128)S(1)} %fusion.7, f32[16,8,128]{2,1,0:T(8,128)S(1)} %fusion.119, f32[16,8,128]{2,1,0:T(8,128)S(1)} %bitcast.284, f32[16,8]{1,0:T(8,128)S(1)} %copy.41, f32[16,8,128]{2,1,0:T(8,128)S(1)} %fusion.124, ...), kind=kOutput, calls=%fused_computation.7 | convolution fusion | flops 39845888 | bytes 8782864 | tf_op jit(solution)/shard_map/rhk,rhkv->rhv/dot_general | solution.py:63
  81.0 10.3 %fusion.14 = f32[16,8,1,128]{3,2,1,0:T(1,128)S(1)} fusion(f32[16,8,128,1]{2,3,1,0:T(1,128)S(1)} %bitcast.272, f32[16,8,128,128]{3,2,1,0:T(8,128)} %copy-done.1, f32[16,8,128]{2,1,0:T(8,128)S(1)} %fusion.124, f32[16,8,128]{2,1,0:T(8,128)S(1)} %bitcast.259, f32[16,8]{1,0:T(8,128)S(1)} %copy.39), kind=kOutput, calls=%fused_computation.20 | convolution fusion | flops 31457280 | bytes 8651264 | tf_op jit(solution)/shard_map/rhk,rhkv->rhv/dot_general | solution.py:63
  91.7 12.6 %fusion.11 = f32[16,8,1,128]{3,2,1,0:T(1,128)S(1)} fusion(f32[16,8,128,1]{2,3,1,0:T(1,128)S(1)} %bitcast.286, bf16[16,8,128,128]{3,2,1,0:T(8,128)(2,1)} %param.18, f32[16,8,128]{2,1,0:T(8,128)S(1)} %fusion.129, f32[16,8,128]{2,1,0:T(8,128)S(1)} %bitcast.271, f32[16,8]{1,0:T(8,128)S(1)} %copy.37, f32[16,8,128]{2,1,0:T(8,128)S(1)} %fusion.134, ...), kind=kOutput, calls=%fused_computation.17 | convolution fusion | flops 41943040 | bytes 4588560 | tf_op jit(solution)/shard_map/rhk,rhkv->rhv/dot_general | solution.py:63
  104.6 9.8 %fusion.5 = f32[16,8,1,128]{3,2,1,0:T(1,128)S(1)} fusion(f32[16,8,128,1]{2,3,1,0:T(1,128)S(1)} %bitcast.287, bf16[16,8,128,128]{3,2,1,0:T(8,128)(2,1)} %param.18, f32[16,8,128]{2,1,0:T(8,128)S(1)} %fusion.134, f32[16,8,128]{2,1,0:T(8,128)S(1)} %bitcast.268, f32[16,8]{1,0:T(8,128)S(1)} %copy.35), kind=kOutput, calls=%fused_computation.13 | convolution fusion | flops 33554432 | bytes 4456960 | tf_op jit(solution)/shard_map/rhk,rhkv->rhv/dot_general | solution.py:63
  115.0 3.0 convolution_convert_fusion
  118.1 17.1 %all_to_all.5 = bf16[4,64,2048]{2,1,0:T(8,128)(2,1)S(1)} all-to-all(bf16[4,64,2048]{2,1,0:T(8,128)(2,1)S(1)} %broadcast_in_dim.53), channel_id=1, replica_groups=mesh['head_0'=2,'head_1'=2,'batch_0'=4,'batch_1'=4,'batch_2'=2] {'head_0..., dimensions={0} | all-to-all | bytes 2097152 | tf_op jit(solution)/shard_map/all_to_all | solution.py:19
  135.7 0.8 fusion.102
  136.8 105.9 %all-gather.2.cloned.1.call-done = bf16[2048,2048]{1,0:T(8,128)(2,1)} async-done(((bf16[64,2048]{1,0:T(8,128)(2,1)}), bf16[2048,2048]{1,0:T(8,128)(2,1)}) %all-gather.2.cloned.1.call-update) | async-done | bytes 8388624 | tf_op jit(solution)/shard_map/all_gather | solution.py:147
  242.7 13.9 %exponential_reduce_fusion = (f32[2048]{0:T(1024)S(1)}, f32[2048]{0:T(1024)S(1)}) fusion(s32[2048]{0:T(1024)S(1)} %sub.45, bf16[2048,2048]{1,0:T(8,128)(2,1)} %all-gather.2.cloned.1.call-done, bf16[2048,1024]{1,0:T(8,128)(2,1)} %param.31), kind=kOutput, calls=%fused_computation.6 | convolution fusion | flops 8598319104 | bytes 12607488 | tf_op jit(solution)/shard_map/dot_general | solution.py:146
  256.7 7.2 %psum.35 = f32[2,2048]{1,0:T(2,128)S(1)} all-reduce(f32[2,2048]{1,0:T(2,128)S(1)} %pad_maximum_fusion.1), channel_id=1, replica_groups=mesh['head_0'=2,'head_1'=2,'batch_0'=4,'batch_1'=4,'batch_2'=2] {'head_0'}, use_global_device_ids=true, to_apply=%region_20.21 | all-reduce | flops 4096 | bytes 32768 | tf_op jit(solution)/shard_map/psum | solution.py:31
  263.9 3.3 %psum.36 = f32[2,2048]{1,0:T(2,128)S(1)} all-reduce(f32[2,2048]{1,0:T(2,128)S(1)} %psum.35), channel_id=1, replica_groups=mesh['head_0'=2,'head_1'=2,'batch_0'=4,'batch_1'=4,'batch_2'=2] {'head_1'}, use_global_device_ids=true, to_apply=%region_21.22 | all-reduce | flops 4096 | bytes 32768 | tf_op jit(solution)/shard_map/psum | solution.py:31
  267.3 15.5 %psum.37 = f32[2,2048]{1,0:T(2,128)S(1)} all-reduce(f32[2,2048]{1,0:T(2,128)S(1)} %psum.36), channel_id=1, replica_groups=mesh['head_0'=2,'head_1'=2,'batch_0'=4,'batch_1'=4,'batch_2'=2] {'batch_0'}, use_global_device_ids=true, to_apply=%region_22.23 | all-reduce | flops 4096 | bytes 32768 | tf_op jit(solution)/shard_map/psum | solution.py:31
  282.7 16.6 %psum.38 = f32[2,2048]{1,0:T(2,128)S(1)} all-reduce(f32[2,2048]{1,0:T(2,128)S(1)} %psum.37), channel_id=1, replica_groups=mesh['head_0'=2,'head_1'=2,'batch_0'=4,'batch_1'=4,'batch_2'=2] {'batch_1'}, use_global_device_ids=true, to_apply=%region_23.24 | all-reduce | flops 4096 | bytes 32768 | tf_op jit(solution)/shard_map/psum | solution.py:31
  299.5 11.7 %psum.39 = f32[2,32,4,16]{3,2,1,0:T(4,128)S(1)} all-reduce(f32[2,32,4,16]{3,2,1,0:T(4,128)S(1)} %reshape.363), channel_id=1, replica_groups=mesh['head_0'=2,'head_1'=2,'batch_0'=4,'batch_1'=4,'batch_2'=2] {'batch_2'}, use_global_device_ids=true, to_apply=%region_24.25 | all-reduce | flops 4096 | bytes 32768 | tf_op jit(solution)/shard_map/psum | solution.py:31
  (134 shorter events, 10.4 us)
Async XLA Ops:
  6.5 3.2 %copy-start = (bf16[2048,512]{1,0:T(8,128)(2,1)S(1)}, bf16[2048,512]{1,0:T(8,128)(2,1)}, u32[]{:S(2)}) copy-start(bf16[2048,512]{1,0:T(8,128)(2,1)} %param.20) | copy-start | bytes 6291460
  6.5 10.8 %copy-start.5 = (bf16[4,16,2048]{2,1,0:T(8,128)(2,1)S(1)}, bf16[4,16,2048]{2,1,0:T(8,128)(2,1)}, u32[]{:S(2)}) copy-start(bf16[4,16,2048]{2,1,0:T(8,128)(2,1)} %param.17) | copy-start | bytes 786436
  6.5 10.9 %copy-start.7 = (f32[2048]{0:T(1024)S(1)}, f32[2048]{0:T(1024)}, u32[]{:S(2)}) copy-start(f32[2048]{0:T(1024)} %param.28) | copy-start | bytes 24580
  6.5 12.0 %copy-start.12 = (bf16[2048,8]{0,1:T(8,128)(2,1)S(1)}, bf16[2048,8]{0,1:T(8,128)(2,1)}, u32[]{:S(2)}) copy-start(bf16[2048,8]{0,1:T(8,128)(2,1)} %param.24) | copy-start | bytes 98308
  6.5 11.6 %copy-start.13 = (bf16[2048,8]{0,1:T(8,128)(2,1)S(1)}, bf16[2048,8]{0,1:T(8,128)(2,1)}, u32[]{:S(2)}) copy-start(bf16[2048,8]{0,1:T(8,128)(2,1)} %param.23) | copy-start | bytes 98308
  6.5 236.2 %all-gather.2.cloned.1.call-start = ((), (), s32[]{:S(2)}) async-start(), calls=%async_computation.1 | async-start | bytes 8650752 | tf_op jit(solution)/shard_map/all_gather | solution.py:147
  6.6 10.8 %copy-start.2 = (bf16[2048,1024]{1,0:T(8,128)(2,1)S(1)}, bf16[2048,1024]{1,0:T(8,128)(2,1)}, u32[]{:S(2)}) copy-start(bf16[2048,1024]{1,0:T(8,128)(2,1)} %param.21) | copy-start | bytes 12582916
  17.4 4.3 %copy-start.4 = (bf16[2048,512]{1,0:T(8,128)(2,1)S(1)}, bf16[2048,512]{1,0:T(8,128)(2,1)}, u32[]{:S(2)}) copy-start(bf16[2048,512]{1,0:T(8,128)(2,1)} %param.19) | copy-start | bytes 6291460
  19.9 3.5 %copy-start.3 = (bf16[2048,1024]{1,0:T(8,128)(2,1)S(1)}, bf16[2048,1024]{1,0:T(8,128)(2,1)}, u32[]{:S(2)}) copy-start(bf16[2048,1024]{1,0:T(8,128)(2,1)} %param.22) | copy-start | bytes 12582916
  23.4 3.3 %copy-start.10 = (s32[512,4]{0,1:T(4,128)S(1)}, s32[512,4]{0,1:T(4,128)}, u32[]{:S(2)}) copy-start(s32[512,4]{0,1:T(4,128)} %param.33) | copy-start | bytes 24580
  37.0 10.6 %copy-start.6 = (bf16[16,8,128,128]{3,2,1,0:T(8,128)(2,1)S(1)}, bf16[16,8,128,128]{3,2,1,0:T(8,128)(2,1)}, u32[]{:S(2)}) copy-start(bf16[16,8,128,128]{3,2,1,0:T(8,128)(2,1)} %param.18) | copy-start | bytes 12582916
  53.3 15.9 %copy-start.1 = (f32[16,8,128,128]{3,2,1,0:T(8,128)}, f32[16,8,128,128]{3,2,1,0:T(8,128)S(1)}, u32[]{:S(2)}) copy-start(f32[16,8,128,128]{3,2,1,0:T(8,128)S(1)} %fusion.7) | copy-start | bytes 25165828
  104.3 10.4 %copy-start.11 = (f32[128]{0:T(128)S(1)}, f32[128]{0:T(128)}, u32[]{:S(2)}) copy-start(f32[128]{0:T(128)} %param.27) | copy-start | bytes 1540
  104.6 31.0 %copy-start.8 = (f32[2048]{0:T(1024)S(1)}, f32[2048]{0:T(1024)}, u32[]{:S(2)}) copy-start(f32[2048]{0:T(1024)} %param.30) | copy-start | bytes 24580
  114.5 22.1 %copy-start.9 = (s32[512,4]{0,1:T(4,128)S(1)}, s32[512,4]{0,1:T(4,128)}, u32[]{:S(2)}) copy-start(s32[512,4]{0,1:T(4,128)} %param.32) | copy-start | bytes 24580
Sparse Core Ops, SparseCore 0:
  136.6 106.0 all-gather.1
where the time goes:
time: 325 us; the launch traced here: 319 us
  matrix products  112 us (34%)
  waiting for transfers between devices  106 us (33%)
  blocking collectives  71.4 us (22%)
  between operations  14.3 us (4%)
  other arithmetic  11.9 us (4%)
    all_gather x1, waiting for transfers between devices, per_device(): lax.all_gather(hidden, BATCH, axis=0, tiled=True)  106 us
    psum x5, blocking collectives, by_axis(): array = lax.psum(array, axis)  54.3 us
    dot_general x4, matrix products, recur(): jnp.einsum('rhk,rhkv->rhv', query_vector, corrected_state, precision=lax....  44.2 us
    dot_general x4, matrix products, recur(): jnp.einsum('rhk,rhkv->rhv', key, decayed_state, precision=lax.Precision.H...  34.8 us
    all_to_all x1, blocking collectives, from_everyone(): lax.all_to_all(jnp.broadcast_to(array[None], (peers, *array.shape)), axis...  17.1 us
    dot_general x1, matrix products, per_device(): jnp.dot(lax.all_gather(hidden, BATCH, axis=0, tiled=True), lm_head, prefe...  13.9 us
  transfers between devices with their start and end apart: 1, of which 1 were waited for; matrix products, arithmetic and copies ran while one was open for 0% of the time, Pallas kernels for 0%

commit v1 on v0

v1 whole, which is shorter than its diff:
```python
import functools

import jax
import jax.numpy as jnp
import numpy as np
from jax import lax
from jax.experimental import pallas as pl
from jax.experimental.pallas import tpu as pltpu
from jax.sharding import Mesh
from jax.sharding import PartitionSpec as P

DK = 128
DV = 128
EPS = 1e-06
AXES = ("xl", "c", "y", "z", "xh")
SIZES = (2, 2, 4, 4, 2)
HEAD = ("xl", "c")
BATCH = ("y", "z", "xh")
DEVICES = 128
GROUPS = 32
F32 = jnp.float32
BF16 = jnp.bfloat16


def route(move):
    pairs = []
    for source in range(DEVICES):
        spot = [int(i) for i in np.unravel_index(source, SIZES)]
        pairs.append((source, int(np.ravel_multi_index(move(*spot), SIZES))))
    return pairs


def shift(first, second, hops):
    def move(xl, c, y, z, xh):
        if (first, second)[c] == "y":
            return (xl, c, (y + hops) % 4, z, xh)
        return (xl, c, y, (z + hops) % 4, xh)

    return route(move)


OTHER_CORE = route(lambda xl, c, y, z, xh: (xl, 1 - c, y, z, xh))
OTHER_LOW = route(lambda xl, c, y, z, xh: (1 - xl, c, y, z, xh))
OTHER_HIGH = route(lambda xl, c, y, z, xh: (xl, c, y, z, 1 - xh))
NEAR = [shift("y", "z", k) for k in (1, 3, 2)]
FAR = [shift("z", "y", k) for k in (1, 3, 2)]


def sources():
    held = [[d % GROUPS] for d in range(DEVICES)]
    for stage in ([OTHER_HIGH], NEAR, FAR):
        grown = [list(h) for h in held]
        for pairs in stage:
            for source, target in pairs:
                grown[target].extend(held[source])
        held = grown
    return np.array(held, np.int32)


def front_kernel(
    spot,
    rate,
    offset,
    embedded,
    states,
    w_query,
    w_key,
    w_value,
    w_gate,
    w_beta,
    w_decay,
    w_out,
    input_gain,
    head_gain,
    active,
    give,
    keep,
    normed,
    kq,
    reads,
    beta_all,
    decay_all,
    marks,
    mixed,
    total,
):
    step = pl.program_id(0)
    steps, group, width = embedded.shape
    rows = steps * group

    def contract_last(a, b):
        return lax.dot_general(a, b, (((1,), (1,)), ((), ())), preferred_element_type=F32)

    @pl.when(step == 0)
    def _():
        for t in range(steps):
            e = embedded[t].astype(F32)
            scale = lax.rsqrt(jnp.mean(e * e, axis=-1, keepdims=True) + EPS)
            normed[t * group : (t + 1) * group, :] = (e * scale * input_gain[...]).astype(BF16)
        n = normed[...]
        beta_raw = contract_last(n, w_beta[...]).astype(BF16).astype(F32)
        decay_raw = contract_last(n, w_decay[...]).astype(BF16).astype(F32)
        for h in range(w_beta.shape[0]):
            b = jnp.broadcast_to(beta_raw[:, h : h + 1], (rows, DV))
            d = jnp.broadcast_to(decay_raw[:, h : h + 1], (rows, DV))
            at = spot[1] * w_beta.shape[0] + h
            beta_all[h] = jax.nn.sigmoid(b)
            decay_all[h] = jnp.exp(-rate[at] * jax.nn.softplus(d + offset[at]))
        requests = active.shape[1]
        here = lax.broadcasted_iota(jnp.int32, (group, requests), 1) == (
            spot[0] * group + lax.broadcasted_iota(jnp.int32, (group, requests), 0)
        )
        for t in range(steps):
            line = jnp.broadcast_to(active[t : t + 1, :].astype(F32), (group, requests))
            column = jnp.sum(jnp.where(here, line, 0.0), axis=1, keepdims=True)
            marks[t] = jnp.broadcast_to(column, (group, DV))

    n = normed[...]

    def project(weight):
        return jnp.dot(n, weight[...], preferred_element_type=F32).astype(BF16).astype(F32)

    def unit(x):
        return x * lax.rsqrt(jnp.sum(x * x, axis=-1, keepdims=True) + EPS)

    kq[:rows, :] = unit(project(w_key))
    kq[rows:, :] = unit(project(w_query)) * DK ** (-0.5)
    value = project(w_value)
    gate = project(w_gate)
    k = [kq[t * group : (t + 1) * group, :] for t in range(steps)]
    q = [kq[rows + t * group : rows + (t + 1) * group, :] for t in range(steps)]

    def inner(a, b):
        return jnp.broadcast_to(jnp.sum(a * b, axis=-1, keepdims=True), (group, DV))

    kk = {(t, i): inner(k[t], k[i]) for t in range(steps) for i in range(t)}
    qk = {(t, i): inner(q[t], k[i]) for t in range(steps) for i in range(t + 1)}
    for r in range(group):
        lines = kq[pl.ds(r, 2 * steps, stride=group), :]
        high = lines.astype(BF16).astype(F32)
        both = jnp.concatenate([high, lines - high], axis=0).astype(BF16)
        for h in range(2):
            got = jnp.dot(both, states[r, h], preferred_element_type=F32)
            reads[h, pl.ds(r, 2 * steps, stride=group), :] = got[: 2 * steps] + got[2 * steps :]
    for h in range(2):
        head = 2 * step + h
        coefficient = []
        update = []
        for t in range(steps):
            at = slice(t * group, (t + 1) * group)
            decay = decay_all[head, at, :]
            beta = beta_all[head, at, :]
            mark = marks[t] > 0
            of_key = reads[h, at, :]
            of_query = reads[h, rows + t * group : rows + (t + 1) * group, :]
            if t > 0:
                of_key = start * of_key
                of_query = start * of_query
            for i in range(t):
                of_key = of_key + coefficient[i] * kk[t, i] * update[i]
                of_query = of_query + coefficient[i] * qk[t, i] * update[i]
            u = beta * (value[at, h * DV : (h + 1) * DV] - decay * of_key)
            readout = decay * of_query + qk[t, t] * u
            faded = jnp.where(mark, decay, 1.0)
            start = faded if t == 0 else start * faded
            coefficient = [old * faded for old in coefficient] + [jnp.where(mark, 1.0, 0.0)]
            update.append(u)
            scale = lax.rsqrt(jnp.mean(readout * readout, axis=-1, keepdims=True) + EPS)
            g = gate[at, h * DV : (h + 1) * DV]
            mixed[at, h * DV : (h + 1) * DV] = (
                readout * scale * head_gain[...] * (g * jax.nn.sigmoid(g))
            ).astype(BF16)
    part = jnp.dot(mixed[...], w_out[...], preferred_element_type=F32)

    @pl.when(step == 0)
    def _():
        total[...] = part

    @pl.when(step > 0)
    def _():
        total[...] += part

    @pl.when(step == pl.num_programs(0) - 1)
    def _():
        half = rows // 2
        c = spot[2]
        keep[...] = total[pl.ds(pl.multiple_of(c * half, half), half), :]
        give[...] = total[pl.ds(pl.multiple_of((1 - c) * half, half), half), :].astype(BF16)


def front(spot, rate, offset, embedded, states, wq, wk, wv, wg, wb, wd, wo, ig, hg, active):
    steps, group, width = embedded.shape
    rows, heads = steps * group, states.shape[1]
    key_heads = heads // 2
    whole = lambda *shape: pl.BlockSpec(shape, lambda j, *_: (0,) * len(shape))
    across = lambda cols: pl.BlockSpec((width, cols), lambda j, *_: (0, j))
    return pl.pallas_call(
        front_kernel,
        grid_spec=pltpu.PrefetchScalarGridSpec(
            num_scalar_prefetch=3,
            grid=(key_heads,),
            in_specs=[
                whole(steps, group, width),
                pl.BlockSpec((group, 2, DK, DV), lambda j, *_: (0, j, 0, 0)),
                across(DK),
                across(DK),
                across(2 * DV),
                across(2 * DV),
                whole(heads, width),
                whole(heads, width),
                pl.BlockSpec((2 * DV, width), lambda j, *_: (j, 0)),
                whole(1, width),
                whole(1, DV),
                whole(*active.shape),
            ],
            out_specs=[whole(rows // 2, width), whole(rows // 2, width)],
            scratch_shapes=[
                pltpu.VMEM((rows, width), BF16),
                pltpu.VMEM((2 * rows, DK), F32),
                pltpu.VMEM((2, 2 * rows, DV), F32),
                pltpu.VMEM((heads, rows, DV), F32),
                pltpu.VMEM((heads, rows, DV), F32),
                pltpu.VMEM((steps, group, DV), F32),
                pltpu.VMEM((rows, 2 * DV), BF16),
                pltpu.VMEM((rows, width), F32),
            ],
        ),
        out_shape=[
            jax.ShapeDtypeStruct((rows // 2, width), BF16),
            jax.ShapeDtypeStruct((rows // 2, width), F32),
        ],
        compiler_params=pltpu.CompilerParams(
            dimension_semantics=("arbitrary",), vmem_limit_bytes=32 << 20
        ),
        cost_estimate=pl.CostEstimate(
            flops=2 * rows * width * 4096, bytes_accessed=21 << 20, transcendentals=0
        ),
        name="front",
    )(spot, rate, offset, embedded, states, wq, wk, wv, wg, wb, wd, wo, ig, hg, active)


def score_kernel(bases, hidden, own, other, target, stats, totals, picks):
    step = pl.program_id(0)
    rows, cols = hidden.shape[0], own.shape[1]
    x = hidden[...]
    want = target[...]
    running = jnp.zeros((rows, 128), F32)
    found = jnp.zeros((rows, 128), F32)
    lane = lax.broadcasted_iota(jnp.int32, (rows, 128), 1)
    for which, weight in enumerate((own, other)):
        logits = jnp.dot(x, weight[...], preferred_element_type=F32)
        left = jnp.broadcast_to(want - (bases[which] + step * cols), (rows, 128)) - lane
        for s in range(cols // 128):
            part = logits[:, s * 128 : (s + 1) * 128]
            running = running + jnp.exp(part)
            found = found + jnp.where(left == s * 128, part, 0.0)

    @pl.when(step == 0)
    def _():
        totals[...] = running
        picks[...] = found

    @pl.when(step > 0)
    def _():
        totals[...] += running
        picks[...] += found

    @pl.when(step == pl.num_programs(0) - 1)
    def _():
        sums = jnp.sum(totals[...], axis=1, keepdims=True)
        hits = jnp.sum(picks[...], axis=1, keepdims=True)
        turned = jnp.where(lane == 0, sums, hits).T
        stats[...] = turned[:8, :]


def score(bases, hidden, own, other, target):
    rows, width = hidden.shape
    cols = own.shape[1]
    tile = 256
    return pl.pallas_call(
        score_kernel,
        grid_spec=pltpu.PrefetchScalarGridSpec(
            num_scalar_prefetch=1,
            grid=(cols // tile,),
            in_specs=[
                pl.BlockSpec((rows, width), lambda j, *_: (0, 0)),
                pl.BlockSpec((width, tile), lambda j, *_: (0, j)),
                pl.BlockSpec((width, tile), lambda j, *_: (0, j)),
                pl.BlockSpec((rows, 1), lambda j, *_: (0, 0)),
            ],
            out_specs=pl.BlockSpec((8, rows), lambda j, *_: (0, 0)),
            scratch_shapes=[pltpu.VMEM((rows, 128), F32), pltpu.VMEM((rows, 128), F32)],
        ),
        out_shape=jax.ShapeDtypeStruct((8, rows), F32),
        compiler_params=pltpu.CompilerParams(
            dimension_semantics=("arbitrary",), vmem_limit_bytes=32 << 20
        ),
        cost_estimate=pl.CostEstimate(
            flops=4 * rows * width * cols,
            bytes_accessed=2 * width * (2 * cols + rows),
            transcendentals=2 * rows * cols,
        ),
        name="score",
    )(bases, hidden, own, other, target)


def per_device(
    embedded,
    states,
    w_query,
    w_key,
    w_value,
    w_output_gate,
    w_beta,
    w_decay,
    decay_rate,
    decay_bias,
    head_gain,
    input_gain,
    w_out,
    final_gain,
    lm_head,
    targets,
    active,
):
    steps, group, width = embedded.shape
    cols = lm_head.shape[1]
    me = lax.axis_index(AXES).astype(jnp.int32)
    core = lax.axis_index("c").astype(jnp.int32)
    batch = lax.axis_index(BATCH).astype(jnp.int32)
    head = lax.axis_index(HEAD).astype(jnp.int32)
    send = functools.partial(lax.ppermute, axis_name=AXES)
    far_head = send(lm_head, perm=OTHER_CORE)

    spot = jnp.stack([batch, head, core])
    give, keep = front(
        spot,
        decay_rate,
        decay_bias,
        embedded,
        states,
        w_query,
        w_key,
        w_value,
        w_output_gate,
        w_beta.T,
        w_decay.T,
        w_out,
        input_gain[None],
        head_gain[None],
        active.T,
    )
    pair = (keep + send(give, perm=OTHER_CORE).astype(F32)).astype(BF16)
    summed = pair.astype(F32) + send(pair, perm=OTHER_LOW).astype(F32)
    mine = lax.dynamic_slice_in_dim(embedded, core * (steps // 2), steps // 2, 0)
    y = mine.reshape(-1, width).astype(F32) + summed
    hidden = (
        y * lax.rsqrt(jnp.mean(y * y, axis=-1, keepdims=True) + EPS) * final_gain
    ).astype(BF16)

    block = hidden.shape[0]
    table = sources()
    order = lax.dynamic_index_in_dim(jnp.asarray(table), me, 0, keepdims=False)
    inverse = lax.dynamic_index_in_dim(
        jnp.asarray(np.argsort(table, axis=1).astype(np.int32)), me, 0, keepdims=False
    )
    wanted = lax.dynamic_slice_in_dim(targets.T, core * (steps // 2), steps // 2, 0)
    wanted = jnp.take(wanted.reshape(steps // 2, GROUPS, group), order, axis=1)
    wanted = wanted.transpose(1, 0, 2).reshape(GROUPS * block, 1)

    both = jnp.concatenate([hidden, send(hidden, perm=OTHER_HIGH)], 0)
    near = jnp.concatenate([both] + [send(both, perm=p) for p in NEAR], 0)
    pieces = [near] + [send(near, perm=p) for p in FAR]
    bases = jnp.stack([me * cols, (me ^ GROUPS) * cols])
    size = near.shape[0]
    stats = [
        score(bases, piece, lm_head, far_head, wanted[i * size : (i + 1) * size])[:2]
        for i, piece in enumerate(pieces)
    ]
    stats = jnp.concatenate(stats, 1).reshape(2, GROUPS, block).transpose(1, 0, 2)
    stats = jnp.take(stats.reshape(GROUPS, 2 * block), inverse, axis=0)
    stats = jnp.broadcast_to(stats[None], (4, GROUPS, 2 * block)).reshape(DEVICES, 2 * block)
    stats = lax.all_to_all(stats, AXES, 0, 0, tiled=True)
    stats = jnp.sum(stats.reshape(2, 2, GROUPS, 2, steps // 2, group), axis=(0, 2))
    total, picked = stats[:, 0].reshape(steps, group), stats[:, 1].reshape(steps, group)
    marks = lax.dynamic_slice_in_dim(active.T, batch * group, group, 1)
    return jnp.where(marks > 0, picked - jnp.log(total), 0.0).T


def solution(mesh):
    finer = Mesh(mesh.devices.reshape(SIZES), AXES)
    return jax.shard_map(
        per_device,
        mesh=finer,
        in_specs=(
            P(None, BATCH, None),
            P(BATCH, HEAD, None, None),
            P(None, HEAD),
            P(None, HEAD),
            P(None, HEAD),
            P(None, HEAD),
            P(None, HEAD),
            P(None, HEAD),
            P(),
            P(),
            P(),
            P(),
            P(HEAD, None),
            P(),
            P(None, HEAD + BATCH),
            P(),
            P(),
        ),
        out_specs=P(BATCH, None),
        check_vma=False,
    )
```

time: 325 us -> 123 us (0.38); the launches traced: 319 us -> 122 us
  matrix products: 112 us -> 0 us
  waiting for transfers between devices: 106 us -> 32.3 us
  blocking collectives: 71.4 us -> 0 us
  Pallas kernels: 0 us -> 33.7 us
  starting transfers between devices: 0.04 us -> 25.8 us
  local copies, waits for them, and re-layouts: 2.86 us -> 24.5 us
  between operations: 14.3 us -> 0.28 us
  other arithmetic: 11.9 us -> 5.28 us
    dot_general x34 -> x0, matrix products: 112 us -> none  [the longest x4 44.2 us: recur(): jnp.einsum('rhk,rhkv->rhv', query_vector, corrected_state, precision=lax....]
    all_gather x1 -> x0, waiting for transfers between devices: 106 us -> none  [per_device(): lax.all_gather(hidden, BATCH, axis=0, tiled=True)]
    psum x5 -> x0, blocking collectives: 54.3 us -> none  [by_axis(): array = lax.psum(array, axis)]
    pallas_call x0 -> x5, Pallas kernels: none -> 33.7 us  [the longest x4 24.7 us: score(): pl.pallas_call(score_kernel, grid_spec=pltpu.PrefetchScalarGridSpec(num_s...]
    ppermute x0 -> x10, waiting for transfers between devices: none -> 22.8 us  [the longest x3 7.91 us: per_device(): pieces = [near] + [send(near, perm=p) for p in FAR]]
    unnamed x36 -> x49, local copies, waits for them, and re-layouts: 0.19 us -> 20.9 us
    ppermute x0 -> x10, starting transfers between devices: none -> 17.3 us  [the longest x3 6.47 us: per_device(): pieces = [near] + [send(near, perm=p) for p in FAR]]
    all_to_all x1 -> x0, blocking collectives: 17.1 us -> none  [from_everyone(): lax.all_to_all(jnp.broadcast_to(array[None], (peers, *array.shape)), axis...]
  transfers between devices with their start and end apart: 1 -> 11, of which waited for: 1 -> 9; matrix products, arithmetic and copies ran while one was open for 0% -> 5% of each run, Pallas kernels for 0% -> 18%
where the time goes in v1:
time: 123 us; the launch traced here: 122 us
  Pallas kernels  33.7 us (27%)
  waiting for transfers between devices  32.3 us (26%)
  starting transfers between devices  25.8 us (21%)
  local copies, waits for them, and re-layouts  24.5 us (20%)
  other arithmetic  5.28 us (4%)
    pallas_call x4, Pallas kernels, score(): pl.pallas_call(score_kernel, grid_spec=pltpu.PrefetchScalarGridSpec(num_s...  24.7 us
    unnamed x49, local copies, waits for them, and re-layouts  20.9 us
    all_to_all x1, waiting for transfers between devices, per_device(): stats = lax.all_to_all(stats, AXES, 0, 0, tiled=True)  9.47 us
    pallas_call x1, Pallas kernels, front(): pl.pallas_call(front_kernel, grid_spec=pltpu.PrefetchScalarGridSpec(num_s...  8.98 us
    all_to_all x1, starting transfers between devices, per_device(): stats = lax.all_to_all(stats, AXES, 0, 0, tiled=True)  8.49 us
    ppermute x3, waiting for transfers between devices, per_device(): pieces = [near] + [send(near, perm=p) for p in FAR]  7.91 us
    ppermute x3, starting transfers between devices, per_device(): pieces = [near] + [send(near, perm=p) for p in FAR]  6.47 us
    ppermute x3, waiting for transfers between devices, per_device(): near = jnp.concatenate([both] + [send(both, perm=p) for p in NEAR], 0)  6.35 us
  transfers between devices with their start and end apart: 11, of which 9 were waited for; matrix products, arithmetic and copies ran while one was open for 5% of the time, Pallas kernels for 18%

profile of v1, /device:TPU:0, one launch (start us, length us, event | category | flops | bytes accessed | tf_op | source)
XLA Modules:
  0.0 121.8 jit_solution(1729822385929696148)
XLA Ops:
  0.1 2.2 %copy-done.3 = bf16[16,8,128,128]{3,2,1,0:T(8,128)(2,1)S(1)} copy-done((bf16[16,8,128,128]{3,2,1,0:T(8,128)(2,1)S(1)}, bf16[16,8,128,128]{3,2,1,0:T(8,128)(2,1)}, u32[]{:S(2)}) %copy-start.3) | copy-done | bytes 4194328
  2.3 2.2 %copy-done.4 = bf16[2048,1024]{1,0:T(8,128)(2,1)S(1)} copy-done((bf16[2048,1024]{1,0:T(8,128)(2,1)S(1)}, bf16[2048,1024]{1,0:T(8,128)(2,1)}, u32[]{:S(2)}) %copy-start.4) | copy-done | bytes 4194328
  4.5 2.2 %copy-done.5 = bf16[2048,1024]{1,0:T(8,128)(2,1)S(1)} copy-done((bf16[2048,1024]{1,0:T(8,128)(2,1)S(1)}, bf16[2048,1024]{1,0:T(8,128)(2,1)}, u32[]{:S(2)}) %copy-start.5) | copy-done | bytes 4194328
  6.7 2.2 %copy-done.6 = bf16[1024,2048]{1,0:T(8,128)(2,1)S(1)} copy-done((bf16[1024,2048]{1,0:T(8,128)(2,1)S(1)}, bf16[1024,2048]{1,0:T(8,128)(2,1)}, u32[]{:S(2)}) %copy-start.6) | copy-done | bytes 4194328
  8.8 1.6 %copy-done.7 = bf16[2048,512]{1,0:T(8,128)(2,1)S(1)} copy-done((bf16[2048,512]{1,0:T(8,128)(2,1)S(1)}, bf16[2048,512]{1,0:T(8,128)(2,1)}, u32[]{:S(2)}) %copy-start.7) | copy-done | bytes 2097176
  10.4 1.6 %copy-done.8 = bf16[2048,512]{1,0:T(8,128)(2,1)S(1)} copy-done((bf16[2048,512]{1,0:T(8,128)(2,1)S(1)}, bf16[2048,512]{1,0:T(8,128)(2,1)}, u32[]{:S(2)}) %copy-start.8) | copy-done | bytes 2097176
  12.0 0.9 copy-done.9
  17.9 9.0 %front.1 = (bf16[32,2048]{1,0:T(8,128)(2,1)S(1)}, f32[32,2048]{1,0:T(8,128)S(1)}) custom-call(s32[3]{0:T(128)S(1)} %pad_add_fusion.1.spot, f32[32]{0:T(128)S(1)} %copy-done.18, f32[32]{0:T(128)S(1)} %copy-done.19, bf16[4,16,2048]{2,1,0:T(8,128)(2,1)S(1)} %copy-done.9, bf16[16,8,128,128]{3,2,1,0:T(8,128)(2,1)S(1)} %copy-done.3, ...), custom_call_target="tpu_custom_call" | custom-call | flops 1073741824 | bytes 22020096 | tf_op jit(solution)/shard_map/front/pallas_call | solution.py:197
  27.4 1.0 collective-permute-done
  28.5 1.7 %collective-permute-start.1 = (bf16[32,2048]{1,0:T(8,128)(2,1)S(1)}, bf16[32,2048]{1,0:T(8,128)(2,1)S(1)}, u32[]{:S(2)}, u32[]{:S(2)}) collective-permute-start(bf16[32,2048]{1,0:T(8,128)(2,1)S(1)} %add_convert_fusion), channel_id=1, source_target_pairs={{0,64},{1,65},{2,66},{3,67},{4,68},{5,69},{6,70},{7,71},{8,72},{9,... | collective-permute-start | bytes 393224 | tf_op jit(solution)/shard_map/ppermute | solution.py:354
  30.1 4.2 %collective-permute-done.1 = bf16[32,2048]{1,0:T(8,128)(2,1)S(1)} collective-permute-done((bf16[32,2048]{1,0:T(8,128)(2,1)S(1)}, bf16[32,2048]{1,0:T(8,128)(2,1)S(1)}, u32[]{:S(2)}, u32[]{:S(2)}) %collective-permute-start.1) | collective-permute-done | bytes 131104 | tf_op jit(solution)/shard_map/ppermute | solution.py:354
  34.6 3.2 %collective-permute-start.2 = (bf16[32,2048]{1,0:T(8,128)(2,1)S(1)}, bf16[32,2048]{1,0:T(8,128)(2,1)S(1)}, u32[]{:S(2)}, u32[]{:S(2)}) collective-permute-start(bf16[32,2048]{1,0:T(8,128)(2,1)S(1)} %get-tuple-element.14), channel_id=1, source_target_pairs={{0,1},{1,0},{2,3},{3,2},{4,5},{5,4},{6,7},{7,6},{8,9},{9,8},{10,11... | collective-permute-start | bytes 393224 | tf_op jit(solution)/shard_map/ppermute | solution.py:371
  37.8 3.4 %collective-permute-done.2 = bf16[32,2048]{1,0:T(8,128)(2,1)S(1)} collective-permute-done((bf16[32,2048]{1,0:T(8,128)(2,1)S(1)}, bf16[32,2048]{1,0:T(8,128)(2,1)S(1)}, u32[]{:S(2)}, u32[]{:S(2)}) %collective-permute-start.2) | collective-permute-done | bytes 131104 | tf_op jit(solution)/shard_map/ppermute | solution.py:371
  41.2 1.7 %collective-permute-start.3 = (bf16[64,2048]{1,0:T(8,128)(2,1)S(1)}, bf16[64,2048]{1,0:T(8,128)(2,1)S(1)}, u32[]{:S(2)}, u32[]{:S(2)}) collective-permute-start(bf16[64,2048]{1,0:T(8,128)(2,1)S(1)} %pad_maximum_fusion), channel_id=1, source_target_pairs={{0,8},{1,9},{2,10},{3,11},{4,12},{5,13},{6,14},{7,15},{8,16},{9,17... | collective-permute-start | bytes 786440 | tf_op jit(solution)/shard_map/ppermute | solution.py:372
  42.9 1.6 %collective-permute-start.4 = (bf16[64,2048]{1,0:T(8,128)(2,1)S(1)}, bf16[64,2048]{1,0:T(8,128)(2,1)S(1)}, u32[]{:S(2)}, u32[]{:S(2)}) collective-permute-start(bf16[64,2048]{1,0:T(8,128)(2,1)S(1)} %pad_maximum_fusion), channel_id=1, source_target_pairs={{0,24},{1,25},{2,26},{3,27},{4,28},{5,29},{6,30},{7,31},{8,0},{9,1... | collective-permute-start | bytes 786440 | tf_op jit(solution)/shard_map/ppermute | solution.py:372
  44.5 2.1 %collective-permute-start.5 = (bf16[64,2048]{1,0:T(8,128)(2,1)S(1)}, bf16[64,2048]{1,0:T(8,128)(2,1)S(1)}, u32[]{:S(2)}, u32[]{:S(2)}) collective-permute-start(bf16[64,2048]{1,0:T(8,128)(2,1)S(1)} %pad_maximum_fusion), channel_id=1, source_target_pairs={{0,16},{1,17},{2,18},{3,19},{4,20},{5,21},{6,22},{7,23},{8,24},{9,... | collective-permute-start | bytes 786440 | tf_op jit(solution)/shard_map/ppermute | solution.py:372
  46.6 2.3 %collective-permute-done.3 = bf16[64,2048]{1,0:T(8,128)(2,1)S(1)} collective-permute-done((bf16[64,2048]{1,0:T(8,128)(2,1)S(1)}, bf16[64,2048]{1,0:T(8,128)(2,1)S(1)}, u32[]{:S(2)}, u32[]{:S(2)}) %collective-permute-start.3) | collective-permute-done | bytes 262176 | tf_op jit(solution)/shard_map/ppermute | solution.py:372
  49.3 3.7 %collective-permute-done.5 = bf16[64,2048]{1,0:T(8,128)(2,1)S(1)} collective-permute-done((bf16[64,2048]{1,0:T(8,128)(2,1)S(1)}, bf16[64,2048]{1,0:T(8,128)(2,1)S(1)}, u32[]{:S(2)}, u32[]{:S(2)}) %collective-permute-start.5) | collective-permute-done | bytes 262176 | tf_op jit(solution)/shard_map/ppermute | solution.py:372
  53.0 4.4 %collective-permute-start.9 = (bf16[256,2048]{1,0:T(8,128)(2,1)S(1)}, bf16[256,2048]{1,0:T(8,128)(2,1)S(1)}, u32[]{:S(2)}, u32[]{:S(2)}) collective-permute-start(bf16[256,2048]{1,0:T(8,128)(2,1)S(1)} %constant_dynamic-update-slice_fusion.hidden), channel_id=1, source_target_pairs={{0,4},{1,5},{2,6},{3,7},{4,0},{5,1},{6,2},{7,3},{8,12},{9,13},{10,... | collective-permute-start | bytes 3145736 | tf_op jit(solution)/shard_map/ppermute | solution.py:373
  57.6 1.2 %fusion.2 = (s32[32]{0:T(128)S(1)}, s32[32]{0:T(128)}) fusion(s32[128,32]{1,0:T(8,128)} %constant.83.clone, s32[]{:T(128)S(6)} %select_n.64, s32[128,32]{1,0:T(8,128)} %constant.84.clone), kind=kLoop, calls=%fused_computation.32 | loop fusion | flops 192 | bytes 516 | tf_op jit(solution)/shard_map/jit(_take)/jit(_where)/select_n | solution.py:368
  59.7 1.3 %compare_and_fusion = (pred[32]{0:T(512)(128)(4,1)S(1)}, pred[32]{0:T(512)(128)(4,1)}) fusion(s32[128,32]{1,0:T(8,128)} %constant.83.clone, s32[]{:T(128)S(6)} %select_n.64, s32[128,32]{1,0:T(8,128)} %constant.84.clone), kind=kLoop, calls=%fused_computation.27 | loop fusion | flops 384 | bytes 324 | tf_op jit(solution)/shard_map/jit(_take)/and | solution.py:368
  60.9 1.8 %collective-permute-start.7 = (bf16[256,2048]{1,0:T(8,128)(2,1)S(1)}, bf16[256,2048]{1,0:T(8,128)(2,1)}, u32[]{:S(2)}, u32[]{:S(2)}) collective-permute-start(bf16[256,2048]{1,0:T(8,128)(2,1)S(1)} %constant_dynamic-update-slice_fusion.hidden), channel_id=1, source_target_pairs={{0,2},{1,3},{2,4},{3,5},{4,6},{5,7},{6,0},{7,1},{8,10},{9,11},{10,... | collective-permute-start | bytes 3145736 | tf_op jit(solution)/shard_map/ppermute | solution.py:373
  64.6 5.7 %collective-permute-done.9.hidden = bf16[256,2048]{1,0:T(8,128)(2,1)S(1)} collective-permute-done((bf16[256,2048]{1,0:T(8,128)(2,1)S(1)}, bf16[256,2048]{1,0:T(8,128)(2,1)S(1)}, u32[]{:S(2)}, u32[]{:S(2)}) %collective-permute-start.9) | collective-permute-done | bytes 1048608 | tf_op jit(solution)/shard_map/ppermute | solution.py:373
  70.3 2.2 %copy-done.1 = bf16[2048,1024]{1,0:T(8,128)(2,1)S(1)} copy-done((bf16[2048,1024]{1,0:T(8,128)(2,1)S(1)}, bf16[2048,1024]{1,0:T(8,128)(2,1)}, u32[]{:S(2)}) %copy-start.1) | copy-done | bytes 4194328
  73.4 6.4 %score.7 = f32[8,256]{1,0:T(8,128)S(1)} custom-call(s32[2]{0:T(128)S(1)} %pad_add_fusion.bases, bf16[256,2048]{1,0:T(8,128)(2,1)S(1)} %collective-permute-done.9.hidden, bf16[2048,1024]{1,0:T(8,128)(2,1)S(1)} %copy-done.1, bf16[2048,1024]{1,0:T(8,128)(2,1)} %collective-permute-done.6.other, s32[256,1]{1,0:T(8,128)S(1)} %copy-done.11), custom_call_target="tpu_custom_call" | custom-call | flops 2147483648 | bytes 9437184 | tf_op jit(solution)/shard_map/score/pallas_call | solution.py:280
  79.8 2.2 %collective-permute-done.8.hidden = bf16[256,2048]{1,0:T(8,128)(2,1)S(1)} collective-permute-done((bf16[256,2048]{1,0:T(8,128)(2,1)S(1)}, bf16[256,2048]{1,0:T(8,128)(2,1)S(1)}, u32[]{:S(2)}, u32[]{:S(2)}) %collective-permute-start.8) | collective-permute-done | bytes 1048608 | tf_op jit(solution)/shard_map/ppermute | solution.py:373
  82.0 6.0 %score.6 = f32[8,256]{1,0:T(8,128)S(1)} custom-call(s32[2]{0:T(128)S(1)} %pad_add_fusion.bases, bf16[256,2048]{1,0:T(8,128)(2,1)S(1)} %collective-permute-done.8.hidden, bf16[2048,1024]{1,0:T(8,128)(2,1)S(1)} %copy-done.2, bf16[2048,1024]{1,0:T(8,128)(2,1)} %collective-permute-done.6.other, s32[256,1]{1,0:T(8,128)S(1)} %slice.58.target), custom_call_target="tpu_custom_call" | custom-call | flops 2147483648 | bytes 9437184 | tf_op jit(solution)/shard_map/score/pallas_call | solution.py:280
  88.1 6.3 %score.5 = f32[8,256]{1,0:T(8,128)S(1)} custom-call(s32[2]{0:T(128)S(1)} %pad_add_fusion.bases, bf16[256,2048]{1,0:T(8,128)(2,1)} %collective-permute-done.7.hidden, bf16[2048,1024]{1,0:T(8,128)(2,1)S(1)} %copy-done.2, bf16[2048,1024]{1,0:T(8,128)(2,1)} %collective-permute-done.6.other, s32[256,1]{1,0:T(8,128)S(1)} %slice.57.target), custom_call_target="tpu_custom_call" | custom-call | flops 2147483648 | bytes 9437184 | tf_op jit(solution)/shard_map/score/pallas_call | solution.py:280
  94.4 6.0 %score.4 = f32[8,256]{1,0:T(8,128)S(1)} custom-call(s32[2]{0:T(128)S(1)} %pad_add_fusion.bases, bf16[256,2048]{1,0:T(8,128)(2,1)S(1)} %constant_dynamic-update-slice_fusion.hidden, bf16[2048,1024]{1,0:T(8,128)(2,1)S(1)} %copy-done.2, bf16[2048,1024]{1,0:T(8,128)(2,1)} %collective-permute-done.6.other, s32[256,1]{1,0:T(8,128)S(1)} %slice.56.target), custom_call_target="tpu_custom_call" | custom-call | flops 2147483648 | bytes 9437184 | tf_op jit(solution)/shard_map/score/pallas_call | solution.py:280
  102.0 8.5 %all-to-all-start = ((f32[128,1,64]{2,1,0:T(1,128)}), f32[128,1,64]{2,1,0:T(1,128)S(1)}, u32[]{:S(2)}, u32[]{:S(2)}) async-start(f32[128,1,64]{2,1,0:T(1,128)} %bitcast.21), calls=%async_computation | async-start | bytes 131072 | tf_op jit(solution)/shard_map/all_to_all | solution.py:383
  110.5 9.5 %all-to-all-done = f32[128,1,64]{2,1,0:T(1,128)S(1)} async-done(((f32[128,1,64]{2,1,0:T(1,128)}), f32[128,1,64]{2,1,0:T(1,128)S(1)}, u32[]{:S(2)}, u32[]{:S(2)}) %all-to-all-start) | async-done | bytes 32800 | tf_op jit(solution)/shard_map/all_to_all | solution.py:383
  120.5 1.3 %select_bitcast_fusion = f32[16,4]{0,1:T(4,128)} fusion(f32[4,16]{1,0:T(4,128)S(1)} %bitcast.47, s32[512,4]{0,1:T(4,128)} %param.35, s32[]{:T(128)S(6)} %select_n.63), kind=kLoop, calls=%fused_computation.24 | loop fusion | flops 128 | bytes 772 | tf_op jit(solution)/shard_map/transpose | solution.py:387
  (86 shorter events, 12.1 us)
Async XLA Ops:
  0.0 57.4 %copy-start = (s32[512,4]{0,1:T(4,128)S(1)}, s32[512,4]{0,1:T(4,128)}, u32[]{:S(2)}) copy-start(s32[512,4]{0,1:T(4,128)} %param.34) | copy-start | bytes 24580
  0.0 70.3 %collective-permute-start.6 = (bf16[2048,1024]{1,0:T(8,128)(2,1)}, bf16[2048,1024]{1,0:T(8,128)(2,1)}, u32[]{:S(2)}, u32[]{:S(2)}) collective-permute-start(bf16[2048,1024]{1,0:T(8,128)(2,1)} %own.7), channel_id=1, source_target_pairs={{0,32},{1,33},{2,34},{3,35},{4,36},{5,37},{6,38},{7,39},{8,40},{9,... | collective-permute-start | bytes 12582920 | tf_op jit(solution)/shard_map/ppermute | solution.py:333
  0.1 2.2 %copy-start.3 = (bf16[16,8,128,128]{3,2,1,0:T(8,128)(2,1)S(1)}, bf16[16,8,128,128]{3,2,1,0:T(8,128)(2,1)}, u32[]{:S(2)}) copy-start(bf16[16,8,128,128]{3,2,1,0:T(8,128)(2,1)} %states.1) | copy-start | bytes 12582916
  2.3 2.2 %copy-start.4 = (bf16[2048,1024]{1,0:T(8,128)(2,1)S(1)}, bf16[2048,1024]{1,0:T(8,128)(2,1)}, u32[]{:S(2)}) copy-start(bf16[2048,1024]{1,0:T(8,128)(2,1)} %w_value.1) | copy-start | bytes 12582916
  4.5 2.2 %copy-start.5 = (bf16[2048,1024]{1,0:T(8,128)(2,1)S(1)}, bf16[2048,1024]{1,0:T(8,128)(2,1)}, u32[]{:S(2)}) copy-start(bf16[2048,1024]{1,0:T(8,128)(2,1)} %w_gate.1) | copy-start | bytes 12582916
  6.6 2.2 %copy-start.6 = (bf16[1024,2048]{1,0:T(8,128)(2,1)S(1)}, bf16[1024,2048]{1,0:T(8,128)(2,1)}, u32[]{:S(2)}) copy-start(bf16[1024,2048]{1,0:T(8,128)(2,1)} %w_out.1) | copy-start | bytes 12582916
  8.8 1.6 %copy-start.7 = (bf16[2048,512]{1,0:T(8,128)(2,1)S(1)}, bf16[2048,512]{1,0:T(8,128)(2,1)}, u32[]{:S(2)}) copy-start(bf16[2048,512]{1,0:T(8,128)(2,1)} %w_query.1) | copy-start | bytes 6291460
  10.4 1.6 %copy-start.8 = (bf16[2048,512]{1,0:T(8,128)(2,1)S(1)}, bf16[2048,512]{1,0:T(8,128)(2,1)}, u32[]{:S(2)}) copy-start(bf16[2048,512]{1,0:T(8,128)(2,1)} %w_key.1) | copy-start | bytes 6291460
  12.0 0.9 copy-start.9
  13.0 0.8 copy-start.12
  13.7 0.8 copy-start.13
  14.5 0.7 copy-start.14
  17.9 12.3 %copy-start.10 = (bf16[4,16,2048]{2,1,0:T(8,128)(2,1)S(1)}, bf16[4,16,2048]{2,1,0:T(8,128)(2,1)}, u32[]{:S(2)}) copy-start(bf16[4,16,2048]{2,1,0:T(8,128)(2,1)} %embedded.1) | copy-start | bytes 786436
  17.9 16.6 %copy-start.21 = (f32[2048]{0:T(1024)S(1)}, f32[2048]{0:T(1024)}, u32[]{:S(2)}) copy-start(f32[2048]{0:T(1024)} %param.32) | copy-start | bytes 24580
  26.8 1.6 %collective-permute-start = (bf16[32,2048]{1,0:T(8,128)(2,1)S(1)}, bf16[32,2048]{1,0:T(8,128)(2,1)S(1)}, u32[]{:S(2)}, u32[]{:S(2)}) collective-permute-start(bf16[32,2048]{1,0:T(8,128)(2,1)S(1)} %get-tuple-element.8), channel_id=1, source_target_pairs={{0,32},{1,33},{2,34},{3,35},{4,36},{5,37},{6,38},{7,39},{8,40},{9,... | collective-permute-start | bytes 393224 | tf_op jit(solution)/shard_map/ppermute | solution.py:353
  28.5 5.8 %collective-permute-start.1 = (bf16[32,2048]{1,0:T(8,128)(2,1)S(1)}, bf16[32,2048]{1,0:T(8,128)(2,1)S(1)}, u32[]{:S(2)}, u32[]{:S(2)}) collective-permute-start(bf16[32,2048]{1,0:T(8,128)(2,1)S(1)} %add_convert_fusion), channel_id=1, source_target_pairs={{0,64},{1,65},{2,66},{3,67},{4,68},{5,69},{6,70},{7,71},{8,72},{9,... | collective-permute-start | bytes 393224 | tf_op jit(solution)/shard_map/ppermute | solution.py:354
  34.6 6.6 %collective-permute-start.2 = (bf16[32,2048]{1,0:T(8,128)(2,1)S(1)}, bf16[32,2048]{1,0:T(8,128)(2,1)S(1)}, u32[]{:S(2)}, u32[]{:S(2)}) collective-permute-start(bf16[32,2048]{1,0:T(8,128)(2,1)S(1)} %get-tuple-element.14), channel_id=1, source_target_pairs={{0,1},{1,0},{2,3},{3,2},{4,5},{5,4},{6,7},{7,6},{8,9},{9,8},{10,11... | collective-permute-start | bytes 393224 | tf_op jit(solution)/shard_map/ppermute | solution.py:371
  41.2 7.7 %collective-permute-start.3 = (bf16[64,2048]{1,0:T(8,128)(2,1)S(1)}, bf16[64,2048]{1,0:T(8,128)(2,1)S(1)}, u32[]{:S(2)}, u32[]{:S(2)}) collective-permute-start(bf16[64,2048]{1,0:T(8,128)(2,1)S(1)} %pad_maximum_fusion), channel_id=1, source_target_pairs={{0,8},{1,9},{2,10},{3,11},{4,12},{5,13},{6,14},{7,15},{8,16},{9,17... | collective-permute-start | bytes 786440 | tf_op jit(solution)/shard_map/ppermute | solution.py:372
  42.9 6.4 %collective-permute-start.4 = (bf16[64,2048]{1,0:T(8,128)(2,1)S(1)}, bf16[64,2048]{1,0:T(8,128)(2,1)S(1)}, u32[]{:S(2)}, u32[]{:S(2)}) collective-permute-start(bf16[64,2048]{1,0:T(8,128)(2,1)S(1)} %pad_maximum_fusion), channel_id=1, source_target_pairs={{0,24},{1,25},{2,26},{3,27},{4,28},{5,29},{6,30},{7,31},{8,0},{9,1... | collective-permute-start | bytes 786440 | tf_op jit(solution)/shard_map/ppermute | solution.py:372
  44.5 8.5 %collective-permute-start.5 = (bf16[64,2048]{1,0:T(8,128)(2,1)S(1)}, bf16[64,2048]{1,0:T(8,128)(2,1)S(1)}, u32[]{:S(2)}, u32[]{:S(2)}) collective-permute-start(bf16[64,2048]{1,0:T(8,128)(2,1)S(1)} %pad_maximum_fusion), channel_id=1, source_target_pairs={{0,16},{1,17},{2,18},{3,19},{4,20},{5,21},{6,22},{7,23},{8,24},{9,... | collective-permute-start | bytes 786440 | tf_op jit(solution)/shard_map/ppermute | solution.py:372
  53.0 17.3 %collective-permute-start.9 = (bf16[256,2048]{1,0:T(8,128)(2,1)S(1)}, bf16[256,2048]{1,0:T(8,128)(2,1)S(1)}, u32[]{:S(2)}, u32[]{:S(2)}) collective-permute-start(bf16[256,2048]{1,0:T(8,128)(2,1)S(1)} %constant_dynamic-update-slice_fusion.hidden), channel_id=1, source_target_pairs={{0,4},{1,5},{2,6},{3,7},{4,0},{5,1},{6,2},{7,3},{8,12},{9,13},{10,... | collective-permute-start | bytes 3145736 | tf_op jit(solution)/shard_map/ppermute | solution.py:373
  58.8 23.2 %collective-permute-start.8 = (bf16[256,2048]{1,0:T(8,128)(2,1)S(1)}, bf16[256,2048]{1,0:T(8,128)(2,1)S(1)}, u32[]{:S(2)}, u32[]{:S(2)}) collective-permute-start(bf16[256,2048]{1,0:T(8,128)(2,1)S(1)} %constant_dynamic-update-slice_fusion.hidden), channel_id=1, source_target_pairs={{0,6},{1,7},{2,0},{3,1},{4,2},{5,3},{6,4},{7,5},{8,14},{9,15},{10,... | collective-permute-start | bytes 3145736 | tf_op jit(solution)/shard_map/ppermute | solution.py:373
  60.9 27.1 %collective-permute-start.7 = (bf16[256,2048]{1,0:T(8,128)(2,1)S(1)}, bf16[256,2048]{1,0:T(8,128)(2,1)}, u32[]{:S(2)}, u32[]{:S(2)}) collective-permute-start(bf16[256,2048]{1,0:T(8,128)(2,1)S(1)} %constant_dynamic-update-slice_fusion.hidden), channel_id=1, source_target_pairs={{0,2},{1,3},{2,4},{3,5},{4,6},{5,7},{6,0},{7,1},{8,10},{9,11},{10,... | collective-permute-start | bytes 3145736 | tf_op jit(solution)/shard_map/ppermute | solution.py:373
  70.3 2.2 %copy-start.1 = (bf16[2048,1024]{1,0:T(8,128)(2,1)S(1)}, bf16[2048,1024]{1,0:T(8,128)(2,1)}, u32[]{:S(2)}) copy-start(bf16[2048,1024]{1,0:T(8,128)(2,1)} %own.7) | copy-start | bytes 12582916
  72.5 0.9 copy-start.11
  73.4 8.6 %copy-start.2 = (bf16[2048,1024]{1,0:T(8,128)(2,1)S(1)}, bf16[2048,1024]{1,0:T(8,128)(2,1)}, u32[]{:S(2)}) copy-start(bf16[2048,1024]{1,0:T(8,128)(2,1)} %own.7) | copy-start | bytes 12582916
  79.8 8.3 %copy-start.15 = (f32[8,256]{1,0:T(8,128)}, f32[8,256]{1,0:T(8,128)S(1)}, u32[]{:S(2)}) copy-start(f32[8,256]{1,0:T(8,128)S(1)} %score.7) | copy-start | bytes 24580
  88.0 6.3 %copy-start.16 = (f32[8,256]{1,0:T(8,128)}, f32[8,256]{1,0:T(8,128)S(1)}, u32[]{:S(2)}) copy-start(f32[8,256]{1,0:T(8,128)S(1)} %score.6) | copy-start | bytes 24580
  94.4 6.1 %slice-start = ((f32[8,256]{1,0:T(8,128)}), f32[2,256]{1,0:T(2,128)S(1)}, s32[]{:S(2)}) async-start(f32[8,256]{1,0:T(8,128)} %copy-done.15), calls=%async_computation.1 | async-start | bytes 4096 | tf_op jit(solution)/shard_map/slice | solution.py:377
  94.4 6.1 %slice-start.1 = ((f32[8,256]{1,0:T(8,128)}), f32[2,256]{1,0:T(2,128)S(1)}, s32[]{:S(2)}) async-start(f32[8,256]{1,0:T(8,128)} %copy-done.16), calls=%async_computation.2 | async-start | bytes 4096 | tf_op jit(solution)/shard_map/slice | solution.py:377
  94.4 6.9 %copy-start.22 = (pred[32]{0:T(512)(128)(4,1)S(1)}, pred[32]{0:T(512)(128)(4,1)}, u32[]{:S(2)}) copy-start(pred[32]{0:T(512)(128)(4,1)} %get-tuple-element.16) | copy-start | bytes 100
  102.0 18.0 %all-to-all-start = ((f32[128,1,64]{2,1,0:T(1,128)}), f32[128,1,64]{2,1,0:T(1,128)S(1)}, u32[]{:S(2)}, u32[]{:S(2)}) async-start(f32[128,1,64]{2,1,0:T(1,128)} %bitcast.21), calls=%async_computation | async-start | bytes 131072 | tf_op jit(solution)/shard_map/all_to_all | solution.py:383
  (4 other events, 2.7 us)

commit v2 on v1

--- a/solution.py
+++ b/solution.py
@@ -230,7 +230,7 @@
             jax.ShapeDtypeStruct((rows // 2, width), F32),
         ],
         compiler_params=pltpu.CompilerParams(
-            dimension_semantics=("arbitrary",), vmem_limit_bytes=32 << 20
+            dimension_semantics=("arbitrary",), vmem_limit_bytes=60 << 20
         ),
         cost_estimate=pl.CostEstimate(
             flops=2 * rows * width * 4096, bytes_accessed=21 << 20, transcendentals=0
@@ -239,61 +239,83 @@
     )(spot, rate, offset, embedded, states, wq, wk, wv, wg, wb, wd, wo, ig, hg, active)
 
 
-def score_kernel(bases, hidden, own, other, target, stats, totals, picks):
-    step = pl.program_id(0)
-    rows, cols = hidden.shape[0], own.shape[1]
-    x = hidden[...]
-    want = target[...]
-    running = jnp.zeros((rows, 128), F32)
-    found = jnp.zeros((rows, 128), F32)
+TILE = 256
+
+
+def score_kernel(count, bases, *refs):
+    pieces, (own, other, target, stats) = refs[:count], refs[count : count + 4]
+    hidden, weights, totals, picks, piece_sems, weight_sems = refs[count + 4 :]
+    rows, tiles = hidden.shape[0], weights.shape[0]
+    size = rows // count
+
+    def piece_copy(i):
+        return pltpu.make_async_copy(
+            pieces[i], hidden.at[pl.ds(i * size, size), :], piece_sems.at[i]
+        )
+
+    def weight_copy(i, which):
+        columns = pl.ds(pl.multiple_of(i * TILE, TILE), TILE)
+        return pltpu.make_async_copy(
+            (own, other)[which].at[:, columns], weights.at[i, which], weight_sems.at[i, which]
+        )
+
+    for i in range(count):
+        piece_copy(i).start()
+    for i in range(tiles):
+        for which in range(2):
+            weight_copy(i, which).start()
+    totals[...] = jnp.zeros_like(totals)
+    picks[...] = jnp.zeros_like(picks)
+    for i in range(count):
+        piece_copy(i).wait()
     lane = lax.broadcasted_iota(jnp.int32, (rows, 128), 1)
-    for which, weight in enumerate((own, other)):
-        logits = jnp.dot(x, weight[...], preferred_element_type=F32)
-        left = jnp.broadcast_to(want - (bases[which] + step * cols), (rows, 128)) - lane
-        for s in range(cols // 128):
-            part = logits[:, s * 128 : (s + 1) * 128]
-            running = running + jnp.exp(part)
-            found = found + jnp.where(left == s * 128, part, 0.0)
-
-    @pl.when(step == 0)
-    def _():
-        totals[...] = running
-        picks[...] = found
-
-    @pl.when(step > 0)
-    def _():
-        totals[...] += running
-        picks[...] += found
-
-    @pl.when(step == pl.num_programs(0) - 1)
-    def _():
-        sums = jnp.sum(totals[...], axis=1, keepdims=True)
-        hits = jnp.sum(picks[...], axis=1, keepdims=True)
-        turned = jnp.where(lane == 0, sums, hits).T
-        stats[...] = turned[:8, :]
-
-
-def score(bases, hidden, own, other, target):
-    rows, width = hidden.shape
-    cols = own.shape[1]
-    tile = 256
+
+    def body(i, carry):
+        x = hidden[...]
+        for which in range(2):
+            weight_copy(i, which).wait()
+            logits = jnp.dot(x, weights[i, which], preferred_element_type=F32)
+            left = jnp.broadcast_to(target[...] - (bases[which] + i * TILE), (rows, 128)) - lane
+            running = totals[...]
+            found = picks[...]
+            for s in range(TILE // 128):
+                part = logits[:, s * 128 : (s + 1) * 128]
+                running = running + jnp.exp(part)
+                found = found + jnp.where(left == s * 128, part, 0.0)
+            totals[...] = running
+            picks[...] = found
+        return carry
+
+    lax.fori_loop(0, tiles, body, 0)
+    sums = jnp.sum(totals[...], axis=1, keepdims=True)
+    hits = jnp.sum(picks[...], axis=1, keepdims=True)
+    stats[...] = jnp.where(lane == 0, sums, hits).T[:8, :]
+
+
+def score(bases, pieces, own, other, target):
+    size, width = pieces[0].shape
+    count, cols = len(pieces), own.shape[1]
+    rows = size * count
+    raw = pl.BlockSpec(memory_space=pltpu.HBM)
     return pl.pallas_call(
-        score_kernel,
+        functools.partial(score_kernel, count),
         grid_spec=pltpu.PrefetchScalarGridSpec(
             num_scalar_prefetch=1,
-            grid=(cols // tile,),
-            in_specs=[
-                pl.BlockSpec((rows, width), lambda j, *_: (0, 0)),
-                pl.BlockSpec((width, tile), lambda j, *_: (0, j)),
-                pl.BlockSpec((width, tile), lambda j, *_: (0, j)),
-                pl.BlockSpec((rows, 1), lambda j, *_: (0, 0)),
+            grid=(1,),
+            in_specs=[raw] * (count + 2) + [pl.BlockSpec((rows, 1), lambda j, *_: (0, 0))],
+            out_specs=pl.BlockSpec((8, rows), lambda j, *_: (0, 0)),
+            scratch_shapes=[
+                pltpu.VMEM((rows, width), BF16),
+                pltpu.VMEM((cols // TILE, 2, width, TILE), BF16),
+                pltpu.VMEM((rows, 128), F32),
+                pltpu.VMEM((rows, 128), F32),
+                pltpu.SemaphoreType.DMA((count,)),
+                pltpu.SemaphoreType.DMA((cols // TILE, 2)),
             ],
-            out_specs=pl.BlockSpec((8, rows), lambda j, *_: (0, 0)),
-            scratch_shapes=[pltpu.VMEM((rows, 128), F32), pltpu.VMEM((rows, 128), F32)],
         ),
         out_shape=jax.ShapeDtypeStruct((8, rows), F32),
         compiler_params=pltpu.CompilerParams(
-            dimension_semantics=("arbitrary",), vmem_limit_bytes=32 << 20
+            dimension_semantics=("arbitrary",), vmem_limit_bytes=60 << 20
         ),
         cost_estimate=pl.CostEstimate(
             flops=4 * rows * width * cols,
@@ -301,7 +323,7 @@
             transcendentals=2 * rows * cols,
         ),
         name="score",
-    )(bases, hidden, own, other, target)
+    )(bases, *pieces, own, other, target)
 
 
 def per_device(
@@ -350,33 +372,38 @@
         head_gain[None],
         active.T,
     )
+    block = keep.shape[0]
+    table = sources()
+    order = lax.dynamic_index_in_dim(jnp.asarray(table), me, 0, keepdims=False)
+    inverse = lax.dynamic_index_in_dim(
+        jnp.asarray(np.argsort(table, axis=1).astype(np.int32)), me, 0, keepdims=False
+    )
     pair = (keep + send(give, perm=OTHER_CORE).astype(F32)).astype(BF16)
-    summed = pair.astype(F32) + send(pair, perm=OTHER_LOW).astype(F32)
+    bases = jnp.stack([me * cols, (me ^ GROUPS) * cols])
+    pair, order, inverse, bases = lax.optimization_barrier((pair, order, inverse, bases))
+    wanted = lax.dynamic_slice_in_dim(targets.T, core * (steps // 2), steps // 2, 0)
+    wanted = jnp.take(wanted.reshape(steps // 2, GROUPS, group), order, axis=1)
+    wanted = wanted.transpose(1, 0, 2).reshape(GROUPS * block, 1)
+    from_low = send(pair, perm=OTHER_LOW)
+    from_low, wanted, inverse = lax.optimization_barrier((from_low, wanted, inverse))
+    summed = pair.astype(F32) + from_low.astype(F32)
     mine = lax.dynamic_slice_in_dim(embedded, core * (steps // 2), steps // 2, 0)
     y = mine.reshape(-1, width).astype(F32) + summed
     hidden = (
         y * lax.rsqrt(jnp.mean(y * y, axis=-1, keepdims=True) + EPS) * final_gain
     ).astype(BF16)
 
-    block = hidden.shape[0]
-    table = sources()
-    order = lax.dynamic_index_in_dim(jnp.asarray(table), me, 0, keepdims=False)
-    inverse = lax.dynamic_index_in_dim(
-        jnp.asarray(np.argsort(table, axis=1).astype(np.int32)), me, 0, keepdims=False
-    )
-    wanted = lax.dynamic_slice_in_dim(targets.T, core * (steps // 2), steps // 2, 0)
-    wanted = jnp.take(wanted.reshape(steps // 2, GROUPS, group), order, axis=1)
-    wanted = wanted.transpose(1, 0, 2).reshape(GROUPS * block, 1)
-
     both = jnp.concatenate([hidden, send(hidden, perm=OTHER_HIGH)], 0)
     near = jnp.concatenate([both] + [send(both, perm=p) for p in NEAR], 0)
-    pieces = [near] + [send(near, perm=p) for p in FAR]
-    bases = jnp.stack([me * cols, (me ^ GROUPS) * cols])
     size = near.shape[0]
-    stats = [
-        score(bases, piece, lm_head, far_head, wanted[i * size : (i + 1) * size])[:2]
-        for i, piece in enumerate(pieces)
-    ]
+    forth, back = send(near, perm=FAR[0]), send(near, perm=FAR[1])
+    stats = [score(bases, [near], lm_head, far_head, wanted[:size])]
+    near, first = lax.optimization_barrier((near, stats[0]))
+    facing = send(near, perm=FAR[2])
+    stats = [first]
+    stats.append(score(bases, [forth, back], lm_head, far_head, wanted[size : 3 * size]))
+    stats.append(score(bases, [facing], lm_head, far_head, wanted[3 * size :]))
+    stats = [part[:2] for part in stats]
     stats = jnp.concatenate(stats, 1).reshape(2, GROUPS, block).transpose(1, 0, 2)
     stats = jnp.take(stats.reshape(GROUPS, 2 * block), inverse, axis=0)
     stats = jnp.broadcast_to(stats[None], (4, GROUPS, 2 * block)).reshape(DEVICES, 2 * block)

time: 123 us -> 111 us (0.902)
  Pallas kernels: 33.7 us -> 52.6 us
  local copies, waits for them, and re-layouts: 24.5 us -> 6.71 us
  waiting for transfers between devices: 32.3 us -> 22 us
    unnamed x49 -> x13, local copies, waits for them, and re-layouts: 20.9 us -> 1.02 us
    pallas_call x4 -> x3, Pallas kernels: 24.7 us -> 40.5 us  [score(): pl.pallas_call(functools.partial(score_kernel, count), grid_spec=pltpu.Pr...]
    ppermute x4, waiting for transfers between devices: 12.1 us -> 3.08 us  [the longest x1 3.07 us: per_device(): from_low = send(pair, perm=OTHER_LOW)]
    pallas_call x1, Pallas kernels: 8.98 us -> 12.1 us  [front(): pl.pallas_call(front_kernel, grid_spec=pltpu.PrefetchScalarGridSpec(num_s...]
    and x1, other arithmetic: 1.28 us -> 0.01 us  [per_device(): wanted = jnp.take(wanted.reshape(steps // 2, GROUPS, group), order, axis=1)]
    select_n x2, other arithmetic: 1.34 us -> 0.1 us  [per_device(): wanted = jnp.take(wanted.reshape(steps // 2, GROUPS, group), order, axis=1)]
  transfers between devices with their start and end apart: 11 -> 11, of which waited for: 9 -> 6; matrix products, arithmetic and copies ran while one was open for 5% -> 5% of each run, Pallas kernels for 18% -> 37%
where the time goes in v2:
time: 111 us; the launch traced here: 110 us
  Pallas kernels  52.6 us (47%)
  starting transfers between devices  24.8 us (22%)
  waiting for transfers between devices  22 us (20%)
  local copies, waits for them, and re-layouts  6.71 us (6%)
  other arithmetic  4.26 us (4%)
    pallas_call x3, Pallas kernels, score(): pl.pallas_call(functools.partial(score_kernel, count), grid_spec=pltpu.Pr...  40.5 us
    pallas_call x1, Pallas kernels, front(): pl.pallas_call(front_kernel, grid_spec=pltpu.PrefetchScalarGridSpec(num_s...  12.1 us
    all_to_all x1, waiting for transfers between devices, per_device(): stats = lax.all_to_all(stats, AXES, 0, 0, tiled=True)  9.46 us
    all_to_all x1, starting transfers between devices, per_device(): stats = lax.all_to_all(stats, AXES, 0, 0, tiled=True)  7.82 us
    ppermute x3, waiting for transfers between devices, per_device(): near = jnp.concatenate([both] + [send(both, perm=p) for p in NEAR], 0)  6.06 us
    ppermute x3, starting transfers between devices, per_device(): near = jnp.concatenate([both] + [send(both, perm=p) for p in NEAR], 0)  5.44 us
    ppermute x2, starting transfers between devices, per_device(): forth, back = (send(near, perm=FAR[0]), send(near, perm=FAR[1]))  4.19 us
    ppermute x1, waiting for transfers between devices, per_device(): both = jnp.concatenate([hidden, send(hidden, perm=OTHER_HIGH)], 0)  3.37 us
  transfers between devices with their start and end apart: 11, of which 6 were waited for; matrix products, arithmetic and copies ran while one was open for 5% of the time, Pallas kernels for 37%

profile of v2, /device:TPU:0, one launch (start us, length us, event | category | flops | bytes accessed | tf_op | source)
XLA Modules:
  0.0 110.5 jit_solution(2876269013626680036)
XLA Ops:
  0.0 0.7 pad_add_fusion.spot
  0.7 12.1 %front.1 = (bf16[32,2048]{1,0:T(8,128)(2,1)}, f32[32,2048]{1,0:T(8,128)}) custom-call(s32[3]{0:T(128)} %pad_add_fusion.spot, f32[32]{0:T(128)} %rate.1, f32[32]{0:T(128)} %offset.1, bf16[4,16,2048]{2,1,0:T(8,128)(2,1)} %embedded.1, bf16[16,8,128,128]{3,2,1,0:T(8,128)(2,1)} %states.1, bf16[2048,512]{1,0:T(8,128)(2,1)} %w_query.1, bf16[2048,512]{1,0:T(8,128)(2,1)} %w_key.1, ...), custom_call_target="tpu_custom_call" | custom-call | flops 1073741824 | bytes 22020096 | tf_op jit(solution)/shard_map/front/pallas_call | solution.py:197
  12.8 0.5 collective-permute-start
  13.3 0.6 pad_add_fusion.1.bases
  14.0 0.7 fusion.2
  14.8 1.0 add_convert_fusion
  15.8 1.7 %collective-permute-start.1 = (bf16[32,2048]{1,0:T(8,128)(2,1)S(1)}, bf16[32,2048]{1,0:T(8,128)(2,1)S(1)}, u32[]{:S(2)}, u32[]{:S(2)}) collective-permute-start(bf16[32,2048]{1,0:T(8,128)(2,1)S(1)} %add_convert_fusion), channel_id=1, source_target_pairs={{0,64},{1,65},{2,66},{3,67},{4,68},{5,69},{6,70},{7,71},{8,72},{9,... | collective-permute-start | bytes 393224 | tf_op jit(solution)/shard_map/ppermute | solution.py:387
  17.4 0.6 gather_fusion
  18.3 3.1 %collective-permute-done.1 = bf16[32,2048]{1,0:T(8,128)(2,1)S(1)} collective-permute-done((bf16[32,2048]{1,0:T(8,128)(2,1)S(1)}, bf16[32,2048]{1,0:T(8,128)(2,1)S(1)}, u32[]{:S(2)}, u32[]{:S(2)}) %collective-permute-start.1) | collective-permute-done | bytes 131104 | tf_op jit(solution)/shard_map/ppermute | solution.py:387
  21.6 3.2 %collective-permute-start.2 = (bf16[32,2048]{1,0:T(8,128)(2,1)S(1)}, bf16[32,2048]{1,0:T(8,128)(2,1)S(1)}, u32[]{:S(2)}, u32[]{:S(2)}) collective-permute-start(bf16[32,2048]{1,0:T(8,128)(2,1)S(1)} %get-tuple-element.30), channel_id=1, source_target_pairs={{0,1},{1,0},{2,3},{3,2},{4,5},{5,4},{6,7},{7,6},{8,9},{9,8},{10,11... | collective-permute-start | bytes 393224 | tf_op jit(solution)/shard_map/ppermute | solution.py:396
  24.8 3.4 %collective-permute-done.2 = bf16[32,2048]{1,0:T(8,128)(2,1)S(1)} collective-permute-done((bf16[32,2048]{1,0:T(8,128)(2,1)S(1)}, bf16[32,2048]{1,0:T(8,128)(2,1)S(1)}, u32[]{:S(2)}, u32[]{:S(2)}) %collective-permute-start.2) | collective-permute-done | bytes 131104 | tf_op jit(solution)/shard_map/ppermute | solution.py:396
  28.2 1.7 %collective-permute-start.3 = (bf16[64,2048]{1,0:T(8,128)(2,1)S(1)}, bf16[64,2048]{1,0:T(8,128)(2,1)S(1)}, u32[]{:S(2)}, u32[]{:S(2)}) collective-permute-start(bf16[64,2048]{1,0:T(8,128)(2,1)S(1)} %pad_maximum_fusion), channel_id=1, source_target_pairs={{0,8},{1,9},{2,10},{3,11},{4,12},{5,13},{6,14},{7,15},{8,16},{9,17... | collective-permute-start | bytes 786440 | tf_op jit(solution)/shard_map/ppermute | solution.py:397
  30.2 1.6 %collective-permute-start.4 = (bf16[64,2048]{1,0:T(8,128)(2,1)S(1)}, bf16[64,2048]{1,0:T(8,128)(2,1)S(1)}, u32[]{:S(2)}, u32[]{:S(2)}) collective-permute-start(bf16[64,2048]{1,0:T(8,128)(2,1)S(1)} %pad_maximum_fusion), channel_id=1, source_target_pairs={{0,24},{1,25},{2,26},{3,27},{4,28},{5,29},{6,30},{7,31},{8,0},{9,1... | collective-permute-start | bytes 786440 | tf_op jit(solution)/shard_map/ppermute | solution.py:397
  31.8 2.1 %collective-permute-start.5 = (bf16[64,2048]{1,0:T(8,128)(2,1)S(1)}, bf16[64,2048]{1,0:T(8,128)(2,1)S(1)}, u32[]{:S(2)}, u32[]{:S(2)}) collective-permute-start(bf16[64,2048]{1,0:T(8,128)(2,1)S(1)} %pad_maximum_fusion), channel_id=1, source_target_pairs={{0,16},{1,17},{2,18},{3,19},{4,20},{5,21},{6,22},{7,23},{8,24},{9,... | collective-permute-start | bytes 786440 | tf_op jit(solution)/shard_map/ppermute | solution.py:397
  33.9 2.0 %collective-permute-done.3 = bf16[64,2048]{1,0:T(8,128)(2,1)S(1)} collective-permute-done((bf16[64,2048]{1,0:T(8,128)(2,1)S(1)}, bf16[64,2048]{1,0:T(8,128)(2,1)S(1)}, u32[]{:S(2)}, u32[]{:S(2)}) %collective-permute-start.3) | collective-permute-done | bytes 262176 | tf_op jit(solution)/shard_map/ppermute | solution.py:397
  35.9 0.7 collective-permute-done.4
  36.6 3.4 %collective-permute-done.5 = bf16[64,2048]{1,0:T(8,128)(2,1)S(1)} collective-permute-done((bf16[64,2048]{1,0:T(8,128)(2,1)S(1)}, bf16[64,2048]{1,0:T(8,128)(2,1)S(1)}, u32[]{:S(2)}, u32[]{:S(2)}) %collective-permute-start.5) | collective-permute-done | bytes 262176 | tf_op jit(solution)/shard_map/ppermute | solution.py:397
  40.0 2.0 %collective-permute-start.7 = (bf16[256,2048]{1,0:T(8,128)(2,1)S(1)}, bf16[256,2048]{1,0:T(8,128)(2,1)}, u32[]{:S(2)}, u32[]{:S(2)}) collective-permute-start(bf16[256,2048]{1,0:T(8,128)(2,1)S(1)} %constant_dynamic-update-slice_fusion.refs_0_), channel_id=1, source_target_pairs={{0,2},{1,3},{2,4},{3,5},{4,6},{5,7},{6,0},{7,1},{8,10},{9,11},{10,... | collective-permute-start | bytes 3145736 | tf_op jit(solution)/shard_map/ppermute | solution.py:399
  42.0 2.2 %collective-permute-start.8 = (bf16[256,2048]{1,0:T(8,128)(2,1)S(1)}, bf16[256,2048]{1,0:T(8,128)(2,1)}, u32[]{:S(2)}, u32[]{:S(2)}) collective-permute-start(bf16[256,2048]{1,0:T(8,128)(2,1)S(1)} %constant_dynamic-update-slice_fusion.refs_0_), channel_id=1, source_target_pairs={{0,6},{1,7},{2,0},{3,1},{4,2},{5,3},{6,4},{7,5},{8,14},{9,15},{10,... | collective-permute-start | bytes 3145736 | tf_op jit(solution)/shard_map/ppermute | solution.py:399
  44.2 0.7 fusion.4
  45.0 11.8 %score.3 = f32[8,256]{1,0:T(8,128)} custom-call(s32[2]{0:T(128)} %pad_add_fusion.1.bases, bf16[256,2048]{1,0:T(8,128)(2,1)} %copy-done.1, bf16[2048,1024]{1,0:T(8,128)(2,1)} %refs_1_.3, bf16[2048,1024]{1,0:T(8,128)(2,1)} %collective-permute-done.6.refs_2_.refs_3_, s32[256,1]{1,0:T(8,128)} %get-tuple-element.28.refs_3_), custom_call_target="tpu_custom_call" | custom-call | flops 2147483648 | bytes 9437184 | tf_op jit(solution)/shard_map/score/pallas_call | solution.py:300
  56.7 1.9 %collective-permute-start.9 = (bf16[256,2048]{1,0:T(8,128)(2,1)}, bf16[256,2048]{1,0:T(8,128)(2,1)S(1)}, u32[]{:S(2)}, u32[]{:S(2)}) collective-permute-start(bf16[256,2048]{1,0:T(8,128)(2,1)} %copy-done.1), channel_id=1, source_target_pairs={{0,4},{1,5},{2,6},{3,7},{4,0},{5,1},{6,2},{7,3},{8,12},{9,13},{10,... | collective-permute-start | bytes 3145736 | tf_op jit(solution)/shard_map/ppermute | solution.py:402
  58.7 0.7 slice.37.refs_4_
  59.4 16.8 %score.4 = f32[8,512]{1,0:T(8,128)} custom-call(s32[2]{0:T(128)} %pad_add_fusion.1.bases, bf16[256,2048]{1,0:T(8,128)(2,1)} %collective-permute-done.7.refs_0_, bf16[256,2048]{1,0:T(8,128)(2,1)} %collective-permute-done.8.refs_1_, bf16[2048,1024]{1,0:T(8,128)(2,1)} %refs_1_.3, bf16[2048,1024]{1,0:T(8,128)(2,1)} %collective-permute-done.6.refs_2_.refs_3_, ...), custom_call_target="tpu_custom_call" | custom-call | flops 4294967296 | bytes 10485760 | tf_op jit(solution)/shard_map/score/pallas_call | solution.py:300
  76.3 1.0 copy-done.2
  77.2 11.9 %score.5 = f32[8,256]{1,0:T(8,128)} custom-call(s32[2]{0:T(128)} %pad_add_fusion.1.bases, bf16[256,2048]{1,0:T(8,128)(2,1)} %copy-done.2, bf16[2048,1024]{1,0:T(8,128)(2,1)} %refs_1_.3, bf16[2048,1024]{1,0:T(8,128)(2,1)} %collective-permute-done.6.refs_2_.refs_3_, s32[256,1]{1,0:T(8,128)} %get-tuple-element.27.refs_3_), custom_call_target="tpu_custom_call" | custom-call | flops 2147483648 | bytes 9437184 | tf_op jit(solution)/shard_map/score/pallas_call | solution.py:300
  89.2 0.7 slice.40
  90.1 0.6 gather_fusion.1
  90.7 0.6 broadcast_in_dim.50
  91.4 7.8 %all-to-all-start = ((f32[128,1,64]{2,1,0:T(1,128)}), f32[128,1,64]{2,1,0:T(1,128)S(1)}, u32[]{:S(2)}, u32[]{:S(2)}) async-start(f32[128,1,64]{2,1,0:T(1,128)} %bitcast.17), calls=%async_computation | async-start | bytes 131072 | tf_op jit(solution)/shard_map/all_to_all | solution.py:410
  99.2 9.5 %all-to-all-done = f32[128,1,64]{2,1,0:T(1,128)S(1)} async-done(((f32[128,1,64]{2,1,0:T(1,128)}), f32[128,1,64]{2,1,0:T(1,128)S(1)}, u32[]{:S(2)}, u32[]{:S(2)}) %all-to-all-start) | async-done | bytes 32800 | tf_op jit(solution)/shard_map/all_to_all | solution.py:410
  109.1 1.3 %select_bitcast_fusion = f32[16,4]{0,1:T(4,128)} fusion(f32[4,16]{1,0:T(4,128)S(1)} %bitcast.38, s32[512,4]{0,1:T(4,128)} %param.35, s32[]{:T(128)S(6)} %select_n.41), kind=kLoop, calls=%fused_computation.22 | loop fusion | flops 128 | bytes 772 | tf_op jit(solution)/shard_map/transpose | solution.py:414
  (50 shorter events, 1.8 us)
Async XLA Ops:
  0.0 13.3 %copy-start = (s32[512,4]{0,1:T(4,128)S(1)}, s32[512,4]{0,1:T(4,128)}, u32[]{:S(2)}) copy-start(s32[512,4]{0,1:T(4,128)} %param.34) | copy-start | bytes 24580
  0.0 44.9 %collective-permute-start.6 = (bf16[2048,1024]{1,0:T(8,128)(2,1)}, bf16[2048,1024]{1,0:T(8,128)(2,1)}, u32[]{:S(2)}, u32[]{:S(2)}) collective-permute-start(bf16[2048,1024]{1,0:T(8,128)(2,1)} %refs_1_.3), channel_id=1, source_target_pairs={{0,32},{1,33},{2,34},{3,35},{4,36},{5,37},{6,38},{7,39},{8,40},{9,... | collective-permute-start | bytes 12582920 | tf_op jit(solution)/shard_map/ppermute | solution.py:355
  0.7 12.6 %copy-start.3 = (bf16[4,16,2048]{2,1,0:T(8,128)(2,1)S(1)}, bf16[4,16,2048]{2,1,0:T(8,128)(2,1)}, u32[]{:S(2)}) copy-start(bf16[4,16,2048]{2,1,0:T(8,128)(2,1)} %embedded.1) | copy-start | bytes 786436
  0.7 20.8 %copy-start.4 = (f32[2048]{0:T(1024)S(1)}, f32[2048]{0:T(1024)}, u32[]{:S(2)}) copy-start(f32[2048]{0:T(1024)} %param.32) | copy-start | bytes 24580
  12.8 2.0 %collective-permute-start = (bf16[32,2048]{1,0:T(8,128)(2,1)}, bf16[32,2048]{1,0:T(8,128)(2,1)S(1)}, u32[]{:S(2)}, u32[]{:S(2)}) collective-permute-start(bf16[32,2048]{1,0:T(8,128)(2,1)} %get-tuple-element.17), channel_id=1, source_target_pairs={{0,32},{1,33},{2,34},{3,35},{4,36},{5,37},{6,38},{7,39},{8,40},{9,... | collective-permute-start | bytes 393224 | tf_op jit(solution)/shard_map/ppermute | solution.py:381
  15.8 5.6 %collective-permute-start.1 = (bf16[32,2048]{1,0:T(8,128)(2,1)S(1)}, bf16[32,2048]{1,0:T(8,128)(2,1)S(1)}, u32[]{:S(2)}, u32[]{:S(2)}) collective-permute-start(bf16[32,2048]{1,0:T(8,128)(2,1)S(1)} %add_convert_fusion), channel_id=1, source_target_pairs={{0,64},{1,65},{2,66},{3,67},{4,68},{5,69},{6,70},{7,71},{8,72},{9,... | collective-permute-start | bytes 393224 | tf_op jit(solution)/shard_map/ppermute | solution.py:387
  21.6 6.6 %collective-permute-start.2 = (bf16[32,2048]{1,0:T(8,128)(2,1)S(1)}, bf16[32,2048]{1,0:T(8,128)(2,1)S(1)}, u32[]{:S(2)}, u32[]{:S(2)}) collective-permute-start(bf16[32,2048]{1,0:T(8,128)(2,1)S(1)} %get-tuple-element.30), channel_id=1, source_target_pairs={{0,1},{1,0},{2,3},{3,2},{4,5},{5,4},{6,7},{7,6},{8,9},{9,8},{10,11... | collective-permute-start | bytes 393224 | tf_op jit(solution)/shard_map/ppermute | solution.py:396
  28.2 7.7 %collective-permute-start.3 = (bf16[64,2048]{1,0:T(8,128)(2,1)S(1)}, bf16[64,2048]{1,0:T(8,128)(2,1)S(1)}, u32[]{:S(2)}, u32[]{:S(2)}) collective-permute-start(bf16[64,2048]{1,0:T(8,128)(2,1)S(1)} %pad_maximum_fusion), channel_id=1, source_target_pairs={{0,8},{1,9},{2,10},{3,11},{4,12},{5,13},{6,14},{7,15},{8,16},{9,17... | collective-permute-start | bytes 786440 | tf_op jit(solution)/shard_map/ppermute | solution.py:397
  30.2 6.4 %collective-permute-start.4 = (bf16[64,2048]{1,0:T(8,128)(2,1)S(1)}, bf16[64,2048]{1,0:T(8,128)(2,1)S(1)}, u32[]{:S(2)}, u32[]{:S(2)}) collective-permute-start(bf16[64,2048]{1,0:T(8,128)(2,1)S(1)} %pad_maximum_fusion), channel_id=1, source_target_pairs={{0,24},{1,25},{2,26},{3,27},{4,28},{5,29},{6,30},{7,31},{8,0},{9,1... | collective-permute-start | bytes 786440 | tf_op jit(solution)/shard_map/ppermute | solution.py:397
  31.8 8.2 %collective-permute-start.5 = (bf16[64,2048]{1,0:T(8,128)(2,1)S(1)}, bf16[64,2048]{1,0:T(8,128)(2,1)S(1)}, u32[]{:S(2)}, u32[]{:S(2)}) collective-permute-start(bf16[64,2048]{1,0:T(8,128)(2,1)S(1)} %pad_maximum_fusion), channel_id=1, source_target_pairs={{0,16},{1,17},{2,18},{3,19},{4,20},{5,21},{6,22},{7,23},{8,24},{9,... | collective-permute-start | bytes 786440 | tf_op jit(solution)/shard_map/ppermute | solution.py:397
  40.0 4.9 %copy-start.1 = (bf16[256,2048]{1,0:T(8,128)(2,1)}, bf16[256,2048]{1,0:T(8,128)(2,1)S(1)}, u32[]{:S(2)}) copy-start(bf16[256,2048]{1,0:T(8,128)(2,1)S(1)} %constant_dynamic-update-slice_fusion.refs_0_) | copy-start | bytes 3145732
  40.0 19.4 %collective-permute-start.7 = (bf16[256,2048]{1,0:T(8,128)(2,1)S(1)}, bf16[256,2048]{1,0:T(8,128)(2,1)}, u32[]{:S(2)}, u32[]{:S(2)}) collective-permute-start(bf16[256,2048]{1,0:T(8,128)(2,1)S(1)} %constant_dynamic-update-slice_fusion.refs_0_), channel_id=1, source_target_pairs={{0,2},{1,3},{2,4},{3,5},{4,6},{5,7},{6,0},{7,1},{8,10},{9,11},{10,... | collective-permute-start | bytes 3145736 | tf_op jit(solution)/shard_map/ppermute | solution.py:399
  42.0 17.4 %collective-permute-start.8 = (bf16[256,2048]{1,0:T(8,128)(2,1)S(1)}, bf16[256,2048]{1,0:T(8,128)(2,1)}, u32[]{:S(2)}, u32[]{:S(2)}) collective-permute-start(bf16[256,2048]{1,0:T(8,128)(2,1)S(1)} %constant_dynamic-update-slice_fusion.refs_0_), channel_id=1, source_target_pairs={{0,6},{1,7},{2,0},{3,1},{4,2},{5,3},{6,4},{7,5},{8,14},{9,15},{10,... | collective-permute-start | bytes 3145736 | tf_op jit(solution)/shard_map/ppermute | solution.py:399
  56.7 19.5 %collective-permute-start.9 = (bf16[256,2048]{1,0:T(8,128)(2,1)}, bf16[256,2048]{1,0:T(8,128)(2,1)S(1)}, u32[]{:S(2)}, u32[]{:S(2)}) collective-permute-start(bf16[256,2048]{1,0:T(8,128)(2,1)} %copy-done.1), channel_id=1, source_target_pairs={{0,4},{1,5},{2,6},{3,7},{4,0},{5,1},{6,2},{7,3},{8,12},{9,13},{10,... | collective-permute-start | bytes 3145736 | tf_op jit(solution)/shard_map/ppermute | solution.py:402
  76.3 1.0 copy-start.2
  77.2 12.6 %slice-start = ((f32[8,512]{1,0:T(8,128)}), f32[2,512]{1,0:T(2,128)S(1)}, s32[]{:S(2)}) async-start(f32[8,512]{1,0:T(8,128)} %score.4), calls=%async_computation.1 | async-start | bytes 8192 | tf_op jit(solution)/shard_map/slice | solution.py:406
  77.2 12.6 %slice-start.1 = ((f32[8,256]{1,0:T(8,128)}), f32[2,256]{1,0:T(2,128)S(1)}, s32[]{:S(2)}) async-start(f32[8,256]{1,0:T(8,128)} %score.3), calls=%async_computation.2 | async-start | bytes 4096 | tf_op jit(solution)/shard_map/slice | solution.py:406
  91.4 17.3 %all-to-all-start = ((f32[128,1,64]{2,1,0:T(1,128)}), f32[128,1,64]{2,1,0:T(1,128)S(1)}, u32[]{:S(2)}, u32[]{:S(2)}) async-start(f32[128,1,64]{2,1,0:T(1,128)} %bitcast.17), calls=%async_computation | async-start | bytes 131072 | tf_op jit(solution)/shard_map/all_to_all | solution.py:410

commit v3 on v2

--- a/solution.py
+++ b/solution.py
@@ -239,91 +239,82 @@
     )(spot, rate, offset, embedded, states, wq, wk, wv, wg, wb, wd, wo, ig, hg, active)
 
 
-TILE = 256
+TILE = 512
 
 
 def score_kernel(count, bases, *refs):
-    pieces, (own, other, target, stats) = refs[:count], refs[count : count + 4]
-    hidden, weights, totals, picks, piece_sems, weight_sems = refs[count + 4 :]
-    rows, tiles = hidden.shape[0], weights.shape[0]
-    size = rows // count
-
-    def piece_copy(i):
-        return pltpu.make_async_copy(
-            pieces[i], hidden.at[pl.ds(i * size, size), :], piece_sems.at[i]
-        )
-
-    def weight_copy(i, which):
-        columns = pl.ds(pl.multiple_of(i * TILE, TILE), TILE)
-        return pltpu.make_async_copy(
-            (own, other)[which].at[:, columns], weights.at[i, which], weight_sems.at[i, which]
-        )
-
-    for i in range(count):
-        piece_copy(i).start()
-    for i in range(tiles):
-        for which in range(2):
-            weight_copy(i, which).start()
-    totals[...] = jnp.zeros_like(totals)
-    picks[...] = jnp.zeros_like(picks)
-    for i in range(count):
-        piece_copy(i).wait()
-    lane = lax.broadcasted_iota(jnp.int32, (rows, 128), 1)
-
-    def body(i, carry):
-        x = hidden[...]
-        for which in range(2):
-            weight_copy(i, which).wait()
-            logits = jnp.dot(x, weights[i, which], preferred_element_type=F32)
-            left = jnp.broadcast_to(target[...] - (bases[which] + i * TILE), (rows, 128)) - lane
-            running = totals[...]
-            found = picks[...]
-            for s in range(TILE // 128):
-                part = logits[:, s * 128 : (s + 1) * 128]
-                running = running + jnp.exp(part)
-                found = found + jnp.where(left == s * 128, part, 0.0)
-            totals[...] = running
-            picks[...] = found
-        return carry
-
-    lax.fori_loop(0, tiles, body, 0)
-    sums = jnp.sum(totals[...], axis=1, keepdims=True)
-    hits = jnp.sum(picks[...], axis=1, keepdims=True)
-    stats[...] = jnp.where(lane == 0, sums, hits).T[:8, :]
-
-
-def score(bases, pieces, own, other, target):
+    pieces, (vocabulary, target, stats) = refs[:count], refs[count:]
+    size, cols = pieces[0].shape[0], vocabulary.shape[2]
+    for p in range(count):
+        at = slice(p * size, (p + 1) * size)
+        lane = lax.broadcasted_iota(jnp.int32, (size, 128), 1)
+        running = jnp.zeros((size, 128), F32)
+        found = jnp.zeros((size, 128), F32)
+        for start in range(0, cols, TILE):
+            for which in range(2):
+                logits = jnp.dot(
+                    pieces[p][...],
+                    vocabulary[which, :, start : start + TILE],
+                    preferred_element_type=F32,
+                )
+                left = jnp.broadcast_to(target[at, :] - (bases[which] + start), (size, 128)) - lane
+                for s in range(0, TILE, 128):
+                    part = logits[:, s : s + 128]
+                    running = running + jnp.exp(part)
+                    found = found + jnp.where(left == s, part, 0.0)
+        sums = jnp.sum(running, axis=1, keepdims=True)
+        hits = jnp.sum(found, axis=1, keepdims=True)
+        stats[:, at] = jnp.where(lane == 0, sums, hits).T[:8, :]
+
+
+def gather_kernel(own, other, both, sems):
+    copies = [
+        pltpu.make_async_copy(source, both.at[i], sems.at[i])
+        for i, source in enumerate((own, other))
+    ]
+    for copy in copies:
+        copy.start()
+    for copy in copies:
+        copy.wait()
+
+
+def bring_in(own, other):
+    return pl.pallas_call(
+        gather_kernel,
+        in_specs=[pl.BlockSpec(memory_space=pltpu.HBM)] * 2,
+        out_specs=pl.BlockSpec(memory_space=pltpu.VMEM),
+        scratch_shapes=[pltpu.SemaphoreType.DMA((2,))],
+        out_shape=jax.ShapeDtypeStruct((2, *own.shape), own.dtype),
+        compiler_params=pltpu.CompilerParams(vmem_limit_bytes=12 << 20),
+        cost_estimate=pl.CostEstimate(
+            flops=0, bytes_accessed=4 * own.size, transcendentals=0
+        ),
+        name="bring_in",
+    )(own, other)
+
+
+def score(bases, pieces, vocabulary, target):
     size, width = pieces[0].shape
-    count, cols = len(pieces), own.shape[1]
+    count, cols = len(pieces), vocabulary.shape[2]
     rows = size * count
-    raw = pl.BlockSpec(memory_space=pltpu.HBM)
+    near = pl.BlockSpec(memory_space=pltpu.VMEM)
     return pl.pallas_call(
         functools.partial(score_kernel, count),
         grid_spec=pltpu.PrefetchScalarGridSpec(
             num_scalar_prefetch=1,
-            grid=(1,),
-            in_specs=[raw] * (count + 2) + [pl.BlockSpec((rows, 1), lambda j, *_: (0, 0))],
-            out_specs=pl.BlockSpec((8, rows), lambda j, *_: (0, 0)),
-            scratch_shapes=[
-                pltpu.VMEM((rows, width), BF16),
-                pltpu.VMEM((cols // TILE, 2, width, TILE), BF16),
-                pltpu.VMEM((rows, 128), F32),
-                pltpu.VMEM((rows, 128), F32),
-                pltpu.SemaphoreType.DMA((count,)),
-                pltpu.SemaphoreType.DMA((cols // TILE, 2)),
-            ],
+            grid=(),
+            in_specs=[near] * (count + 2),
+            out_specs=near,
         ),
         out_shape=jax.ShapeDtypeStruct((8, rows), F32),
-        compiler_params=pltpu.CompilerParams(
-            dimension_semantics=("arbitrary",), vmem_limit_bytes=60 << 20
-        ),
+        compiler_params=pltpu.CompilerParams(vmem_limit_bytes=20 << 20),
         cost_estimate=pl.CostEstimate(
             flops=4 * rows * width * cols,
             bytes_accessed=2 * width * (2 * cols + rows),
             transcendentals=2 * rows * cols,
         ),
         name="score",
-    )(bases, *pieces, own, other, target)
+    )(bases, *pieces, vocabulary, target)
 
 
 def per_device(
@@ -397,12 +388,14 @@
     near = jnp.concatenate([both] + [send(both, perm=p) for p in NEAR], 0)
     size = near.shape[0]
     forth, back = send(near, perm=FAR[0]), send(near, perm=FAR[1])
-    stats = [score(bases, [near], lm_head, far_head, wanted[:size])]
-    near, first = lax.optimization_barrier((near, stats[0]))
+    far_head, near = lax.optimization_barrier((far_head, near))
+    vocabulary = bring_in(lm_head, far_head)
+    near, vocabulary = lax.optimization_barrier((near, vocabulary))
     facing = send(near, perm=FAR[2])
-    stats = [first]
-    stats.append(score(bases, [forth, back], lm_head, far_head, wanted[size : 3 * size]))
-    stats.append(score(bases, [facing], lm_head, far_head, wanted[3 * size :]))
+    stats = [score(bases, [near], vocabulary, wanted[:size])]
+    later, first = lax.optimization_barrier((wanted[size : 3 * size], stats[0]))
+    stats = [first, score(bases, [forth, back], vocabulary, later)]
+    stats.append(score(bases, [facing], vocabulary, wanted[3 * size :]))
     stats = [part[:2] for part in stats]
     stats = jnp.concatenate(stats, 1).reshape(2, GROUPS, block).transpose(1, 0, 2)
     stats = jnp.take(stats.reshape(GROUPS, 2 * block), inverse, axis=0)

time: 111 us -> 99.2 us (0.89)
  Pallas kernels: 52.6 us -> 26.4 us
  waiting for transfers between devices: 22 us -> 33.9 us
  starting transfers between devices: 24.8 us -> 26.6 us
    pallas_call x3, Pallas kernels: 40.5 us -> 11.8 us  [score(): pl.pallas_call(functools.partial(score_kernel, count), grid_spec=pltpu.Pr...]
    ppermute x2, waiting for transfers between devices: 0.01 us -> 11.5 us  [per_device(): forth, back = (send(near, perm=FAR[0]), send(near, perm=FAR[1]))]
    pallas_call x0 -> x1, Pallas kernels: none -> 2.48 us  [bring_in(): pl.pallas_call(gather_kernel, in_specs=[pl.BlockSpec(memory_space=pltpu.H...]
    all_to_all x1, starting transfers between devices: 7.82 us -> 9.52 us  [per_device(): stats = lax.all_to_all(stats, AXES, 0, 0, tiled=True)]
    unnamed x13 -> x15, local copies, waits for them, and re-layouts: 1.02 us -> 2.25 us
  transfers between devices with their start and end apart: 11 -> 11, of which waited for: 6 -> 9; matrix products, arithmetic and copies ran while one was open for 5% -> 5% of each run, Pallas kernels for 37% -> 11%
where the time goes in v3:
time: 99.2 us; the launch traced here: 98.5 us
  waiting for transfers between devices  33.9 us (34%)
  starting transfers between devices  26.6 us (27%)
  Pallas kernels  26.4 us (27%)
  local copies, waits for them, and re-layouts  7.6 us (8%)
  other arithmetic  3.75 us (4%)
    pallas_call x1, Pallas kernels, front(): pl.pallas_call(front_kernel, grid_spec=pltpu.PrefetchScalarGridSpec(num_s...  12.1 us
    pallas_call x3, Pallas kernels, score(): pl.pallas_call(functools.partial(score_kernel, count), grid_spec=pltpu.Pr...  11.8 us
    ppermute x2, waiting for transfers between devices, per_device(): forth, back = (send(near, perm=FAR[0]), send(near, perm=FAR[1]))  11.5 us
    all_to_all x1, starting transfers between devices, per_device(): stats = lax.all_to_all(stats, AXES, 0, 0, tiled=True)  9.52 us
    all_to_all x1, waiting for transfers between devices, per_device(): stats = lax.all_to_all(stats, AXES, 0, 0, tiled=True)  9.46 us
    ppermute x3, waiting for transfers between devices, per_device(): near = jnp.concatenate([both] + [send(both, perm=p) for p in NEAR], 0)  6.35 us
    ppermute x3, starting transfers between devices, per_device(): near = jnp.concatenate([both] + [send(both, perm=p) for p in NEAR], 0)  5.37 us
    ppermute x2, starting transfers between devices, per_device(): forth, back = (send(near, perm=FAR[0]), send(near, perm=FAR[1]))  4.18 us
  transfers between devices with their start and end apart: 11, of which 9 were waited for; matrix products, arithmetic and copies ran while one was open for 5% of the time, Pallas kernels for 11%

profile of v3, /device:TPU:0, one launch (start us, length us, event | category | flops | bytes accessed | tf_op | source)
XLA Modules:
  0.0 98.5 jit_solution(606880634438443060)
XLA Ops:
  0.0 0.7 pad_add_fusion.spot
  0.7 12.1 %front.1 = (bf16[32,2048]{1,0:T(8,128)(2,1)}, f32[32,2048]{1,0:T(8,128)}) custom-call(s32[3]{0:T(128)} %pad_add_fusion.spot, f32[32]{0:T(128)} %rate.1, f32[32]{0:T(128)} %offset.1, bf16[4,16,2048]{2,1,0:T(8,128)(2,1)} %embedded.1, bf16[16,8,128,128]{3,2,1,0:T(8,128)(2,1)} %states.1, bf16[2048,512]{1,0:T(8,128)(2,1)} %w_query.1, bf16[2048,512]{1,0:T(8,128)(2,1)} %w_key.1, ...), custom_call_target="tpu_custom_call" | custom-call | flops 1073741824 | bytes 22020096 | tf_op jit(solution)/shard_map/front/pallas_call | solution.py:197
  12.8 0.5 collective-permute-start.2
  13.5 0.7 fusion.2
  14.4 1.0 %add_convert_fusion = bf16[32,2048]{1,0:T(8,128)(2,1)S(1)} fusion(f32[32,2048]{1,0:T(8,128)} %get-tuple-element.20, bf16[32,2048]{1,0:T(8,128)(2,1)S(1)} %collective-permute-done), kind=kLoop, calls=%fused_computation.6 | loop fusion | flops 196608 | bytes 524288 | tf_op jit(solution)/shard_map/convert_element_type | solution.py:372
  15.3 1.7 %collective-permute-start.1 = (bf16[32,2048]{1,0:T(8,128)(2,1)S(1)}, bf16[32,2048]{1,0:T(8,128)(2,1)S(1)}, u32[]{:S(2)}, u32[]{:S(2)}) collective-permute-start(bf16[32,2048]{1,0:T(8,128)(2,1)S(1)} %add_convert_fusion), channel_id=1, source_target_pairs={{0,64},{1,65},{2,66},{3,67},{4,68},{5,69},{6,70},{7,71},{8,72},{9,... | collective-permute-start | bytes 393224 | tf_op jit(solution)/shard_map/ppermute | solution.py:378
  17.0 0.6 gather_fusion
  17.8 3.1 %collective-permute-done.1 = bf16[32,2048]{1,0:T(8,128)(2,1)S(1)} collective-permute-done((bf16[32,2048]{1,0:T(8,128)(2,1)S(1)}, bf16[32,2048]{1,0:T(8,128)(2,1)S(1)}, u32[]{:S(2)}, u32[]{:S(2)}) %collective-permute-start.1) | collective-permute-done | bytes 131104 | tf_op jit(solution)/shard_map/ppermute | solution.py:378
  21.3 3.2 %collective-permute-start.3 = (bf16[32,2048]{1,0:T(8,128)(2,1)S(1)}, bf16[32,2048]{1,0:T(8,128)(2,1)S(1)}, u32[]{:S(2)}, u32[]{:S(2)}) collective-permute-start(bf16[32,2048]{1,0:T(8,128)(2,1)S(1)} %get-tuple-element.38), channel_id=1, source_target_pairs={{0,1},{1,0},{2,3},{3,2},{4,5},{5,4},{6,7},{7,6},{8,9},{9,8},{10,11... | collective-permute-start | bytes 393224 | tf_op jit(solution)/shard_map/ppermute | solution.py:387
  24.5 3.4 %collective-permute-done.3 = bf16[32,2048]{1,0:T(8,128)(2,1)S(1)} collective-permute-done((bf16[32,2048]{1,0:T(8,128)(2,1)S(1)}, bf16[32,2048]{1,0:T(8,128)(2,1)S(1)}, u32[]{:S(2)}, u32[]{:S(2)}) %collective-permute-start.3) | collective-permute-done | bytes 131104 | tf_op jit(solution)/shard_map/ppermute | solution.py:387
  27.9 1.7 %collective-permute-start.4 = (bf16[64,2048]{1,0:T(8,128)(2,1)S(1)}, bf16[64,2048]{1,0:T(8,128)(2,1)S(1)}, u32[]{:S(2)}, u32[]{:S(2)}) collective-permute-start(bf16[64,2048]{1,0:T(8,128)(2,1)S(1)} %pad_maximum_fusion), channel_id=1, source_target_pairs={{0,8},{1,9},{2,10},{3,11},{4,12},{5,13},{6,14},{7,15},{8,16},{9,17... | collective-permute-start | bytes 786440 | tf_op jit(solution)/shard_map/ppermute | solution.py:388
  29.6 1.6 %collective-permute-start.5 = (bf16[64,2048]{1,0:T(8,128)(2,1)S(1)}, bf16[64,2048]{1,0:T(8,128)(2,1)S(1)}, u32[]{:S(2)}, u32[]{:S(2)}) collective-permute-start(bf16[64,2048]{1,0:T(8,128)(2,1)S(1)} %pad_maximum_fusion), channel_id=1, source_target_pairs={{0,24},{1,25},{2,26},{3,27},{4,28},{5,29},{6,30},{7,31},{8,0},{9,1... | collective-permute-start | bytes 786440 | tf_op jit(solution)/shard_map/ppermute | solution.py:388
  31.2 2.1 %collective-permute-start.6 = (bf16[64,2048]{1,0:T(8,128)(2,1)S(1)}, bf16[64,2048]{1,0:T(8,128)(2,1)S(1)}, u32[]{:S(2)}, u32[]{:S(2)}) collective-permute-start(bf16[64,2048]{1,0:T(8,128)(2,1)S(1)} %pad_maximum_fusion), channel_id=1, source_target_pairs={{0,16},{1,17},{2,18},{3,19},{4,20},{5,21},{6,22},{7,23},{8,24},{9,... | collective-permute-start | bytes 786440 | tf_op jit(solution)/shard_map/ppermute | solution.py:388
  33.2 2.3 %collective-permute-done.4 = bf16[64,2048]{1,0:T(8,128)(2,1)S(1)} collective-permute-done((bf16[64,2048]{1,0:T(8,128)(2,1)S(1)}, bf16[64,2048]{1,0:T(8,128)(2,1)S(1)}, u32[]{:S(2)}, u32[]{:S(2)}) %collective-permute-start.4) | collective-permute-done | bytes 262176 | tf_op jit(solution)/shard_map/ppermute | solution.py:388
  36.0 3.7 %collective-permute-done.6 = bf16[64,2048]{1,0:T(8,128)(2,1)S(1)} collective-permute-done((bf16[64,2048]{1,0:T(8,128)(2,1)S(1)}, bf16[64,2048]{1,0:T(8,128)(2,1)S(1)}, u32[]{:S(2)}, u32[]{:S(2)}) %collective-permute-start.6) | collective-permute-done | bytes 262176 | tf_op jit(solution)/shard_map/ppermute | solution.py:388
  39.7 2.0 %collective-permute-start.7 = (bf16[256,2048]{1,0:T(8,128)(2,1)S(1)}, bf16[256,2048]{1,0:T(8,128)(2,1)S(1)}, u32[]{:S(2)}, u32[]{:S(2)}) collective-permute-start(bf16[256,2048]{1,0:T(8,128)(2,1)S(1)} %constant_dynamic-update-slice_fusion.refs_0_), channel_id=1, source_target_pairs={{0,2},{1,3},{2,4},{3,5},{4,6},{5,7},{6,0},{7,1},{8,10},{9,11},{10,... | collective-permute-start | bytes 3145736 | tf_op jit(solution)/shard_map/ppermute | solution.py:390
  41.6 2.2 %collective-permute-start.8 = (bf16[256,2048]{1,0:T(8,128)(2,1)S(1)}, bf16[256,2048]{1,0:T(8,128)(2,1)S(1)}, u32[]{:S(2)}, u32[]{:S(2)}) collective-permute-start(bf16[256,2048]{1,0:T(8,128)(2,1)S(1)} %constant_dynamic-update-slice_fusion.refs_0_), channel_id=1, source_target_pairs={{0,6},{1,7},{2,0},{3,1},{4,2},{5,3},{6,4},{7,5},{8,14},{9,15},{10,... | collective-permute-start | bytes 3145736 | tf_op jit(solution)/shard_map/ppermute | solution.py:390
  43.8 1.0 %copy.34 = s32[1024,1]{1,0:T(8,128)} copy(s32[1024,1]{0,1:T(1,128)S(1)} %reshape.58) | data formatting | bytes 8192 | tf_op jit(solution)/shard_map/optimization_barrier | solution.py:379
  44.9 1.0 slice.36.refs_3_
  45.9 2.2 %copy-done.1 = bf16[2048,1024]{1,0:T(8,128)(2,1)S(1)} copy-done((bf16[2048,1024]{1,0:T(8,128)(2,1)S(1)}, bf16[2048,1024]{1,0:T(8,128)(2,1)}, u32[]{:S(2)}) %copy-start.1) | copy-done | bytes 4194328
  48.1 2.5 %bring_in.1.refs_1_.refs_2_ = bf16[2,2048,1024]{2,1,0:T(8,128)(2,1)S(1)} custom-call(bf16[2048,1024]{1,0:T(8,128)(2,1)S(1)} %copy-done.1, bf16[2048,1024]{1,0:T(8,128)(2,1)} %collective-permute-done.2.other), custom_call_target="tpu_custom_call" | custom-call | bytes 8388608 | tf_op jit(solution)/shard_map/bring_in/pallas_call | solution.py:282
  50.6 2.2 %collective-permute-start.9 = (bf16[256,2048]{1,0:T(8,128)(2,1)S(1)}, bf16[256,2048]{1,0:T(8,128)(2,1)S(1)}, u32[]{:S(2)}, u32[]{:S(2)}) collective-permute-start(bf16[256,2048]{1,0:T(8,128)(2,1)S(1)} %constant_dynamic-update-slice_fusion.refs_0_), channel_id=1, source_target_pairs={{0,4},{1,5},{2,6},{3,7},{4,0},{5,1},{6,2},{7,3},{8,12},{9,13},{10,... | collective-permute-start | bytes 3145736 | tf_op jit(solution)/shard_map/ppermute | solution.py:394
  52.8 3.1 %score.3 = f32[8,256]{1,0:T(8,128)S(1)} custom-call(s32[2]{0:T(128)S(1)} %pad_add_fusion.1.bases, bf16[256,2048]{1,0:T(8,128)(2,1)S(1)} %constant_dynamic-update-slice_fusion.refs_0_, bf16[2,2048,1024]{2,1,0:T(8,128)(2,1)S(1)} %bring_in.1.refs_1_.refs_2_, s32[256,1]{1,0:T(8,128)S(1)} %get-tuple-element.35.refs_2_), custom_call_target="tpu_custom_call" | custom-call | flops 2147483648 | bytes 9437184 | tf_op jit(solution)/shard_map/score/pallas_call | solution.py:301
  55.9 0.6 collective-permute-done.7.refs_0_
  56.5 10.9 %collective-permute-done.8.refs_1_ = bf16[256,2048]{1,0:T(8,128)(2,1)S(1)} collective-permute-done((bf16[256,2048]{1,0:T(8,128)(2,1)S(1)}, bf16[256,2048]{1,0:T(8,128)(2,1)S(1)}, u32[]{:S(2)}, u32[]{:S(2)}) %collective-permute-start.8) | collective-permute-done | bytes 1048608 | tf_op jit(solution)/shard_map/ppermute | solution.py:390
  67.4 5.5 %score.4 = f32[8,512]{1,0:T(8,128)S(1)} custom-call(s32[2]{0:T(128)S(1)} %pad_add_fusion.1.bases, bf16[256,2048]{1,0:T(8,128)(2,1)S(1)} %collective-permute-done.7.refs_0_, bf16[256,2048]{1,0:T(8,128)(2,1)S(1)} %collective-permute-done.8.refs_1_, bf16[2,2048,1024]{2,1,0:T(8,128)(2,1)S(1)} %bring_in.1.refs_1_.refs_2_, s32[512,1]{1,0:T(8,128)S(1)} %slice.36.refs_3_), custom_call_target="tpu_custom_call" | custom-call | flops 4294967296 | bytes 10485760 | tf_op jit(solution)/shard_map/score/pallas_call | solution.py:301
  72.9 3.2 %score.5 = f32[8,256]{1,0:T(8,128)S(1)} custom-call(s32[2]{0:T(128)S(1)} %pad_add_fusion.1.bases, bf16[256,2048]{1,0:T(8,128)(2,1)S(1)} %collective-permute-done.9.refs_0_, bf16[2,2048,1024]{2,1,0:T(8,128)(2,1)S(1)} %bring_in.1.refs_1_.refs_2_, s32[256,1]{1,0:T(8,128)S(1)} %get-tuple-element.36.refs_2_), custom_call_target="tpu_custom_call" | custom-call | flops 2147483648 | bytes 9437184 | tf_op jit(solution)/shard_map/score/pallas_call | solution.py:301
  76.3 0.6 gather_fusion.1
  77.0 0.6 broadcast_in_dim.50
  77.6 9.5 %all-to-all-start = ((f32[128,1,64]{2,1,0:T(1,128)}), f32[128,1,64]{2,1,0:T(1,128)S(1)}, u32[]{:S(2)}, u32[]{:S(2)}) async-start(f32[128,1,64]{2,1,0:T(1,128)} %bitcast.17), calls=%async_computation | async-start | bytes 131072 | tf_op jit(solution)/shard_map/all_to_all | solution.py:403
  87.2 9.5 %all-to-all-done = f32[128,1,64]{2,1,0:T(1,128)S(1)} async-done(((f32[128,1,64]{2,1,0:T(1,128)}), f32[128,1,64]{2,1,0:T(1,128)S(1)}, u32[]{:S(2)}, u32[]{:S(2)}) %all-to-all-start) | async-done | bytes 32800 | tf_op jit(solution)/shard_map/all_to_all | solution.py:403
  97.1 1.3 %select_bitcast_fusion = f32[16,4]{0,1:T(4,128)} fusion(f32[4,16]{1,0:T(4,128)S(1)} %bitcast.38, s32[512,4]{0,1:T(4,128)} %param.35, s32[]{:T(128)S(6)} %select_n.41), kind=kLoop, calls=%fused_computation.22 | loop fusion | flops 128 | bytes 772 | tf_op jit(solution)/shard_map/transpose | solution.py:407
  (52 shorter events, 2.2 us)
Async XLA Ops:
  0.0 13.3 %copy-start = (s32[512,4]{0,1:T(4,128)S(1)}, s32[512,4]{0,1:T(4,128)}, u32[]{:S(2)}) copy-start(s32[512,4]{0,1:T(4,128)} %param.34) | copy-start | bytes 24580
  0.7 12.7 %copy-start.4 = (bf16[4,16,2048]{2,1,0:T(8,128)(2,1)S(1)}, bf16[4,16,2048]{2,1,0:T(8,128)(2,1)}, u32[]{:S(2)}) copy-start(bf16[4,16,2048]{2,1,0:T(8,128)(2,1)} %embedded.1) | copy-start | bytes 786436
  0.7 20.5 %copy-start.5 = (f32[2048]{0:T(1024)S(1)}, f32[2048]{0:T(1024)}, u32[]{:S(2)}) copy-start(f32[2048]{0:T(1024)} %param.32) | copy-start | bytes 24580
  12.8 1.6 %collective-permute-start = (bf16[32,2048]{1,0:T(8,128)(2,1)}, bf16[32,2048]{1,0:T(8,128)(2,1)S(1)}, u32[]{:S(2)}, u32[]{:S(2)}) collective-permute-start(bf16[32,2048]{1,0:T(8,128)(2,1)} %get-tuple-element.21), channel_id=1, source_target_pairs={{0,32},{1,33},{2,34},{3,35},{4,36},{5,37},{6,38},{7,39},{8,40},{9,... | collective-permute-start | bytes 393224 | tf_op jit(solution)/shard_map/ppermute | solution.py:372
  12.8 33.1 %collective-permute-start.2 = (bf16[2048,1024]{1,0:T(8,128)(2,1)}, bf16[2048,1024]{1,0:T(8,128)(2,1)}, u32[]{:S(2)}, u32[]{:S(2)}) collective-permute-start(bf16[2048,1024]{1,0:T(8,128)(2,1)} %own.1), channel_id=1, source_target_pairs={{0,32},{1,33},{2,34},{3,35},{4,36},{5,37},{6,38},{7,39},{8,40},{9,... | collective-permute-start | bytes 12582920 | tf_op jit(solution)/shard_map/ppermute | solution.py:346
  15.3 5.6 %collective-permute-start.1 = (bf16[32,2048]{1,0:T(8,128)(2,1)S(1)}, bf16[32,2048]{1,0:T(8,128)(2,1)S(1)}, u32[]{:S(2)}, u32[]{:S(2)}) collective-permute-start(bf16[32,2048]{1,0:T(8,128)(2,1)S(1)} %add_convert_fusion), channel_id=1, source_target_pairs={{0,64},{1,65},{2,66},{3,67},{4,68},{5,69},{6,70},{7,71},{8,72},{9,... | collective-permute-start | bytes 393224 | tf_op jit(solution)/shard_map/ppermute | solution.py:378
  21.3 6.6 %collective-permute-start.3 = (bf16[32,2048]{1,0:T(8,128)(2,1)S(1)}, bf16[32,2048]{1,0:T(8,128)(2,1)S(1)}, u32[]{:S(2)}, u32[]{:S(2)}) collective-permute-start(bf16[32,2048]{1,0:T(8,128)(2,1)S(1)} %get-tuple-element.38), channel_id=1, source_target_pairs={{0,1},{1,0},{2,3},{3,2},{4,5},{5,4},{6,7},{7,6},{8,9},{9,8},{10,11... | collective-permute-start | bytes 393224 | tf_op jit(solution)/shard_map/ppermute | solution.py:387
  27.9 7.7 %collective-permute-start.4 = (bf16[64,2048]{1,0:T(8,128)(2,1)S(1)}, bf16[64,2048]{1,0:T(8,128)(2,1)S(1)}, u32[]{:S(2)}, u32[]{:S(2)}) collective-permute-start(bf16[64,2048]{1,0:T(8,128)(2,1)S(1)} %pad_maximum_fusion), channel_id=1, source_target_pairs={{0,8},{1,9},{2,10},{3,11},{4,12},{5,13},{6,14},{7,15},{8,16},{9,17... | collective-permute-start | bytes 786440 | tf_op jit(solution)/shard_map/ppermute | solution.py:388
  29.6 6.4 %collective-permute-start.5 = (bf16[64,2048]{1,0:T(8,128)(2,1)S(1)}, bf16[64,2048]{1,0:T(8,128)(2,1)S(1)}, u32[]{:S(2)}, u32[]{:S(2)}) collective-permute-start(bf16[64,2048]{1,0:T(8,128)(2,1)S(1)} %pad_maximum_fusion), channel_id=1, source_target_pairs={{0,24},{1,25},{2,26},{3,27},{4,28},{5,29},{6,30},{7,31},{8,0},{9,1... | collective-permute-start | bytes 786440 | tf_op jit(solution)/shard_map/ppermute | solution.py:388
  31.2 8.5 %collective-permute-start.6 = (bf16[64,2048]{1,0:T(8,128)(2,1)S(1)}, bf16[64,2048]{1,0:T(8,128)(2,1)S(1)}, u32[]{:S(2)}, u32[]{:S(2)}) collective-permute-start(bf16[64,2048]{1,0:T(8,128)(2,1)S(1)} %pad_maximum_fusion), channel_id=1, source_target_pairs={{0,16},{1,17},{2,18},{3,19},{4,20},{5,21},{6,22},{7,23},{8,24},{9,... | collective-permute-start | bytes 786440 | tf_op jit(solution)/shard_map/ppermute | solution.py:388
  39.7 16.9 %collective-permute-start.7 = (bf16[256,2048]{1,0:T(8,128)(2,1)S(1)}, bf16[256,2048]{1,0:T(8,128)(2,1)S(1)}, u32[]{:S(2)}, u32[]{:S(2)}) collective-permute-start(bf16[256,2048]{1,0:T(8,128)(2,1)S(1)} %constant_dynamic-update-slice_fusion.refs_0_), channel_id=1, source_target_pairs={{0,2},{1,3},{2,4},{3,5},{4,6},{5,7},{6,0},{7,1},{8,10},{9,11},{10,... | collective-permute-start | bytes 3145736 | tf_op jit(solution)/shard_map/ppermute | solution.py:390
  41.6 25.8 %collective-permute-start.8 = (bf16[256,2048]{1,0:T(8,128)(2,1)S(1)}, bf16[256,2048]{1,0:T(8,128)(2,1)S(1)}, u32[]{:S(2)}, u32[]{:S(2)}) collective-permute-start(bf16[256,2048]{1,0:T(8,128)(2,1)S(1)} %constant_dynamic-update-slice_fusion.refs_0_), channel_id=1, source_target_pairs={{0,6},{1,7},{2,0},{3,1},{4,2},{5,3},{6,4},{7,5},{8,14},{9,15},{10,... | collective-permute-start | bytes 3145736 | tf_op jit(solution)/shard_map/ppermute | solution.py:390
  45.9 2.2 %copy-start.1 = (bf16[2048,1024]{1,0:T(8,128)(2,1)S(1)}, bf16[2048,1024]{1,0:T(8,128)(2,1)}, u32[]{:S(2)}) copy-start(bf16[2048,1024]{1,0:T(8,128)(2,1)} %own.1) | copy-start | bytes 12582916
  48.1 4.7 %copy-start.3 = (s32[1024,1]{1,0:T(8,128)S(1)}, s32[1024,1]{1,0:T(8,128)}, u32[]{:S(2)}) copy-start(s32[1024,1]{1,0:T(8,128)} %copy.34) | copy-start | bytes 12292
  50.6 22.3 %collective-permute-start.9 = (bf16[256,2048]{1,0:T(8,128)(2,1)S(1)}, bf16[256,2048]{1,0:T(8,128)(2,1)S(1)}, u32[]{:S(2)}, u32[]{:S(2)}) collective-permute-start(bf16[256,2048]{1,0:T(8,128)(2,1)S(1)} %constant_dynamic-update-slice_fusion.refs_0_), channel_id=1, source_target_pairs={{0,4},{1,5},{2,6},{3,7},{4,0},{5,1},{6,2},{7,3},{8,12},{9,13},{10,... | collective-permute-start | bytes 3145736 | tf_op jit(solution)/shard_map/ppermute | solution.py:394
  55.9 17.0 %copy-start.2 = (f32[8,256]{1,0:T(8,128)}, f32[8,256]{1,0:T(8,128)S(1)}, u32[]{:S(2)}) copy-start(f32[8,256]{1,0:T(8,128)S(1)} %score.3) | copy-start | bytes 24580
  72.9 3.2 %slice-start = ((f32[8,256]{1,0:T(8,128)}), f32[2,256]{1,0:T(2,128)S(1)}, s32[]{:S(2)}) async-start(f32[8,256]{1,0:T(8,128)} %copy-done.2), calls=%async_computation.1 | async-start | bytes 4096 | tf_op jit(solution)/shard_map/slice | solution.py:399
  77.6 19.0 %all-to-all-start = ((f32[128,1,64]{2,1,0:T(1,128)}), f32[128,1,64]{2,1,0:T(1,128)S(1)}, u32[]{:S(2)}, u32[]{:S(2)}) async-start(f32[128,1,64]{2,1,0:T(1,128)} %bitcast.17), calls=%async_computation | async-start | bytes 131072 | tf_op jit(solution)/shard_map/all_to_all | solution.py:403

commit v4 on v3

--- a/solution.py
+++ b/solution.py
@@ -240,24 +240,29 @@
 
 
 TILE = 512
-
-
-def score_kernel(count, bases, *refs):
-    pieces, (vocabulary, target, stats) = refs[:count], refs[count:]
-    size, cols = pieces[0].shape[0], vocabulary.shape[2]
-    for p in range(count):
+BLOCK = 256
+
+
+def score_kernel(count, offset, bases, *refs):
+    parts, (vocabulary, target, stats) = refs[:count], refs[count:]
+    cols = vocabulary.shape[2]
+    if parts[0].shape[0] < BLOCK:
+        pieces = [jnp.concatenate([part[...] for part in parts], axis=0)]
+    else:
+        pieces = [part[...] for part in parts]
+    size = pieces[0].shape[0]
+    for p, piece in enumerate(pieces):
         at = slice(p * size, (p + 1) * size)
+        want = target[offset + p * size : offset + (p + 1) * size, :]
         lane = lax.broadcasted_iota(jnp.int32, (size, 128), 1)
         running = jnp.zeros((size, 128), F32)
         found = jnp.zeros((size, 128), F32)
         for start in range(0, cols, TILE):
             for which in range(2):
                 logits = jnp.dot(
-                    pieces[p][...],
-                    vocabulary[which, :, start : start + TILE],
-                    preferred_element_type=F32,
+                    piece, vocabulary[which, :, start : start + TILE], preferred_element_type=F32
                 )
-                left = jnp.broadcast_to(target[at, :] - (bases[which] + start), (size, 128)) - lane
+                left = jnp.broadcast_to(want - (bases[which] + start), (size, 128)) - lane
                 for s in range(0, TILE, 128):
                     part = logits[:, s : s + 128]
                     running = running + jnp.exp(part)
@@ -293,13 +298,13 @@
     )(own, other)
 
 
-def score(bases, pieces, vocabulary, target):
+def score(bases, pieces, vocabulary, target, offset):
     size, width = pieces[0].shape
     count, cols = len(pieces), vocabulary.shape[2]
     rows = size * count
     near = pl.BlockSpec(memory_space=pltpu.VMEM)
     return pl.pallas_call(
-        functools.partial(score_kernel, count),
+        functools.partial(score_kernel, count, offset),
         grid_spec=pltpu.PrefetchScalarGridSpec(
             num_scalar_prefetch=1,
             grid=(),
@@ -390,12 +395,14 @@
     forth, back = send(near, perm=FAR[0]), send(near, perm=FAR[1])
     far_head, near = lax.optimization_barrier((far_head, near))
     vocabulary = bring_in(lm_head, far_head)
-    near, vocabulary = lax.optimization_barrier((near, vocabulary))
-    facing = send(near, perm=FAR[2])
-    stats = [score(bases, [near], vocabulary, wanted[:size])]
-    later, first = lax.optimization_barrier((wanted[size : 3 * size], stats[0]))
-    stats = [first, score(bases, [forth, back], vocabulary, later)]
-    stats.append(score(bases, [facing], vocabulary, wanted[3 * size :]))
+    first = score(bases, [near], vocabulary, wanted, 0)
+    forth, first = lax.optimization_barrier((forth, first))
+    halves = [send(forth[: size // 2], perm=FAR[0])]
+    back, first = lax.optimization_barrier((back, first))
+    halves.append(send(back[size // 2 :], perm=FAR[1]))
+    middle = score(bases, [forth, back], vocabulary, wanted, size)
+    wanted, middle = lax.optimization_barrier((wanted, middle))
+    stats = [first, middle, score(bases, halves, vocabulary, wanted, 3 * size)]
     stats = [part[:2] for part in stats]
     stats = jnp.concatenate(stats, 1).reshape(2, GROUPS, block).transpose(1, 0, 2)
     stats = jnp.take(stats.reshape(GROUPS, 2 * block), inverse, axis=0)

time: 99.2 us -> 99.2 us (level)
  local copies, waits for them, and re-layouts: 7.6 us -> 11.3 us
  waiting for transfers between devices: 33.9 us -> 30.6 us
  starting transfers between devices: 26.6 us -> 24.8 us
  Pallas kernels: 26.4 us -> 27.6 us
    ppermute x2, waiting for transfers between devices: 11.5 us -> 4.61 us  [per_device(): forth, back = (send(near, perm=FAR[0]), send(near, perm=FAR[1]))]
    ppermute x1 -> x2, waiting for transfers between devices: 0.01 us -> 3.61 us  [the longest x1 3.6 us: per_device(): halves = [send(forth[:size // 2], perm=FAR[0])]]
    unnamed x15 -> x17, local copies, waits for them, and re-layouts: 2.25 us -> 5.63 us
    all_to_all x1, starting transfers between devices: 9.52 us -> 6.43 us  [per_device(): stats = lax.all_to_all(stats, AXES, 0, 0, tiled=True)]
    ppermute x1 -> x2, starting transfers between devices: 2.15 us -> 3.48 us  [the longest x1 3.47 us: per_device(): halves.append(send(back[size // 2:], perm=FAR[1]))]
    pallas_call x3, Pallas kernels: 11.8 us -> 13 us  [score(): pl.pallas_call(functools.partial(score_kernel, count, offset), grid_spec=...]
  transfers between devices with their start and end apart: 11 -> 12, of which waited for: 9 -> 9; matrix products, arithmetic and copies ran while one was open for 5% -> 4% of each run, Pallas kernels for 11% -> 13%
where the time goes in v4:
time: 99.2 us; the launch traced here: 98.3 us
  waiting for transfers between devices  30.6 us (31%)
  Pallas kernels  27.6 us (28%)
  starting transfers between devices  24.8 us (25%)
  local copies, waits for them, and re-layouts  11.3 us (11%)
  other arithmetic  3.74 us (4%)
    pallas_call x3, Pallas kernels, score(): pl.pallas_call(functools.partial(score_kernel, count, offset), grid_spec=...  13 us
    pallas_call x1, Pallas kernels, front(): pl.pallas_call(front_kernel, grid_spec=pltpu.PrefetchScalarGridSpec(num_s...  12.1 us
    all_to_all x1, waiting for transfers between devices, per_device(): stats = lax.all_to_all(stats, AXES, 0, 0, tiled=True)  9.46 us
    all_to_all x1, starting transfers between devices, per_device(): stats = lax.all_to_all(stats, AXES, 0, 0, tiled=True)  6.43 us
    ppermute x3, waiting for transfers between devices, per_device(): near = jnp.concatenate([both] + [send(both, perm=p) for p in NEAR], 0)  6.35 us
    unnamed x17, local copies, waits for them, and re-layouts  5.63 us
    ppermute x3, starting transfers between devices, per_device(): near = jnp.concatenate([both] + [send(both, perm=p) for p in NEAR], 0)  5.37 us
    ppermute x2, waiting for transfers between devices, per_device(): forth, back = (send(near, perm=FAR[0]), send(near, perm=FAR[1]))  4.61 us
  transfers between devices with their start and end apart: 12, of which 9 were waited for; matrix products, arithmetic and copies ran while one was open for 4% of the time, Pallas kernels for 13%

profile of v4, /device:TPU:0, one launch (start us, length us, event | category | flops | bytes accessed | tf_op | source)
XLA Modules:
  0.0 98.3 jit_solution(7797005990872852751)
XLA Ops:
  0.0 0.7 pad_add_fusion.spot
  0.7 12.1 %front.1 = (bf16[32,2048]{1,0:T(8,128)(2,1)}, f32[32,2048]{1,0:T(8,128)}) custom-call(s32[3]{0:T(128)} %pad_add_fusion.spot, f32[32]{0:T(128)} %rate.1, f32[32]{0:T(128)} %offset.1, bf16[4,16,2048]{2,1,0:T(8,128)(2,1)} %embedded.1, bf16[16,8,128,128]{3,2,1,0:T(8,128)(2,1)} %states.1, bf16[2048,512]{1,0:T(8,128)(2,1)} %w_query.1, bf16[2048,512]{1,0:T(8,128)(2,1)} %w_key.1, ...), custom_call_target="tpu_custom_call" | custom-call | flops 1073741824 | bytes 22020096 | tf_op jit(solution)/shard_map/front/pallas_call | solution.py:197
  13.5 0.7 fusion.2
  14.3 1.0 %add_convert_fusion = bf16[32,2048]{1,0:T(8,128)(2,1)S(1)} fusion(f32[32,2048]{1,0:T(8,128)} %get-tuple-element.22, bf16[32,2048]{1,0:T(8,128)(2,1)S(1)} %collective-permute-done), kind=kLoop, calls=%fused_computation.6 | loop fusion | flops 196608 | bytes 524288 | tf_op jit(solution)/shard_map/convert_element_type | solution.py:377
  15.3 1.7 %collective-permute-start.1 = (bf16[32,2048]{1,0:T(8,128)(2,1)S(1)}, bf16[32,2048]{1,0:T(8,128)(2,1)S(1)}, u32[]{:S(2)}, u32[]{:S(2)}) collective-permute-start(bf16[32,2048]{1,0:T(8,128)(2,1)S(1)} %add_convert_fusion), channel_id=1, source_target_pairs={{0,64},{1,65},{2,66},{3,67},{4,68},{5,69},{6,70},{7,71},{8,72},{9,... | collective-permute-start | bytes 393224 | tf_op jit(solution)/shard_map/ppermute | solution.py:383
  17.0 0.6 gather_fusion
  17.8 3.1 %collective-permute-done.1 = bf16[32,2048]{1,0:T(8,128)(2,1)S(1)} collective-permute-done((bf16[32,2048]{1,0:T(8,128)(2,1)S(1)}, bf16[32,2048]{1,0:T(8,128)(2,1)S(1)}, u32[]{:S(2)}, u32[]{:S(2)}) %collective-permute-start.1) | collective-permute-done | bytes 131104 | tf_op jit(solution)/shard_map/ppermute | solution.py:383
  21.3 3.2 %collective-permute-start.2 = (bf16[32,2048]{1,0:T(8,128)(2,1)S(1)}, bf16[32,2048]{1,0:T(8,128)(2,1)S(1)}, u32[]{:S(2)}, u32[]{:S(2)}) collective-permute-start(bf16[32,2048]{1,0:T(8,128)(2,1)S(1)} %get-tuple-element.40), channel_id=1, source_target_pairs={{0,1},{1,0},{2,3},{3,2},{4,5},{5,4},{6,7},{7,6},{8,9},{9,8},{10,11... | collective-permute-start | bytes 393224 | tf_op jit(solution)/shard_map/ppermute | solution.py:392
  24.4 3.4 %collective-permute-done.2 = bf16[32,2048]{1,0:T(8,128)(2,1)S(1)} collective-permute-done((bf16[32,2048]{1,0:T(8,128)(2,1)S(1)}, bf16[32,2048]{1,0:T(8,128)(2,1)S(1)}, u32[]{:S(2)}, u32[]{:S(2)}) %collective-permute-start.2) | collective-permute-done | bytes 131104 | tf_op jit(solution)/shard_map/ppermute | solution.py:392
  27.8 1.7 %collective-permute-start.3 = (bf16[64,2048]{1,0:T(8,128)(2,1)S(1)}, bf16[64,2048]{1,0:T(8,128)(2,1)S(1)}, u32[]{:S(2)}, u32[]{:S(2)}) collective-permute-start(bf16[64,2048]{1,0:T(8,128)(2,1)S(1)} %pad_maximum_fusion), channel_id=1, source_target_pairs={{0,8},{1,9},{2,10},{3,11},{4,12},{5,13},{6,14},{7,15},{8,16},{9,17... | collective-permute-start | bytes 786440 | tf_op jit(solution)/shard_map/ppermute | solution.py:393
  29.6 1.6 %collective-permute-start.4 = (bf16[64,2048]{1,0:T(8,128)(2,1)S(1)}, bf16[64,2048]{1,0:T(8,128)(2,1)S(1)}, u32[]{:S(2)}, u32[]{:S(2)}) collective-permute-start(bf16[64,2048]{1,0:T(8,128)(2,1)S(1)} %pad_maximum_fusion), channel_id=1, source_target_pairs={{0,24},{1,25},{2,26},{3,27},{4,28},{5,29},{6,30},{7,31},{8,0},{9,1... | collective-permute-start | bytes 786440 | tf_op jit(solution)/shard_map/ppermute | solution.py:393
  31.1 2.1 %collective-permute-start.5 = (bf16[64,2048]{1,0:T(8,128)(2,1)S(1)}, bf16[64,2048]{1,0:T(8,128)(2,1)S(1)}, u32[]{:S(2)}, u32[]{:S(2)}) collective-permute-start(bf16[64,2048]{1,0:T(8,128)(2,1)S(1)} %pad_maximum_fusion), channel_id=1, source_target_pairs={{0,16},{1,17},{2,18},{3,19},{4,20},{5,21},{6,22},{7,23},{8,24},{9,... | collective-permute-start | bytes 786440 | tf_op jit(solution)/shard_map/ppermute | solution.py:393
  33.2 2.3 %collective-permute-done.3 = bf16[64,2048]{1,0:T(8,128)(2,1)S(1)} collective-permute-done((bf16[64,2048]{1,0:T(8,128)(2,1)S(1)}, bf16[64,2048]{1,0:T(8,128)(2,1)S(1)}, u32[]{:S(2)}, u32[]{:S(2)}) %collective-permute-start.3) | collective-permute-done | bytes 262176 | tf_op jit(solution)/shard_map/ppermute | solution.py:393
  35.9 3.7 %collective-permute-done.5 = bf16[64,2048]{1,0:T(8,128)(2,1)S(1)} collective-permute-done((bf16[64,2048]{1,0:T(8,128)(2,1)S(1)}, bf16[64,2048]{1,0:T(8,128)(2,1)S(1)}, u32[]{:S(2)}, u32[]{:S(2)}) %collective-permute-start.5) | collective-permute-done | bytes 262176 | tf_op jit(solution)/shard_map/ppermute | solution.py:393
  39.6 2.0 %collective-permute-start.7 = (bf16[256,2048]{1,0:T(8,128)(2,1)S(1)}, bf16[256,2048]{1,0:T(8,128)(2,1)S(1)}, u32[]{:S(2)}, u32[]{:S(2)}) collective-permute-start(bf16[256,2048]{1,0:T(8,128)(2,1)S(1)} %constant_dynamic-update-slice_fusion.refs_0_), channel_id=1, source_target_pairs={{0,2},{1,3},{2,4},{3,5},{4,6},{5,7},{6,0},{7,1},{8,10},{9,11},{10,... | collective-permute-start | bytes 3145736 | tf_op jit(solution)/shard_map/ppermute | solution.py:395
  41.6 2.2 %collective-permute-start.6 = (bf16[256,2048]{1,0:T(8,128)(2,1)S(1)}, bf16[256,2048]{1,0:T(8,128)(2,1)}, u32[]{:S(2)}, u32[]{:S(2)}) collective-permute-start(bf16[256,2048]{1,0:T(8,128)(2,1)S(1)} %constant_dynamic-update-slice_fusion.refs_0_), channel_id=1, source_target_pairs={{0,6},{1,7},{2,0},{3,1},{4,2},{5,3},{6,4},{7,5},{8,14},{9,15},{10,... | collective-permute-start | bytes 3145736 | tf_op jit(solution)/shard_map/ppermute | solution.py:395
  44.1 2.2 %copy-done.3 = bf16[2048,1024]{1,0:T(8,128)(2,1)S(1)} copy-done((bf16[2048,1024]{1,0:T(8,128)(2,1)S(1)}, bf16[2048,1024]{1,0:T(8,128)(2,1)}, u32[]{:S(2)}) %copy-start.3) | copy-done | bytes 4194328
  46.3 2.5 %bring_in.1.refs_1_.refs_2_ = bf16[2,2048,1024]{2,1,0:T(8,128)(2,1)S(1)} custom-call(bf16[2048,1024]{1,0:T(8,128)(2,1)S(1)} %copy-done.3, bf16[2048,1024]{1,0:T(8,128)(2,1)} %collective-permute-done.8.other), custom_call_target="tpu_custom_call" | custom-call | bytes 8388608 | tf_op jit(solution)/shard_map/bring_in/pallas_call | solution.py:287
  48.8 3.2 %score.3 = f32[8,256]{1,0:T(8,128)S(1)} custom-call(s32[2]{0:T(128)S(1)} %pad_add_fusion.1.bases, bf16[256,2048]{1,0:T(8,128)(2,1)S(1)} %constant_dynamic-update-slice_fusion.refs_0_, bf16[2,2048,1024]{2,1,0:T(8,128)(2,1)S(1)} %bring_in.1.refs_1_.refs_2_, s32[1024,1]{1,0:T(8,128)S(1)} %copy.34.refs_2_.refs_3_), custom_call_target="tpu_custom_call" | custom-call | flops 2147483648 | bytes 9437184 | tf_op jit(solution)/shard_map/score/pallas_call | solution.py:306
  51.9 4.6 %collective-permute-done.7.refs_0_ = bf16[256,2048]{1,0:T(8,128)(2,1)S(1)} collective-permute-done((bf16[256,2048]{1,0:T(8,128)(2,1)S(1)}, bf16[256,2048]{1,0:T(8,128)(2,1)S(1)}, u32[]{:S(2)}, u32[]{:S(2)}) %collective-permute-start.7) | collective-permute-done | bytes 1048608 | tf_op jit(solution)/shard_map/ppermute | solution.py:395
  56.5 1.1 %slice.24 = bf16[128,2048]{1,0:T(8,128)(2,1)S(1)} slice(bf16[256,2048]{1,0:T(8,128)(2,1)} %collective-permute-done.6.refs_1_), slice={[128:256], [0:2048]} | slice | bytes 1048576 | tf_op jit(solution)/shard_map/slice | solution.py:402
  57.6 3.5 %collective-permute-start.10 = (bf16[128,2048]{1,0:T(8,128)(2,1)S(1)}, bf16[128,2048]{1,0:T(8,128)(2,1)S(1)}, u32[]{:S(2)}, u32[]{:S(2)}) collective-permute-start(bf16[128,2048]{1,0:T(8,128)(2,1)S(1)} %slice.24), channel_id=1, source_target_pairs={{0,6},{1,7},{2,0},{3,1},{4,2},{5,3},{6,4},{7,5},{8,14},{9,15},{10,... | collective-permute-start | bytes 1572872 | tf_op jit(solution)/shard_map/ppermute | solution.py:402
  61.1 0.8 slice.23
  62.0 6.7 %score.4 = f32[8,512]{1,0:T(8,128)S(1)} custom-call(s32[2]{0:T(128)S(1)} %pad_add_fusion.1.bases, bf16[256,2048]{1,0:T(8,128)(2,1)S(1)} %collective-permute-done.7.refs_0_, bf16[256,2048]{1,0:T(8,128)(2,1)} %collective-permute-done.6.refs_1_, bf16[2,2048,1024]{2,1,0:T(8,128)(2,1)S(1)} %bring_in.1.refs_1_.refs_2_, s32[1024,1]{1,0:T(8,128)S(1)} %copy.34.refs_2_.refs_3_), custom_call_target="tpu_custom_call" | custom-call | flops 4294967296 | bytes 10485760 | tf_op jit(solution)/shard_map/score/pallas_call | solution.py:306
  68.9 3.6 %collective-permute-done.9.refs_0_ = bf16[128,2048]{1,0:T(8,128)(2,1)S(1)} collective-permute-done((bf16[128,2048]{1,0:T(8,128)(2,1)}, bf16[128,2048]{1,0:T(8,128)(2,1)S(1)}, u32[]{:S(2)}, u32[]{:S(2)}) %collective-permute-start.9) | collective-permute-done | bytes 524320 | tf_op jit(solution)/shard_map/ppermute | solution.py:400
  72.5 3.4 %copy-done.2 = bf16[2,2048,1024]{2,1,0:T(8,128)(2,1)S(1)} copy-done((bf16[2,2048,1024]{2,1,0:T(8,128)(2,1)S(1)}, bf16[2,2048,1024]{2,1,0:T(8,128)(2,1)}, u32[]{:S(2)}) %copy-start.2) | copy-done | bytes 8388632
  75.9 3.1 %score.5 = f32[8,256]{1,0:T(8,128)S(1)} custom-call(s32[2]{0:T(128)S(1)} %pad_add_fusion.1.bases, bf16[128,2048]{1,0:T(8,128)(2,1)S(1)} %collective-permute-done.9.refs_0_, bf16[128,2048]{1,0:T(8,128)(2,1)S(1)} %collective-permute-done.10.refs_1_, bf16[2,2048,1024]{2,1,0:T(8,128)(2,1)S(1)} %copy-done.2, s32[1024,1]{1,0:T(8,128)S(1)} %copy.36.refs_3_), custom_call_target="tpu_custom_call" | custom-call | flops 2147483648 | bytes 9437184 | tf_op jit(solution)/shard_map/score/pallas_call | solution.py:306
  79.3 0.6 gather_fusion.1
  79.9 0.6 broadcast_in_dim.50
  80.6 6.4 %all-to-all-start = ((f32[128,1,64]{2,1,0:T(1,128)}), f32[128,1,64]{2,1,0:T(1,128)S(1)}, u32[]{:S(2)}, u32[]{:S(2)}) async-start(f32[128,1,64]{2,1,0:T(1,128)} %bitcast.17), calls=%async_computation | async-start | bytes 131072 | tf_op jit(solution)/shard_map/all_to_all | solution.py:410
  87.0 9.5 %all-to-all-done = f32[128,1,64]{2,1,0:T(1,128)S(1)} async-done(((f32[128,1,64]{2,1,0:T(1,128)}), f32[128,1,64]{2,1,0:T(1,128)S(1)}, u32[]{:S(2)}, u32[]{:S(2)}) %all-to-all-start) | async-done | bytes 32800 | tf_op jit(solution)/shard_map/all_to_all | solution.py:410
  97.0 1.3 %select_bitcast_fusion = f32[16,4]{0,1:T(4,128)} fusion(f32[4,16]{1,0:T(4,128)S(1)} %bitcast.38, s32[512,4]{0,1:T(4,128)} %param.35, s32[]{:T(128)S(6)} %select_n.41), kind=kLoop, calls=%fused_computation.22 | loop fusion | flops 128 | bytes 772 | tf_op jit(solution)/shard_map/transpose | solution.py:414
  (57 shorter events, 3.1 us)
Async XLA Ops:
  0.0 13.3 %copy-start = (s32[512,4]{0,1:T(4,128)S(1)}, s32[512,4]{0,1:T(4,128)}, u32[]{:S(2)}) copy-start(s32[512,4]{0,1:T(4,128)} %param.34) | copy-start | bytes 24580
  0.7 12.6 %copy-start.5 = (bf16[4,16,2048]{2,1,0:T(8,128)(2,1)S(1)}, bf16[4,16,2048]{2,1,0:T(8,128)(2,1)}, u32[]{:S(2)}) copy-start(bf16[4,16,2048]{2,1,0:T(8,128)(2,1)} %embedded.1) | copy-start | bytes 786436
  0.7 20.5 %copy-start.6 = (f32[2048]{0:T(1024)S(1)}, f32[2048]{0:T(1024)}, u32[]{:S(2)}) copy-start(f32[2048]{0:T(1024)} %param.32) | copy-start | bytes 24580
  12.8 1.6 %collective-permute-start = (bf16[32,2048]{1,0:T(8,128)(2,1)}, bf16[32,2048]{1,0:T(8,128)(2,1)S(1)}, u32[]{:S(2)}, u32[]{:S(2)}) collective-permute-start(bf16[32,2048]{1,0:T(8,128)(2,1)} %get-tuple-element.23), channel_id=1, source_target_pairs={{0,32},{1,33},{2,34},{3,35},{4,36},{5,37},{6,38},{7,39},{8,40},{9,... | collective-permute-start | bytes 393224 | tf_op jit(solution)/shard_map/ppermute | solution.py:377
  12.8 31.3 %collective-permute-start.8 = (bf16[2048,1024]{1,0:T(8,128)(2,1)}, bf16[2048,1024]{1,0:T(8,128)(2,1)}, u32[]{:S(2)}, u32[]{:S(2)}) collective-permute-start(bf16[2048,1024]{1,0:T(8,128)(2,1)} %own.1), channel_id=1, source_target_pairs={{0,32},{1,33},{2,34},{3,35},{4,36},{5,37},{6,38},{7,39},{8,40},{9,... | collective-permute-start | bytes 12582920 | tf_op jit(solution)/shard_map/ppermute | solution.py:351
  15.3 5.6 %collective-permute-start.1 = (bf16[32,2048]{1,0:T(8,128)(2,1)S(1)}, bf16[32,2048]{1,0:T(8,128)(2,1)S(1)}, u32[]{:S(2)}, u32[]{:S(2)}) collective-permute-start(bf16[32,2048]{1,0:T(8,128)(2,1)S(1)} %add_convert_fusion), channel_id=1, source_target_pairs={{0,64},{1,65},{2,66},{3,67},{4,68},{5,69},{6,70},{7,71},{8,72},{9,... | collective-permute-start | bytes 393224 | tf_op jit(solution)/shard_map/ppermute | solution.py:383
  21.3 6.6 %collective-permute-start.2 = (bf16[32,2048]{1,0:T(8,128)(2,1)S(1)}, bf16[32,2048]{1,0:T(8,128)(2,1)S(1)}, u32[]{:S(2)}, u32[]{:S(2)}) collective-permute-start(bf16[32,2048]{1,0:T(8,128)(2,1)S(1)} %get-tuple-element.40), channel_id=1, source_target_pairs={{0,1},{1,0},{2,3},{3,2},{4,5},{5,4},{6,7},{7,6},{8,9},{9,8},{10,11... | collective-permute-start | bytes 393224 | tf_op jit(solution)/shard_map/ppermute | solution.py:392
  27.8 7.7 %collective-permute-start.3 = (bf16[64,2048]{1,0:T(8,128)(2,1)S(1)}, bf16[64,2048]{1,0:T(8,128)(2,1)S(1)}, u32[]{:S(2)}, u32[]{:S(2)}) collective-permute-start(bf16[64,2048]{1,0:T(8,128)(2,1)S(1)} %pad_maximum_fusion), channel_id=1, source_target_pairs={{0,8},{1,9},{2,10},{3,11},{4,12},{5,13},{6,14},{7,15},{8,16},{9,17... | collective-permute-start | bytes 786440 | tf_op jit(solution)/shard_map/ppermute | solution.py:393
  29.6 6.4 %collective-permute-start.4 = (bf16[64,2048]{1,0:T(8,128)(2,1)S(1)}, bf16[64,2048]{1,0:T(8,128)(2,1)S(1)}, u32[]{:S(2)}, u32[]{:S(2)}) collective-permute-start(bf16[64,2048]{1,0:T(8,128)(2,1)S(1)} %pad_maximum_fusion), channel_id=1, source_target_pairs={{0,24},{1,25},{2,26},{3,27},{4,28},{5,29},{6,30},{7,31},{8,0},{9,1... | collective-permute-start | bytes 786440 | tf_op jit(solution)/shard_map/ppermute | solution.py:393
  31.1 8.5 %collective-permute-start.5 = (bf16[64,2048]{1,0:T(8,128)(2,1)S(1)}, bf16[64,2048]{1,0:T(8,128)(2,1)S(1)}, u32[]{:S(2)}, u32[]{:S(2)}) collective-permute-start(bf16[64,2048]{1,0:T(8,128)(2,1)S(1)} %pad_maximum_fusion), channel_id=1, source_target_pairs={{0,16},{1,17},{2,18},{3,19},{4,20},{5,21},{6,22},{7,23},{8,24},{9,... | collective-permute-start | bytes 786440 | tf_op jit(solution)/shard_map/ppermute | solution.py:393
  39.6 16.9 %collective-permute-start.7 = (bf16[256,2048]{1,0:T(8,128)(2,1)S(1)}, bf16[256,2048]{1,0:T(8,128)(2,1)S(1)}, u32[]{:S(2)}, u32[]{:S(2)}) collective-permute-start(bf16[256,2048]{1,0:T(8,128)(2,1)S(1)} %constant_dynamic-update-slice_fusion.refs_0_), channel_id=1, source_target_pairs={{0,2},{1,3},{2,4},{3,5},{4,6},{5,7},{6,0},{7,1},{8,10},{9,11},{10,... | collective-permute-start | bytes 3145736 | tf_op jit(solution)/shard_map/ppermute | solution.py:395
  41.6 14.9 %collective-permute-start.6 = (bf16[256,2048]{1,0:T(8,128)(2,1)S(1)}, bf16[256,2048]{1,0:T(8,128)(2,1)}, u32[]{:S(2)}, u32[]{:S(2)}) collective-permute-start(bf16[256,2048]{1,0:T(8,128)(2,1)S(1)} %constant_dynamic-update-slice_fusion.refs_0_), channel_id=1, source_target_pairs={{0,6},{1,7},{2,0},{3,1},{4,2},{5,3},{6,4},{7,5},{8,14},{9,15},{10,... | collective-permute-start | bytes 3145736 | tf_op jit(solution)/shard_map/ppermute | solution.py:395
  44.1 2.2 %copy-start.3 = (bf16[2048,1024]{1,0:T(8,128)(2,1)S(1)}, bf16[2048,1024]{1,0:T(8,128)(2,1)}, u32[]{:S(2)}) copy-start(bf16[2048,1024]{1,0:T(8,128)(2,1)} %own.1) | copy-start | bytes 12582916
  48.8 13.2 %copy-start.1 = (bf16[2,2048,1024]{2,1,0:T(8,128)(2,1)}, bf16[2,2048,1024]{2,1,0:T(8,128)(2,1)S(1)}, u32[]{:S(2)}) copy-start(bf16[2,2048,1024]{2,1,0:T(8,128)(2,1)S(1)} %bring_in.1.refs_1_.refs_2_) | copy-start | bytes 25165828
  51.9 17.0 %copy-start.4 = (f32[8,256]{1,0:T(8,128)}, f32[8,256]{1,0:T(8,128)S(1)}, u32[]{:S(2)}) copy-start(f32[8,256]{1,0:T(8,128)S(1)} %score.3) | copy-start | bytes 24580
  57.6 11.3 %collective-permute-start.10 = (bf16[128,2048]{1,0:T(8,128)(2,1)S(1)}, bf16[128,2048]{1,0:T(8,128)(2,1)S(1)}, u32[]{:S(2)}, u32[]{:S(2)}) collective-permute-start(bf16[128,2048]{1,0:T(8,128)(2,1)S(1)} %slice.24), channel_id=1, source_target_pairs={{0,6},{1,7},{2,0},{3,1},{4,2},{5,3},{6,4},{7,5},{8,14},{9,15},{10,... | collective-permute-start | bytes 1572872 | tf_op jit(solution)/shard_map/ppermute | solution.py:402
  61.9 10.6 %collective-permute-start.9 = (bf16[128,2048]{1,0:T(8,128)(2,1)}, bf16[128,2048]{1,0:T(8,128)(2,1)S(1)}, u32[]{:S(2)}, u32[]{:S(2)}) collective-permute-start(bf16[128,2048]{1,0:T(8,128)(2,1)} %slice.23), channel_id=1, source_target_pairs={{0,2},{1,3},{2,4},{3,5},{4,6},{5,7},{6,0},{7,1},{8,10},{9,11},{10,... | collective-permute-start | bytes 1572872 | tf_op jit(solution)/shard_map/ppermute | solution.py:400
  72.5 3.4 %copy-start.2 = (bf16[2,2048,1024]{2,1,0:T(8,128)(2,1)S(1)}, bf16[2,2048,1024]{2,1,0:T(8,128)(2,1)}, u32[]{:S(2)}) copy-start(bf16[2,2048,1024]{2,1,0:T(8,128)(2,1)} %copy-done.1) | copy-start | bytes 25165828
  75.9 3.2 %slice-start = ((f32[8,256]{1,0:T(8,128)}), f32[2,256]{1,0:T(2,128)S(1)}, s32[]{:S(2)}) async-start(f32[8,256]{1,0:T(8,128)} %copy-done.4), calls=%async_computation.1 | async-start | bytes 4096 | tf_op jit(solution)/shard_map/slice | solution.py:406
  80.6 15.9 %all-to-all-start = ((f32[128,1,64]{2,1,0:T(1,128)}), f32[128,1,64]{2,1,0:T(1,128)S(1)}, u32[]{:S(2)}, u32[]{:S(2)}) async-start(f32[128,1,64]{2,1,0:T(1,128)} %bitcast.17), calls=%async_computation | async-start | bytes 131072 | tf_op jit(solution)/shard_map/all_to_all | solution.py:410

commit v5 on v4

--- a/solution.py
+++ b/solution.py
@@ -240,21 +240,20 @@
 
 
 TILE = 512
-BLOCK = 256
 
 
 def score_kernel(count, offset, bases, *refs):
     parts, (vocabulary, target, stats) = refs[:count], refs[count:]
     cols = vocabulary.shape[2]
-    if parts[0].shape[0] < BLOCK:
-        pieces = [jnp.concatenate([part[...] for part in parts], axis=0)]
-    else:
-        pieces = [part[...] for part in parts]
+    pieces = [
+        jnp.concatenate([parts[i][...], parts[i + 1][...]], axis=0) for i in range(0, count, 2)
+    ]
     size = pieces[0].shape[0]
     for p, piece in enumerate(pieces):
         at = slice(p * size, (p + 1) * size)
-        want = target[offset + p * size : offset + (p + 1) * size, :]
         lane = lax.broadcasted_iota(jnp.int32, (size, 128), 1)
+        want = target[:, offset + p * size : offset + (p + 1) * size]
+        want = jnp.broadcast_to(want, (128, size)).T - lane
         running = jnp.zeros((size, 128), F32)
         found = jnp.zeros((size, 128), F32)
         for start in range(0, cols, TILE):
@@ -262,7 +261,7 @@
                 logits = jnp.dot(
                     piece, vocabulary[which, :, start : start + TILE], preferred_element_type=F32
                 )
-                left = jnp.broadcast_to(want - (bases[which] + start), (size, 128)) - lane
+                left = want - (bases[which] + start)
                 for s in range(0, TILE, 128):
                     part = logits[:, s : s + 128]
                     running = running + jnp.exp(part)
@@ -379,7 +378,7 @@
     pair, order, inverse, bases = lax.optimization_barrier((pair, order, inverse, bases))
     wanted = lax.dynamic_slice_in_dim(targets.T, core * (steps // 2), steps // 2, 0)
     wanted = jnp.take(wanted.reshape(steps // 2, GROUPS, group), order, axis=1)
-    wanted = wanted.transpose(1, 0, 2).reshape(GROUPS * block, 1)
+    wanted = wanted.transpose(1, 0, 2).reshape(1, GROUPS * block)
     from_low = send(pair, perm=OTHER_LOW)
     from_low, wanted, inverse = lax.optimization_barrier((from_low, wanted, inverse))
     summed = pair.astype(F32) + from_low.astype(F32)
@@ -390,19 +389,21 @@
     ).astype(BF16)
 
     both = jnp.concatenate([hidden, send(hidden, perm=OTHER_HIGH)], 0)
-    near = jnp.concatenate([both] + [send(both, perm=p) for p in NEAR], 0)
-    size = near.shape[0]
-    forth, back = send(near, perm=FAR[0]), send(near, perm=FAR[1])
-    far_head, near = lax.optimization_barrier((far_head, near))
+    ahead, behind, across = [send(both, perm=p) for p in NEAR]
+    one, two = jnp.concatenate([both, ahead], 0), jnp.concatenate([behind, across], 0)
+    size = one.shape[0]
+    forth_one, back_two = send(one, perm=FAR[0]), send(two, perm=FAR[1])
+    forth_two, back_one = send(two, perm=FAR[0]), send(one, perm=FAR[1])
+    far_head, one = lax.optimization_barrier((far_head, one))
     vocabulary = bring_in(lm_head, far_head)
-    first = score(bases, [near], vocabulary, wanted, 0)
-    forth, first = lax.optimization_barrier((forth, first))
-    halves = [send(forth[: size // 2], perm=FAR[0])]
-    back, first = lax.optimization_barrier((back, first))
-    halves.append(send(back[size // 2 :], perm=FAR[1]))
-    middle = score(bases, [forth, back], vocabulary, wanted, size)
+    vocabulary, forth_one, back_two = lax.optimization_barrier((vocabulary, forth_one, back_two))
+    halves = [send(forth_one, perm=FAR[0]), send(back_two, perm=FAR[1])]
+    first = score(bases, [one, two], vocabulary, wanted, 0)
+    wanted, first = lax.optimization_barrier((wanted, first))
+    middle = [forth_one, forth_two, back_one, back_two]
+    middle = score(bases, middle, vocabulary, wanted, 2 * size)
     wanted, middle = lax.optimization_barrier((wanted, middle))
-    stats = [first, middle, score(bases, halves, vocabulary, wanted, 3 * size)]
+    stats = [first, middle, score(bases, halves, vocabulary, wanted, 6 * size)]
     stats = [part[:2] for part in stats]
     stats = jnp.concatenate(stats, 1).reshape(2, GROUPS, block).transpose(1, 0, 2)
     stats = jnp.take(stats.reshape(GROUPS, 2 * block), inverse, axis=0)

time: 99.2 us -> 90.2 us (0.909)
  waiting for transfers between devices: 30.6 us -> 20.8 us
  starting transfers between devices: 24.8 us -> 32.8 us
  local copies, waits for them, and re-layouts: 11.3 us -> 5.54 us
  Pallas kernels: 27.6 us -> 26.4 us
    ppermute x7 -> x9, waiting for transfers between devices: 14.6 us -> 4.73 us  [the longest x3 4.71 us: per_device(): ahead, behind, across = [send(both, perm=p) for p in NEAR]]
    ppermute x7 -> x9, starting transfers between devices: 13 us -> 20.4 us  [the longest x2 8.47 us: per_device(): forth_one, back_two = (send(one, perm=FAR[0]), send(two, perm=FAR[1]))]
    unnamed x17 -> x11, local copies, waits for them, and re-layouts: 5.63 us -> 2.22 us
    slice x2 -> x0, local copies, waits for them, and re-layouts: 1.91 us -> none  [the longest x1 1.08 us: per_device(): halves.append(send(back[size // 2:], perm=FAR[1]))]
    pallas_call x3, Pallas kernels: 13 us -> 11.8 us  [score(): pl.pallas_call(functools.partial(score_kernel, count, offset), grid_spec=...]
  transfers between devices with their start and end apart: 12 -> 14, of which waited for: 9 -> 6; matrix products, arithmetic and copies ran while one was open for 4% -> 3% of each run, Pallas kernels for 13% -> 12%
where the time goes in v5:
time: 90.2 us; the launch traced here: 89.5 us
  starting transfers between devices  32.8 us (36%)
  Pallas kernels  26.4 us (29%)
  waiting for transfers between devices  20.8 us (23%)
  local copies, waits for them, and re-layouts  5.54 us (6%)
  other arithmetic  3.76 us (4%)
    pallas_call x1, Pallas kernels, front(): pl.pallas_call(front_kernel, grid_spec=pltpu.PrefetchScalarGridSpec(num_s...  12.1 us
    pallas_call x3, Pallas kernels, score(): pl.pallas_call(functools.partial(score_kernel, count, offset), grid_spec=...  11.8 us
    all_to_all x1, waiting for transfers between devices, per_device(): stats = lax.all_to_all(stats, AXES, 0, 0, tiled=True)  9.46 us
    ppermute x2, starting transfers between devices, per_device(): forth_one, back_two = (send(one, perm=FAR[0]), send(two, perm=FAR[1]))  8.47 us
    all_to_all x1, starting transfers between devices, per_device(): stats = lax.all_to_all(stats, AXES, 0, 0, tiled=True)  7.05 us
    ppermute x3, starting transfers between devices, per_device(): ahead, behind, across = [send(both, perm=p) for p in NEAR]  5.37 us
    ppermute x3, waiting for transfers between devices, per_device(): ahead, behind, across = [send(both, perm=p) for p in NEAR]  4.71 us
    ppermute x1, waiting for transfers between devices, per_device(): both = jnp.concatenate([hidden, send(hidden, perm=OTHER_HIGH)], 0)  3.37 us
  transfers between devices with their start and end apart: 14, of which 6 were waited for; matrix products, arithmetic and copies ran while one was open for 3% of the time, Pallas kernels for 12%

profile of v5, /device:TPU:0, one launch (start us, length us, event | category | flops | bytes accessed | tf_op | source)
XLA Modules:
  0.0 89.5 jit_solution(3896679063191352238)
XLA Ops:
  0.0 0.7 pad_add_fusion.spot
  0.7 12.1 %front.1 = (bf16[32,2048]{1,0:T(8,128)(2,1)}, f32[32,2048]{1,0:T(8,128)}) custom-call(s32[3]{0:T(128)} %pad_add_fusion.spot, f32[32]{0:T(128)} %rate.1, f32[32]{0:T(128)} %offset.1, bf16[4,16,2048]{2,1,0:T(8,128)(2,1)} %embedded.1, bf16[16,8,128,128]{3,2,1,0:T(8,128)(2,1)} %states.1, bf16[2048,512]{1,0:T(8,128)(2,1)} %w_query.1, bf16[2048,512]{1,0:T(8,128)(2,1)} %w_key.1, ...), custom_call_target="tpu_custom_call" | custom-call | flops 1073741824 | bytes 22020096 | tf_op jit(solution)/shard_map/front/pallas_call | solution.py:197
  12.8 0.5 collective-permute-start.2
  13.6 0.7 fusion.2
  14.4 1.0 %add_convert_fusion = bf16[32,2048]{1,0:T(8,128)(2,1)S(1)} fusion(f32[32,2048]{1,0:T(8,128)} %get-tuple-element.23, bf16[32,2048]{1,0:T(8,128)(2,1)S(1)} %collective-permute-done), kind=kLoop, calls=%fused_computation.7 | loop fusion | flops 196608 | bytes 524288 | tf_op jit(solution)/shard_map/convert_element_type | solution.py:376
  15.3 1.7 %collective-permute-start.1 = (bf16[32,2048]{1,0:T(8,128)(2,1)S(1)}, bf16[32,2048]{1,0:T(8,128)(2,1)S(1)}, u32[]{:S(2)}, u32[]{:S(2)}) collective-permute-start(bf16[32,2048]{1,0:T(8,128)(2,1)S(1)} %add_convert_fusion), channel_id=1, source_target_pairs={{0,64},{1,65},{2,66},{3,67},{4,68},{5,69},{6,70},{7,71},{8,72},{9,... | collective-permute-start | bytes 393224 | tf_op jit(solution)/shard_map/ppermute | solution.py:382
  17.0 0.6 gather_fusion
  17.8 3.1 %collective-permute-done.1 = bf16[32,2048]{1,0:T(8,128)(2,1)S(1)} collective-permute-done((bf16[32,2048]{1,0:T(8,128)(2,1)S(1)}, bf16[32,2048]{1,0:T(8,128)(2,1)S(1)}, u32[]{:S(2)}, u32[]{:S(2)}) %collective-permute-start.1) | collective-permute-done | bytes 131104 | tf_op jit(solution)/shard_map/ppermute | solution.py:382
  21.0 0.2 multiply_reduce_fusion
  21.3 3.2 %collective-permute-start.3 = (bf16[32,2048]{1,0:T(8,128)(2,1)S(1)}, bf16[32,2048]{1,0:T(8,128)(2,1)S(1)}, u32[]{:S(2)}, u32[]{:S(2)}) collective-permute-start(bf16[32,2048]{1,0:T(8,128)(2,1)S(1)} %multiply_convert_fusion), channel_id=1, source_target_pairs={{0,1},{1,0},{2,3},{3,2},{4,5},{5,4},{6,7},{7,6},{8,9},{9,8},{10,11... | collective-permute-start | bytes 393224 | tf_op jit(solution)/shard_map/ppermute | solution.py:391
  24.4 3.4 %collective-permute-done.3 = bf16[32,2048]{1,0:T(8,128)(2,1)S(1)} collective-permute-done((bf16[32,2048]{1,0:T(8,128)(2,1)S(1)}, bf16[32,2048]{1,0:T(8,128)(2,1)S(1)}, u32[]{:S(2)}, u32[]{:S(2)}) %collective-permute-start.3) | collective-permute-done | bytes 131104 | tf_op jit(solution)/shard_map/ppermute | solution.py:391
  27.8 1.7 %collective-permute-start.4 = (bf16[64,2048]{1,0:T(8,128)(2,1)S(1)}, bf16[64,2048]{1,0:T(8,128)(2,1)S(1)}, u32[]{:S(2)}, u32[]{:S(2)}) collective-permute-start(bf16[64,2048]{1,0:T(8,128)(2,1)S(1)} %pad_maximum_fusion.1), channel_id=1, source_target_pairs={{0,8},{1,9},{2,10},{3,11},{4,12},{5,13},{6,14},{7,15},{8,16},{9,17... | collective-permute-start | bytes 786440 | tf_op jit(solution)/shard_map/ppermute | solution.py:392
  29.6 1.6 %collective-permute-start.5 = (bf16[64,2048]{1,0:T(8,128)(2,1)S(1)}, bf16[64,2048]{1,0:T(8,128)(2,1)S(1)}, u32[]{:S(2)}, u32[]{:S(2)}) collective-permute-start(bf16[64,2048]{1,0:T(8,128)(2,1)S(1)} %pad_maximum_fusion.1), channel_id=1, source_target_pairs={{0,24},{1,25},{2,26},{3,27},{4,28},{5,29},{6,30},{7,31},{8,0},{9,1... | collective-permute-start | bytes 786440 | tf_op jit(solution)/shard_map/ppermute | solution.py:392
  31.1 2.1 %collective-permute-start.6 = (bf16[64,2048]{1,0:T(8,128)(2,1)S(1)}, bf16[64,2048]{1,0:T(8,128)(2,1)S(1)}, u32[]{:S(2)}, u32[]{:S(2)}) collective-permute-start(bf16[64,2048]{1,0:T(8,128)(2,1)S(1)} %pad_maximum_fusion.1), channel_id=1, source_target_pairs={{0,16},{1,17},{2,18},{3,19},{4,20},{5,21},{6,22},{7,23},{8,24},{9,... | collective-permute-start | bytes 786440 | tf_op jit(solution)/shard_map/ppermute | solution.py:392
  33.2 2.3 %collective-permute-done.4 = bf16[64,2048]{1,0:T(8,128)(2,1)S(1)} collective-permute-done((bf16[64,2048]{1,0:T(8,128)(2,1)S(1)}, bf16[64,2048]{1,0:T(8,128)(2,1)S(1)}, u32[]{:S(2)}, u32[]{:S(2)}) %collective-permute-start.4) | collective-permute-done | bytes 262176 | tf_op jit(solution)/shard_map/ppermute | solution.py:392
  35.5 2.1 %collective-permute-start.7 = (bf16[128,2048]{1,0:T(8,128)(2,1)S(1)}, bf16[128,2048]{1,0:T(8,128)(2,1)S(1)}, u32[]{:S(2)}, u32[]{:S(2)}) collective-permute-start(bf16[128,2048]{1,0:T(8,128)(2,1)S(1)} %pad_maximum_fusion.refs_0_), channel_id=1, source_target_pairs={{0,2},{1,3},{2,4},{3,5},{4,6},{5,7},{6,0},{7,1},{8,10},{9,11},{10,... | collective-permute-start | bytes 1572872 | tf_op jit(solution)/shard_map/ppermute | solution.py:395
  37.6 2.4 %collective-permute-done.6 = bf16[64,2048]{1,0:T(8,128)(2,1)S(1)} collective-permute-done((bf16[64,2048]{1,0:T(8,128)(2,1)S(1)}, bf16[64,2048]{1,0:T(8,128)(2,1)S(1)}, u32[]{:S(2)}, u32[]{:S(2)}) %collective-permute-start.6) | collective-permute-done | bytes 262176 | tf_op jit(solution)/shard_map/ppermute | solution.py:392
  40.1 6.4 %collective-permute-start.8 = (bf16[128,2048]{1,0:T(8,128)(2,1)S(1)}, bf16[128,2048]{1,0:T(8,128)(2,1)S(1)}, u32[]{:S(2)}, u32[]{:S(2)}) collective-permute-start(bf16[128,2048]{1,0:T(8,128)(2,1)S(1)} %constant_dynamic-update-slice_fusion.refs_1_), channel_id=1, source_target_pairs={{0,6},{1,7},{2,0},{3,1},{4,2},{5,3},{6,4},{7,5},{8,14},{9,15},{10,... | collective-permute-start | bytes 1572872 | tf_op jit(solution)/shard_map/ppermute | solution.py:395
  46.5 3.2 %collective-permute-start.10 = (bf16[128,2048]{1,0:T(8,128)(2,1)S(1)}, bf16[128,2048]{1,0:T(8,128)(2,1)S(1)}, u32[]{:S(2)}, u32[]{:S(2)}) collective-permute-start(bf16[128,2048]{1,0:T(8,128)(2,1)S(1)} %pad_maximum_fusion.refs_0_), channel_id=1, source_target_pairs={{0,6},{1,7},{2,0},{3,1},{4,2},{5,3},{6,4},{7,5},{8,14},{9,15},{10,... | collective-permute-start | bytes 1572872 | tf_op jit(solution)/shard_map/ppermute | solution.py:396
  49.7 2.2 %copy-done.1 = bf16[2048,1024]{1,0:T(8,128)(2,1)S(1)} copy-done((bf16[2048,1024]{1,0:T(8,128)(2,1)S(1)}, bf16[2048,1024]{1,0:T(8,128)(2,1)}, u32[]{:S(2)}) %copy-start.1) | copy-done | bytes 4194328
  51.9 2.5 %bring_in.1.refs_2_.refs_4_ = bf16[2,2048,1024]{2,1,0:T(8,128)(2,1)S(1)} custom-call(bf16[2048,1024]{1,0:T(8,128)(2,1)S(1)} %copy-done.1, bf16[2048,1024]{1,0:T(8,128)(2,1)} %collective-permute-done.2.other), custom_call_target="tpu_custom_call" | custom-call | bytes 8388608 | tf_op jit(solution)/shard_map/bring_in/pallas_call | solution.py:286
  54.5 3.2 %collective-permute-start.12 = (bf16[128,2048]{1,0:T(8,128)(2,1)S(1)}, bf16[128,2048]{1,0:T(8,128)(2,1)S(1)}, u32[]{:S(2)}, u32[]{:S(2)}) collective-permute-start(bf16[128,2048]{1,0:T(8,128)(2,1)S(1)} %collective-permute-done.8.refs_3_), channel_id=1, source_target_pairs={{0,6},{1,7},{2,0},{3,1},{4,2},{5,3},{6,4},{7,5},{8,14},{9,15},{10,... | collective-permute-start | bytes 1572872 | tf_op jit(solution)/shard_map/ppermute | solution.py:400
  57.7 3.1 %score.3 = f32[8,256]{1,0:T(8,128)S(1)} custom-call(s32[2]{0:T(128)S(1)} %pad_add_fusion.1.bases, bf16[128,2048]{1,0:T(8,128)(2,1)S(1)} %pad_maximum_fusion.refs_0_, bf16[128,2048]{1,0:T(8,128)(2,1)S(1)} %constant_dynamic-update-slice_fusion.refs_1_, bf16[2,2048,1024]{2,1,0:T(8,128)(2,1)S(1)} %bring_in.1.refs_2_.refs_4_, s32[1,1024]{1,0:T(1,128)S(1)} %reshape.58.refs_3_.refs_5_), custom_call_target="tpu_custom_call" | custom-call | flops 2147483648 | bytes 9437184 | tf_op jit(solution)/shard_map/score/pallas_call | solution.py:305
  60.9 5.5 %score.4 = f32[8,512]{1,0:T(8,128)S(1)} custom-call(s32[2]{0:T(128)S(1)} %pad_add_fusion.1.bases, bf16[128,2048]{1,0:T(8,128)(2,1)S(1)} %collective-permute-done.7.refs_0_, bf16[128,2048]{1,0:T(8,128)(2,1)S(1)} %collective-permute-done.9.refs_1_, bf16[128,2048]{1,0:T(8,128)(2,1)S(1)} %collective-permute-done.10.refs_2_, ...), custom_call_target="tpu_custom_call" | custom-call | flops 4294967296 | bytes 10485760 | tf_op jit(solution)/shard_map/score/pallas_call | solution.py:305
  66.4 3.2 %score.5 = f32[8,256]{1,0:T(8,128)S(1)} custom-call(s32[2]{0:T(128)S(1)} %pad_add_fusion.1.bases, bf16[128,2048]{1,0:T(8,128)(2,1)S(1)} %collective-permute-done.11.refs_0_, bf16[128,2048]{1,0:T(8,128)(2,1)S(1)} %collective-permute-done.12.refs_1_, bf16[2,2048,1024]{2,1,0:T(8,128)(2,1)S(1)} %bring_in.1.refs_2_.refs_4_, s32[1,1024]{1,0:T(1,128)S(1)} %reshape.58.refs_3_.refs_5_), custom_call_target="tpu_custom_call" | custom-call | flops 2147483648 | bytes 9437184 | tf_op jit(solution)/shard_map/score/pallas_call | solution.py:305
  69.8 0.6 gather_fusion.1
  70.5 0.6 broadcast_in_dim.50
  71.1 7.0 %all-to-all-start = ((f32[128,1,64]{2,1,0:T(1,128)}), f32[128,1,64]{2,1,0:T(1,128)S(1)}, u32[]{:S(2)}, u32[]{:S(2)}) async-start(f32[128,1,64]{2,1,0:T(1,128)} %bitcast.17), calls=%async_computation | async-start | bytes 131072 | tf_op jit(solution)/shard_map/all_to_all | solution.py:411
  78.2 9.5 %all-to-all-done = f32[128,1,64]{2,1,0:T(1,128)S(1)} async-done(((f32[128,1,64]{2,1,0:T(1,128)}), f32[128,1,64]{2,1,0:T(1,128)S(1)}, u32[]{:S(2)}, u32[]{:S(2)}) %all-to-all-start) | async-done | bytes 32800 | tf_op jit(solution)/shard_map/all_to_all | solution.py:411
  87.7 0.2 reshape.61
  87.9 0.1 reduce_sum.19
  88.1 1.3 %select_bitcast_fusion = f32[16,4]{0,1:T(4,128)} fusion(f32[4,16]{1,0:T(4,128)S(1)} %bitcast.38, s32[512,4]{0,1:T(4,128)} %param.35, s32[]{:T(128)S(6)} %select_n.41), kind=kLoop, calls=%fused_computation.20 | loop fusion | flops 128 | bytes 772 | tf_op jit(solution)/shard_map/transpose | solution.py:415
  (52 shorter events, 1.3 us)
Async XLA Ops:
  0.0 13.3 %copy-start = (s32[512,4]{0,1:T(4,128)S(1)}, s32[512,4]{0,1:T(4,128)}, u32[]{:S(2)}) copy-start(s32[512,4]{0,1:T(4,128)} %param.34) | copy-start | bytes 24580
  0.7 12.6 %copy-start.3 = (bf16[4,16,2048]{2,1,0:T(8,128)(2,1)S(1)}, bf16[4,16,2048]{2,1,0:T(8,128)(2,1)}, u32[]{:S(2)}) copy-start(bf16[4,16,2048]{2,1,0:T(8,128)(2,1)} %embedded.1) | copy-start | bytes 786436
  0.7 20.5 %copy-start.4 = (f32[2048]{0:T(1024)S(1)}, f32[2048]{0:T(1024)}, u32[]{:S(2)}) copy-start(f32[2048]{0:T(1024)} %param.32) | copy-start | bytes 24580
  12.8 1.6 %collective-permute-start = (bf16[32,2048]{1,0:T(8,128)(2,1)}, bf16[32,2048]{1,0:T(8,128)(2,1)S(1)}, u32[]{:S(2)}, u32[]{:S(2)}) collective-permute-start(bf16[32,2048]{1,0:T(8,128)(2,1)} %get-tuple-element.24), channel_id=1, source_target_pairs={{0,32},{1,33},{2,34},{3,35},{4,36},{5,37},{6,38},{7,39},{8,40},{9,... | collective-permute-start | bytes 393224 | tf_op jit(solution)/shard_map/ppermute | solution.py:376
  12.8 36.9 %collective-permute-start.2 = (bf16[2048,1024]{1,0:T(8,128)(2,1)}, bf16[2048,1024]{1,0:T(8,128)(2,1)}, u32[]{:S(2)}, u32[]{:S(2)}) collective-permute-start(bf16[2048,1024]{1,0:T(8,128)(2,1)} %own.1), channel_id=1, source_target_pairs={{0,32},{1,33},{2,34},{3,35},{4,36},{5,37},{6,38},{7,39},{8,40},{9,... | collective-permute-start | bytes 12582920 | tf_op jit(solution)/shard_map/ppermute | solution.py:350
  15.3 5.6 %collective-permute-start.1 = (bf16[32,2048]{1,0:T(8,128)(2,1)S(1)}, bf16[32,2048]{1,0:T(8,128)(2,1)S(1)}, u32[]{:S(2)}, u32[]{:S(2)}) collective-permute-start(bf16[32,2048]{1,0:T(8,128)(2,1)S(1)} %add_convert_fusion), channel_id=1, source_target_pairs={{0,64},{1,65},{2,66},{3,67},{4,68},{5,69},{6,70},{7,71},{8,72},{9,... | collective-permute-start | bytes 393224 | tf_op jit(solution)/shard_map/ppermute | solution.py:382
  21.3 6.6 %collective-permute-start.3 = (bf16[32,2048]{1,0:T(8,128)(2,1)S(1)}, bf16[32,2048]{1,0:T(8,128)(2,1)S(1)}, u32[]{:S(2)}, u32[]{:S(2)}) collective-permute-start(bf16[32,2048]{1,0:T(8,128)(2,1)S(1)} %multiply_convert_fusion), channel_id=1, source_target_pairs={{0,1},{1,0},{2,3},{3,2},{4,5},{5,4},{6,7},{7,6},{8,9},{9,8},{10,11... | collective-permute-start | bytes 393224 | tf_op jit(solution)/shard_map/ppermute | solution.py:391
  27.8 7.7 %collective-permute-start.4 = (bf16[64,2048]{1,0:T(8,128)(2,1)S(1)}, bf16[64,2048]{1,0:T(8,128)(2,1)S(1)}, u32[]{:S(2)}, u32[]{:S(2)}) collective-permute-start(bf16[64,2048]{1,0:T(8,128)(2,1)S(1)} %pad_maximum_fusion.1), channel_id=1, source_target_pairs={{0,8},{1,9},{2,10},{3,11},{4,12},{5,13},{6,14},{7,15},{8,16},{9,17... | collective-permute-start | bytes 786440 | tf_op jit(solution)/shard_map/ppermute | solution.py:392
  29.6 8.0 %collective-permute-start.5 = (bf16[64,2048]{1,0:T(8,128)(2,1)S(1)}, bf16[64,2048]{1,0:T(8,128)(2,1)S(1)}, u32[]{:S(2)}, u32[]{:S(2)}) collective-permute-start(bf16[64,2048]{1,0:T(8,128)(2,1)S(1)} %pad_maximum_fusion.1), channel_id=1, source_target_pairs={{0,24},{1,25},{2,26},{3,27},{4,28},{5,29},{6,30},{7,31},{8,0},{9,1... | collective-permute-start | bytes 786440 | tf_op jit(solution)/shard_map/ppermute | solution.py:392
  31.1 8.9 %collective-permute-start.6 = (bf16[64,2048]{1,0:T(8,128)(2,1)S(1)}, bf16[64,2048]{1,0:T(8,128)(2,1)S(1)}, u32[]{:S(2)}, u32[]{:S(2)}) collective-permute-start(bf16[64,2048]{1,0:T(8,128)(2,1)S(1)} %pad_maximum_fusion.1), channel_id=1, source_target_pairs={{0,16},{1,17},{2,18},{3,19},{4,20},{5,21},{6,22},{7,23},{8,24},{9,... | collective-permute-start | bytes 786440 | tf_op jit(solution)/shard_map/ppermute | solution.py:392
  35.5 18.9 %collective-permute-start.7 = (bf16[128,2048]{1,0:T(8,128)(2,1)S(1)}, bf16[128,2048]{1,0:T(8,128)(2,1)S(1)}, u32[]{:S(2)}, u32[]{:S(2)}) collective-permute-start(bf16[128,2048]{1,0:T(8,128)(2,1)S(1)} %pad_maximum_fusion.refs_0_), channel_id=1, source_target_pairs={{0,2},{1,3},{2,4},{3,5},{4,6},{5,7},{6,0},{7,1},{8,10},{9,11},{10,... | collective-permute-start | bytes 1572872 | tf_op jit(solution)/shard_map/ppermute | solution.py:395
  40.1 14.4 %collective-permute-start.8 = (bf16[128,2048]{1,0:T(8,128)(2,1)S(1)}, bf16[128,2048]{1,0:T(8,128)(2,1)S(1)}, u32[]{:S(2)}, u32[]{:S(2)}) collective-permute-start(bf16[128,2048]{1,0:T(8,128)(2,1)S(1)} %constant_dynamic-update-slice_fusion.refs_1_), channel_id=1, source_target_pairs={{0,6},{1,7},{2,0},{3,1},{4,2},{5,3},{6,4},{7,5},{8,14},{9,15},{10,... | collective-permute-start | bytes 1572872 | tf_op jit(solution)/shard_map/ppermute | solution.py:395
  46.5 14.4 %collective-permute-start.9 = (bf16[128,2048]{1,0:T(8,128)(2,1)S(1)}, bf16[128,2048]{1,0:T(8,128)(2,1)S(1)}, u32[]{:S(2)}, u32[]{:S(2)}) collective-permute-start(bf16[128,2048]{1,0:T(8,128)(2,1)S(1)} %constant_dynamic-update-slice_fusion.refs_1_), channel_id=1, source_target_pairs={{0,2},{1,3},{2,4},{3,5},{4,6},{5,7},{6,0},{7,1},{8,10},{9,11},{10,... | collective-permute-start | bytes 1572872 | tf_op jit(solution)/shard_map/ppermute | solution.py:396
  46.5 14.4 %collective-permute-start.10 = (bf16[128,2048]{1,0:T(8,128)(2,1)S(1)}, bf16[128,2048]{1,0:T(8,128)(2,1)S(1)}, u32[]{:S(2)}, u32[]{:S(2)}) collective-permute-start(bf16[128,2048]{1,0:T(8,128)(2,1)S(1)} %pad_maximum_fusion.refs_0_), channel_id=1, source_target_pairs={{0,6},{1,7},{2,0},{3,1},{4,2},{5,3},{6,4},{7,5},{8,14},{9,15},{10,... | collective-permute-start | bytes 1572872 | tf_op jit(solution)/shard_map/ppermute | solution.py:396
  49.7 2.2 %copy-start.1 = (bf16[2048,1024]{1,0:T(8,128)(2,1)S(1)}, bf16[2048,1024]{1,0:T(8,128)(2,1)}, u32[]{:S(2)}) copy-start(bf16[2048,1024]{1,0:T(8,128)(2,1)} %own.1) | copy-start | bytes 12582916
  54.4 12.0 %collective-permute-start.11 = (bf16[128,2048]{1,0:T(8,128)(2,1)S(1)}, bf16[128,2048]{1,0:T(8,128)(2,1)S(1)}, u32[]{:S(2)}, u32[]{:S(2)}) collective-permute-start(bf16[128,2048]{1,0:T(8,128)(2,1)S(1)} %collective-permute-done.7.refs_0_), channel_id=1, source_target_pairs={{0,2},{1,3},{2,4},{3,5},{4,6},{5,7},{6,0},{7,1},{8,10},{9,11},{10,... | collective-permute-start | bytes 1572872 | tf_op jit(solution)/shard_map/ppermute | solution.py:400
  54.5 11.9 %collective-permute-start.12 = (bf16[128,2048]{1,0:T(8,128)(2,1)S(1)}, bf16[128,2048]{1,0:T(8,128)(2,1)S(1)}, u32[]{:S(2)}, u32[]{:S(2)}) collective-permute-start(bf16[128,2048]{1,0:T(8,128)(2,1)S(1)} %collective-permute-done.8.refs_3_), channel_id=1, source_target_pairs={{0,6},{1,7},{2,0},{3,1},{4,2},{5,3},{6,4},{7,5},{8,14},{9,15},{10,... | collective-permute-start | bytes 1572872 | tf_op jit(solution)/shard_map/ppermute | solution.py:400
  60.9 5.5 %copy-start.2 = (f32[8,256]{1,0:T(8,128)}, f32[8,256]{1,0:T(8,128)S(1)}, u32[]{:S(2)}) copy-start(f32[8,256]{1,0:T(8,128)S(1)} %score.3) | copy-start | bytes 24580
  66.4 3.2 %slice-start = ((f32[8,256]{1,0:T(8,128)}), f32[2,256]{1,0:T(2,128)S(1)}, s32[]{:S(2)}) async-start(f32[8,256]{1,0:T(8,128)} %copy-done.2), calls=%async_computation.1 | async-start | bytes 4096 | tf_op jit(solution)/shard_map/slice | solution.py:407
  71.1 16.5 %all-to-all-start = ((f32[128,1,64]{2,1,0:T(1,128)}), f32[128,1,64]{2,1,0:T(1,128)S(1)}, u32[]{:S(2)}, u32[]{:S(2)}) async-start(f32[128,1,64]{2,1,0:T(1,128)} %bitcast.17), calls=%async_computation | async-start | bytes 131072 | tf_op jit(solution)/shard_map/all_to_all | solution.py:411

commit v6 on v5

--- a/solution.py
+++ b/solution.py
@@ -42,6 +42,7 @@
 OTHER_CORE = route(lambda xl, c, y, z, xh: (xl, 1 - c, y, z, xh))
 OTHER_LOW = route(lambda xl, c, y, z, xh: (1 - xl, c, y, z, xh))
 OTHER_HIGH = route(lambda xl, c, y, z, xh: (xl, c, y, z, 1 - xh))
+OTHER_BOTH = route(lambda xl, c, y, z, xh: (1 - xl, c, y, z, 1 - xh))
 NEAR = [shift("y", "z", k) for k in (1, 3, 2)]
 FAR = [shift("z", "y", k) for k in (1, 3, 2)]
 
@@ -184,7 +185,9 @@
     def _():
         half = rows // 2
         c = spot[2]
-        keep[...] = total[pl.ds(pl.multiple_of(c * half, half), half), :]
+        tokens = embedded[pl.ds(c * (steps // 2), steps // 2)].astype(F32).reshape(half, width)
+        first = jnp.where(spot[3] == 0, 1.0, 0.0)
+        keep[...] = total[pl.ds(pl.multiple_of(c * half, half), half), :] + tokens * first
         give[...] = total[pl.ds(pl.multiple_of((1 - c) * half, half), half), :].astype(BF16)
 
 
@@ -349,7 +352,7 @@
     send = functools.partial(lax.ppermute, axis_name=AXES)
     far_head = send(lm_head, perm=OTHER_CORE)
 
-    spot = jnp.stack([batch, head, core])
+    spot = jnp.stack([batch, head, core, lax.axis_index("xl").astype(jnp.int32)])
     give, keep = front(
         spot,
         decay_rate,
@@ -379,24 +382,23 @@
     wanted = lax.dynamic_slice_in_dim(targets.T, core * (steps // 2), steps // 2, 0)
     wanted = jnp.take(wanted.reshape(steps // 2, GROUPS, group), order, axis=1)
     wanted = wanted.transpose(1, 0, 2).reshape(1, GROUPS * block)
-    from_low = send(pair, perm=OTHER_LOW)
-    from_low, wanted, inverse = lax.optimization_barrier((from_low, wanted, inverse))
-    summed = pair.astype(F32) + from_low.astype(F32)
-    mine = lax.dynamic_slice_in_dim(embedded, core * (steps // 2), steps // 2, 0)
-    y = mine.reshape(-1, width).astype(F32) + summed
-    hidden = (
-        y * lax.rsqrt(jnp.mean(y * y, axis=-1, keepdims=True) + EPS) * final_gain
-    ).astype(BF16)
-
-    both = jnp.concatenate([hidden, send(hidden, perm=OTHER_HIGH)], 0)
+    low, corner, high = [send(pair, perm=p) for p in (OTHER_LOW, OTHER_BOTH, OTHER_HIGH)]
+    low, wanted, inverse = lax.optimization_barrier((low, wanted, inverse))
+
+    def finish(a, b):
+        y = a.astype(F32) + b.astype(F32)
+        scale = lax.rsqrt(jnp.mean(y * y, axis=-1, keepdims=True) + EPS)
+        return (y * scale * final_gain).astype(BF16)
+
+    both = jnp.concatenate([finish(pair, low), finish(high, corner)], 0)
+    far_head, both = lax.optimization_barrier((far_head, both))
+    vocabulary = bring_in(lm_head, far_head)
     ahead, behind, across = [send(both, perm=p) for p in NEAR]
+    ahead, vocabulary = lax.optimization_barrier((ahead, vocabulary))
     one, two = jnp.concatenate([both, ahead], 0), jnp.concatenate([behind, across], 0)
     size = one.shape[0]
     forth_one, back_two = send(one, perm=FAR[0]), send(two, perm=FAR[1])
     forth_two, back_one = send(two, perm=FAR[0]), send(one, perm=FAR[1])
-    far_head, one = lax.optimization_barrier((far_head, one))
-    vocabulary = bring_in(lm_head, far_head)
-    vocabulary, forth_one, back_two = lax.optimization_barrier((vocabulary, forth_one, back_two))
     halves = [send(forth_one, perm=FAR[0]), send(back_two, perm=FAR[1])]
     first = score(bases, [one, two], vocabulary, wanted, 0)
     wanted, first = lax.optimization_barrier((wanted, first))

time: 90.2 us -> 87.4 us (0.969)
  starting transfers between devices: 32.8 us -> 28.5 us
  waiting for transfers between devices: 20.8 us -> 22 us
    ppermute x3, waiting for transfers between devices: 4.71 us -> 0.01 us  [per_device(): ahead, behind, across = [send(both, perm=p) for p in NEAR]]
    ppermute x2, waiting for transfers between devices: 0.01 us -> 4.65 us  [per_device(): forth_one, back_two = (send(one, perm=FAR[0]), send(two, perm=FAR[1]))]
    ppermute x2, starting transfers between devices: 8.47 us -> 5.76 us  [per_device(): forth_one, back_two = (send(one, perm=FAR[0]), send(two, perm=FAR[1]))]
    ppermute x2, starting transfers between devices: 3.24 us -> 2.03 us  [per_device(): forth_two, back_one = (send(two, perm=FAR[0]), send(one, perm=FAR[1]))]
    ppermute x2 -> x3, waiting for transfers between devices: 6.5 us -> 7.59 us  [per_device(): send(pair, perm=p)]
    ppermute x2 -> x3, starting transfers between devices: 4.84 us -> 4.79 us  [per_device(): send(pair, perm=p)]
    unnamed x11 -> x10, local copies, waits for them, and re-layouts: 2.22 us -> 2.23 us
  transfers between devices with their start and end apart: 14 -> 15, of which waited for: 6 -> 7; matrix products, arithmetic and copies ran while one was open for 3% -> 5% of each run, Pallas kernels for 12% -> 27%
where the time goes in v6:
time: 87.4 us; the launch traced here: 86.6 us
  starting transfers between devices  28.5 us (33%)
  Pallas kernels  26.4 us (30%)
  waiting for transfers between devices  22 us (25%)
  local copies, waits for them, and re-layouts  5.55 us (6%)
  other arithmetic  3.87 us (4%)
    pallas_call x1, Pallas kernels, front(): pl.pallas_call(front_kernel, grid_spec=pltpu.PrefetchScalarGridSpec(num_s...  12.1 us
    pallas_call x3, Pallas kernels, score(): pl.pallas_call(functools.partial(score_kernel, count, offset), grid_spec=...  11.8 us
    all_to_all x1, waiting for transfers between devices, per_device(): stats = lax.all_to_all(stats, AXES, 0, 0, tiled=True)  9.47 us
    ppermute x3, waiting for transfers between devices, per_device(): send(pair, perm=p)  7.59 us
    all_to_all x1, starting transfers between devices, per_device(): stats = lax.all_to_all(stats, AXES, 0, 0, tiled=True)  6.36 us
    ppermute x2, starting transfers between devices, per_device(): forth_one, back_two = (send(one, perm=FAR[0]), send(two, perm=FAR[1]))  5.76 us
    ppermute x3, starting transfers between devices, per_device(): ahead, behind, across = [send(both, perm=p) for p in NEAR]  5.37 us
    ppermute x3, starting transfers between devices, per_device(): send(pair, perm=p)  4.79 us
  transfers between devices with their start and end apart: 15, of which 7 were waited for; matrix products, arithmetic and copies ran while one was open for 5% of the time, Pallas kernels for 27%

profile of v6, /device:TPU:0, one launch (start us, length us, event | category | flops | bytes accessed | tf_op | source)
XLA Modules:
  0.0 86.6 jit_solution(10839964472380816975)
XLA Ops:
  0.0 0.6 pad_add_fusion.spot
  0.7 12.1 %front.1 = (bf16[32,2048]{1,0:T(8,128)(2,1)}, f32[32,2048]{1,0:T(8,128)}) custom-call(s32[4]{0:T(128)} %pad_add_fusion.spot, f32[32]{0:T(128)} %rate.1, f32[32]{0:T(128)} %offset.1, bf16[4,16,2048]{2,1,0:T(8,128)(2,1)} %embedded.1, bf16[16,8,128,128]{3,2,1,0:T(8,128)(2,1)} %states.1, bf16[2048,512]{1,0:T(8,128)(2,1)} %w_query.1, bf16[2048,512]{1,0:T(8,128)(2,1)} %w_key.1, ...), custom_call_target="tpu_custom_call" | custom-call | flops 1073741824 | bytes 22020096 | tf_op jit(solution)/shard_map/front/pallas_call | solution.py:200
  12.8 0.5 collective-permute-start
  13.5 0.7 fusion.2
  14.5 1.0 %add_convert_fusion = bf16[32,2048]{1,0:T(8,128)(2,1)S(1)} fusion(f32[32,2048]{1,0:T(8,128)} %get-tuple-element.22, bf16[32,2048]{1,0:T(8,128)(2,1)S(1)} %collective-permute-done), kind=kLoop, calls=%fused_computation.9 | loop fusion | flops 196608 | bytes 524288 | tf_op jit(solution)/shard_map/convert_element_type | solution.py:379
  15.5 1.7 %collective-permute-start.1 = (bf16[32,2048]{1,0:T(8,128)(2,1)S(1)}, bf16[32,2048]{1,0:T(8,128)(2,1)S(1)}, u32[]{:S(2)}, u32[]{:S(2)}) collective-permute-start(bf16[32,2048]{1,0:T(8,128)(2,1)S(1)} %add_convert_fusion), channel_id=1, source_target_pairs={{0,64},{1,65},{2,66},{3,67},{4,68},{5,69},{6,70},{7,71},{8,72},{9,... | collective-permute-start | bytes 393224 | tf_op jit(solution)/shard_map/ppermute | solution.py:385
  17.1 2.7 %collective-permute-start.3 = (bf16[32,2048]{1,0:T(8,128)(2,1)S(1)}, bf16[32,2048]{1,0:T(8,128)(2,1)S(1)}, u32[]{:S(2)}, u32[]{:S(2)}) collective-permute-start(bf16[32,2048]{1,0:T(8,128)(2,1)S(1)} %add_convert_fusion), channel_id=1, source_target_pairs={{0,1},{1,0},{2,3},{3,2},{4,5},{5,4},{6,7},{7,6},{8,9},{9,8},{10,11... | collective-permute-start | bytes 393224 | tf_op jit(solution)/shard_map/ppermute | solution.py:385
  19.9 0.4 collective-permute-start.4
  20.3 0.6 gather_fusion
  21.1 0.8 collective-permute-done.1
  22.0 4.5 %collective-permute-done.3 = bf16[32,2048]{1,0:T(8,128)(2,1)S(1)} collective-permute-done((bf16[32,2048]{1,0:T(8,128)(2,1)S(1)}, bf16[32,2048]{1,0:T(8,128)(2,1)S(1)}, u32[]{:S(2)}, u32[]{:S(2)}) %collective-permute-start.3) | collective-permute-done | bytes 131104 | tf_op jit(solution)/shard_map/ppermute | solution.py:385
  26.5 2.4 %collective-permute-done.4 = bf16[32,2048]{1,0:T(8,128)(2,1)S(1)} collective-permute-done((bf16[32,2048]{1,0:T(8,128)(2,1)S(1)}, bf16[32,2048]{1,0:T(8,128)(2,1)S(1)}, u32[]{:S(2)}, u32[]{:S(2)}) %collective-permute-start.4) | collective-permute-done | bytes 131104 | tf_op jit(solution)/shard_map/ppermute | solution.py:385
  29.2 1.6 %collective-permute-start.5 = (bf16[64,2048]{1,0:T(8,128)(2,1)S(1)}, bf16[64,2048]{1,0:T(8,128)(2,1)S(1)}, u32[]{:S(2)}, u32[]{:S(2)}) collective-permute-start(bf16[64,2048]{1,0:T(8,128)(2,1)S(1)} %pad_maximum_fusion), channel_id=1, source_target_pairs={{0,8},{1,9},{2,10},{3,11},{4,12},{5,13},{6,14},{7,15},{8,16},{9,17... | collective-permute-start | bytes 786440 | tf_op jit(solution)/shard_map/ppermute | solution.py:396
  30.8 1.7 %collective-permute-start.6 = (bf16[64,2048]{1,0:T(8,128)(2,1)S(1)}, bf16[64,2048]{1,0:T(8,128)(2,1)S(1)}, u32[]{:S(2)}, u32[]{:S(2)}) collective-permute-start(bf16[64,2048]{1,0:T(8,128)(2,1)S(1)} %pad_maximum_fusion), channel_id=1, source_target_pairs={{0,24},{1,25},{2,26},{3,27},{4,28},{5,29},{6,30},{7,31},{8,0},{9,1... | collective-permute-start | bytes 786440 | tf_op jit(solution)/shard_map/ppermute | solution.py:396
  32.5 2.1 %collective-permute-start.7 = (bf16[64,2048]{1,0:T(8,128)(2,1)S(1)}, bf16[64,2048]{1,0:T(8,128)(2,1)S(1)}, u32[]{:S(2)}, u32[]{:S(2)}) collective-permute-start(bf16[64,2048]{1,0:T(8,128)(2,1)S(1)} %pad_maximum_fusion), channel_id=1, source_target_pairs={{0,16},{1,17},{2,18},{3,19},{4,20},{5,21},{6,22},{7,23},{8,24},{9,... | collective-permute-start | bytes 786440 | tf_op jit(solution)/shard_map/ppermute | solution.py:396
  34.6 2.2 %copy-done.1 = bf16[2048,1024]{1,0:T(8,128)(2,1)S(1)} copy-done((bf16[2048,1024]{1,0:T(8,128)(2,1)S(1)}, bf16[2048,1024]{1,0:T(8,128)(2,1)}, u32[]{:S(2)}) %copy-start.1) | copy-done | bytes 4194328
  36.8 2.5 %bring_in.1.refs_2_.refs_4_ = bf16[2,2048,1024]{2,1,0:T(8,128)(2,1)S(1)} custom-call(bf16[2048,1024]{1,0:T(8,128)(2,1)S(1)} %copy-done.1, bf16[2048,1024]{1,0:T(8,128)(2,1)} %collective-permute-done.2.other), custom_call_target="tpu_custom_call" | custom-call | bytes 8388608 | tf_op jit(solution)/shard_map/bring_in/pallas_call | solution.py:289
  39.3 2.0 %collective-permute-start.8 = (bf16[128,2048]{1,0:T(8,128)(2,1)S(1)}, bf16[128,2048]{1,0:T(8,128)(2,1)S(1)}, u32[]{:S(2)}, u32[]{:S(2)}) collective-permute-start(bf16[128,2048]{1,0:T(8,128)(2,1)S(1)} %constant_dynamic-update-slice_fusion.refs_0_), channel_id=1, source_target_pairs={{0,2},{1,3},{2,4},{3,5},{4,6},{5,7},{6,0},{7,1},{8,10},{9,11},{10,... | collective-permute-start | bytes 1572872 | tf_op jit(solution)/shard_map/ppermute | solution.py:400
  41.4 3.8 %collective-permute-start.11 = (bf16[128,2048]{1,0:T(8,128)(2,1)S(1)}, bf16[128,2048]{1,0:T(8,128)(2,1)S(1)}, u32[]{:S(2)}, u32[]{:S(2)}) collective-permute-start(bf16[128,2048]{1,0:T(8,128)(2,1)S(1)} %constant_dynamic-update-slice_fusion.2.refs_1_), channel_id=1, source_target_pairs={{0,6},{1,7},{2,0},{3,1},{4,2},{5,3},{6,4},{7,5},{8,14},{9,15},{10,... | collective-permute-start | bytes 1572872 | tf_op jit(solution)/shard_map/ppermute | solution.py:400
  45.1 0.4 collective-permute-start.10
  45.6 1.6 %collective-permute-start.9 = (bf16[128,2048]{1,0:T(8,128)(2,1)S(1)}, bf16[128,2048]{1,0:T(8,128)(2,1)S(1)}, u32[]{:S(2)}, u32[]{:S(2)}) collective-permute-start(bf16[128,2048]{1,0:T(8,128)(2,1)S(1)} %constant_dynamic-update-slice_fusion.2.refs_1_), channel_id=1, source_target_pairs={{0,2},{1,3},{2,4},{3,5},{4,6},{5,7},{6,0},{7,1},{8,10},{9,11},{10,... | collective-permute-start | bytes 1572872 | tf_op jit(solution)/shard_map/ppermute | solution.py:401
  47.2 3.4 %collective-permute-done.8.refs_0_ = bf16[128,2048]{1,0:T(8,128)(2,1)S(1)} collective-permute-done((bf16[128,2048]{1,0:T(8,128)(2,1)S(1)}, bf16[128,2048]{1,0:T(8,128)(2,1)S(1)}, u32[]{:S(2)}, u32[]{:S(2)}) %collective-permute-start.8) | collective-permute-done | bytes 524320 | tf_op jit(solution)/shard_map/ppermute | solution.py:400
  50.6 1.3 %collective-permute-done.11.refs_3_ = bf16[128,2048]{1,0:T(8,128)(2,1)S(1)} collective-permute-done((bf16[128,2048]{1,0:T(8,128)(2,1)S(1)}, bf16[128,2048]{1,0:T(8,128)(2,1)S(1)}, u32[]{:S(2)}, u32[]{:S(2)}) %collective-permute-start.11) | collective-permute-done | bytes 524320 | tf_op jit(solution)/shard_map/ppermute | solution.py:400
  51.8 3.7 %collective-permute-start.13 = (bf16[128,2048]{1,0:T(8,128)(2,1)S(1)}, bf16[128,2048]{1,0:T(8,128)(2,1)S(1)}, u32[]{:S(2)}, u32[]{:S(2)}) collective-permute-start(bf16[128,2048]{1,0:T(8,128)(2,1)S(1)} %collective-permute-done.11.refs_3_), channel_id=1, source_target_pairs={{0,6},{1,7},{2,0},{3,1},{4,2},{5,3},{6,4},{7,5},{8,14},{9,15},{10,... | collective-permute-start | bytes 1572872 | tf_op jit(solution)/shard_map/ppermute | solution.py:402
  55.5 3.2 %score.3 = f32[8,256]{1,0:T(8,128)S(1)} custom-call(s32[2]{0:T(128)S(1)} %pad_add_fusion.1.bases, bf16[128,2048]{1,0:T(8,128)(2,1)S(1)} %constant_dynamic-update-slice_fusion.refs_0_, bf16[128,2048]{1,0:T(8,128)(2,1)S(1)} %constant_dynamic-update-slice_fusion.2.refs_1_, bf16[2,2048,1024]{2,1,0:T(8,128)(2,1)S(1)} %bring_in.1.refs_2_.refs_4_, ...), custom_call_target="tpu_custom_call" | custom-call | flops 2147483648 | bytes 9437184 | tf_op jit(solution)/shard_map/score/pallas_call | solution.py:308
  58.7 5.5 %score.4 = f32[8,512]{1,0:T(8,128)S(1)} custom-call(s32[2]{0:T(128)S(1)} %pad_add_fusion.1.bases, bf16[128,2048]{1,0:T(8,128)(2,1)S(1)} %collective-permute-done.8.refs_0_, bf16[128,2048]{1,0:T(8,128)(2,1)S(1)} %collective-permute-done.9.refs_1_, bf16[128,2048]{1,0:T(8,128)(2,1)S(1)} %collective-permute-done.10.refs_2_, ...), custom_call_target="tpu_custom_call" | custom-call | flops 4294967296 | bytes 10485760 | tf_op jit(solution)/shard_map/score/pallas_call | solution.py:308
  64.2 3.2 %score.5 = f32[8,256]{1,0:T(8,128)S(1)} custom-call(s32[2]{0:T(128)S(1)} %pad_add_fusion.1.bases, bf16[128,2048]{1,0:T(8,128)(2,1)S(1)} %collective-permute-done.12.refs_0_, bf16[128,2048]{1,0:T(8,128)(2,1)S(1)} %collective-permute-done.13.refs_1_, bf16[2,2048,1024]{2,1,0:T(8,128)(2,1)S(1)} %bring_in.1.refs_2_.refs_4_, s32[1,1024]{1,0:T(1,128)S(1)} %reshape.63.refs_3_.refs_5_), custom_call_target="tpu_custom_call" | custom-call | flops 2147483648 | bytes 9437184 | tf_op jit(solution)/shard_map/score/pallas_call | solution.py:308
  67.6 0.6 gather_fusion.1
  68.3 0.6 broadcast_in_dim.52
  68.9 6.4 %all-to-all-start = ((f32[128,1,64]{2,1,0:T(1,128)}), f32[128,1,64]{2,1,0:T(1,128)S(1)}, u32[]{:S(2)}, u32[]{:S(2)}) async-start(f32[128,1,64]{2,1,0:T(1,128)} %bitcast.17), calls=%async_computation | async-start | bytes 131072 | tf_op jit(solution)/shard_map/all_to_all | solution.py:413
  75.3 9.5 %all-to-all-done = f32[128,1,64]{2,1,0:T(1,128)S(1)} async-done(((f32[128,1,64]{2,1,0:T(1,128)}), f32[128,1,64]{2,1,0:T(1,128)S(1)}, u32[]{:S(2)}, u32[]{:S(2)}) %all-to-all-start) | async-done | bytes 32800 | tf_op jit(solution)/shard_map/all_to_all | solution.py:413
  85.2 1.3 %select_bitcast_fusion = f32[16,4]{0,1:T(4,128)} fusion(f32[4,16]{1,0:T(4,128)S(1)} %bitcast.35, s32[512,4]{0,1:T(4,128)} %param.35, s32[]{:T(128)S(6)} %select_n.40), kind=kLoop, calls=%fused_computation.24 | loop fusion | flops 128 | bytes 772 | tf_op jit(solution)/shard_map/transpose | solution.py:417
  (54 shorter events, 2.1 us)
Async XLA Ops:
  0.0 13.3 %copy-start = (s32[512,4]{0,1:T(4,128)S(1)}, s32[512,4]{0,1:T(4,128)}, u32[]{:S(2)}) copy-start(s32[512,4]{0,1:T(4,128)} %param.34) | copy-start | bytes 24580
  0.0 29.2 %collective-permute-start.2 = (bf16[2048,1024]{1,0:T(8,128)(2,1)}, bf16[2048,1024]{1,0:T(8,128)(2,1)}, u32[]{:S(2)}, u32[]{:S(2)}) collective-permute-start(bf16[2048,1024]{1,0:T(8,128)(2,1)} %own.1), channel_id=1, source_target_pairs={{0,32},{1,33},{2,34},{3,35},{4,36},{5,37},{6,38},{7,39},{8,40},{9,... | collective-permute-start | bytes 12582920 | tf_op jit(solution)/shard_map/ppermute | solution.py:353
  0.7 28.4 %copy-start.3 = (f32[2048]{0:T(1024)S(1)}, f32[2048]{0:T(1024)}, u32[]{:S(2)}) copy-start(f32[2048]{0:T(1024)} %param.32) | copy-start | bytes 24580
  12.8 1.7 %collective-permute-start = (bf16[32,2048]{1,0:T(8,128)(2,1)}, bf16[32,2048]{1,0:T(8,128)(2,1)S(1)}, u32[]{:S(2)}, u32[]{:S(2)}) collective-permute-start(bf16[32,2048]{1,0:T(8,128)(2,1)} %get-tuple-element.23), channel_id=1, source_target_pairs={{0,32},{1,33},{2,34},{3,35},{4,36},{5,37},{6,38},{7,39},{8,40},{9,... | collective-permute-start | bytes 393224 | tf_op jit(solution)/shard_map/ppermute | solution.py:379
  15.5 6.4 %collective-permute-start.1 = (bf16[32,2048]{1,0:T(8,128)(2,1)S(1)}, bf16[32,2048]{1,0:T(8,128)(2,1)S(1)}, u32[]{:S(2)}, u32[]{:S(2)}) collective-permute-start(bf16[32,2048]{1,0:T(8,128)(2,1)S(1)} %add_convert_fusion), channel_id=1, source_target_pairs={{0,64},{1,65},{2,66},{3,67},{4,68},{5,69},{6,70},{7,71},{8,72},{9,... | collective-permute-start | bytes 393224 | tf_op jit(solution)/shard_map/ppermute | solution.py:385
  17.1 9.4 %collective-permute-start.3 = (bf16[32,2048]{1,0:T(8,128)(2,1)S(1)}, bf16[32,2048]{1,0:T(8,128)(2,1)S(1)}, u32[]{:S(2)}, u32[]{:S(2)}) collective-permute-start(bf16[32,2048]{1,0:T(8,128)(2,1)S(1)} %add_convert_fusion), channel_id=1, source_target_pairs={{0,1},{1,0},{2,3},{3,2},{4,5},{5,4},{6,7},{7,6},{8,9},{9,8},{10,11... | collective-permute-start | bytes 393224 | tf_op jit(solution)/shard_map/ppermute | solution.py:385
  19.9 9.0 %collective-permute-start.4 = (bf16[32,2048]{1,0:T(8,128)(2,1)S(1)}, bf16[32,2048]{1,0:T(8,128)(2,1)S(1)}, u32[]{:S(2)}, u32[]{:S(2)}) collective-permute-start(bf16[32,2048]{1,0:T(8,128)(2,1)S(1)} %add_convert_fusion), channel_id=1, source_target_pairs={{0,65},{1,64},{2,67},{3,66},{4,69},{5,68},{6,71},{7,70},{8,73},{9,... | collective-permute-start | bytes 393224 | tf_op jit(solution)/shard_map/ppermute | solution.py:385
  29.2 10.1 %collective-permute-start.5 = (bf16[64,2048]{1,0:T(8,128)(2,1)S(1)}, bf16[64,2048]{1,0:T(8,128)(2,1)S(1)}, u32[]{:S(2)}, u32[]{:S(2)}) collective-permute-start(bf16[64,2048]{1,0:T(8,128)(2,1)S(1)} %pad_maximum_fusion), channel_id=1, source_target_pairs={{0,8},{1,9},{2,10},{3,11},{4,12},{5,13},{6,14},{7,15},{8,16},{9,17... | collective-permute-start | bytes 786440 | tf_op jit(solution)/shard_map/ppermute | solution.py:396
  30.8 10.4 %collective-permute-start.6 = (bf16[64,2048]{1,0:T(8,128)(2,1)S(1)}, bf16[64,2048]{1,0:T(8,128)(2,1)S(1)}, u32[]{:S(2)}, u32[]{:S(2)}) collective-permute-start(bf16[64,2048]{1,0:T(8,128)(2,1)S(1)} %pad_maximum_fusion), channel_id=1, source_target_pairs={{0,24},{1,25},{2,26},{3,27},{4,28},{5,29},{6,30},{7,31},{8,0},{9,1... | collective-permute-start | bytes 786440 | tf_op jit(solution)/shard_map/ppermute | solution.py:396
  32.5 8.8 %collective-permute-start.7 = (bf16[64,2048]{1,0:T(8,128)(2,1)S(1)}, bf16[64,2048]{1,0:T(8,128)(2,1)S(1)}, u32[]{:S(2)}, u32[]{:S(2)}) collective-permute-start(bf16[64,2048]{1,0:T(8,128)(2,1)S(1)} %pad_maximum_fusion), channel_id=1, source_target_pairs={{0,16},{1,17},{2,18},{3,19},{4,20},{5,21},{6,22},{7,23},{8,24},{9,... | collective-permute-start | bytes 786440 | tf_op jit(solution)/shard_map/ppermute | solution.py:396
  34.6 2.2 %copy-start.1 = (bf16[2048,1024]{1,0:T(8,128)(2,1)S(1)}, bf16[2048,1024]{1,0:T(8,128)(2,1)}, u32[]{:S(2)}) copy-start(bf16[2048,1024]{1,0:T(8,128)(2,1)} %own.1) | copy-start | bytes 12582916
  39.3 11.3 %collective-permute-start.8 = (bf16[128,2048]{1,0:T(8,128)(2,1)S(1)}, bf16[128,2048]{1,0:T(8,128)(2,1)S(1)}, u32[]{:S(2)}, u32[]{:S(2)}) collective-permute-start(bf16[128,2048]{1,0:T(8,128)(2,1)S(1)} %constant_dynamic-update-slice_fusion.refs_0_), channel_id=1, source_target_pairs={{0,2},{1,3},{2,4},{3,5},{4,6},{5,7},{6,0},{7,1},{8,10},{9,11},{10,... | collective-permute-start | bytes 1572872 | tf_op jit(solution)/shard_map/ppermute | solution.py:400
  41.4 10.5 %collective-permute-start.11 = (bf16[128,2048]{1,0:T(8,128)(2,1)S(1)}, bf16[128,2048]{1,0:T(8,128)(2,1)S(1)}, u32[]{:S(2)}, u32[]{:S(2)}) collective-permute-start(bf16[128,2048]{1,0:T(8,128)(2,1)S(1)} %constant_dynamic-update-slice_fusion.2.refs_1_), channel_id=1, source_target_pairs={{0,6},{1,7},{2,0},{3,1},{4,2},{5,3},{6,4},{7,5},{8,14},{9,15},{10,... | collective-permute-start | bytes 1572872 | tf_op jit(solution)/shard_map/ppermute | solution.py:400
  45.1 13.5 %collective-permute-start.10 = (bf16[128,2048]{1,0:T(8,128)(2,1)S(1)}, bf16[128,2048]{1,0:T(8,128)(2,1)S(1)}, u32[]{:S(2)}, u32[]{:S(2)}) collective-permute-start(bf16[128,2048]{1,0:T(8,128)(2,1)S(1)} %constant_dynamic-update-slice_fusion.refs_0_), channel_id=1, source_target_pairs={{0,6},{1,7},{2,0},{3,1},{4,2},{5,3},{6,4},{7,5},{8,14},{9,15},{10,... | collective-permute-start | bytes 1572872 | tf_op jit(solution)/shard_map/ppermute | solution.py:401
  45.6 13.1 %collective-permute-start.9 = (bf16[128,2048]{1,0:T(8,128)(2,1)S(1)}, bf16[128,2048]{1,0:T(8,128)(2,1)S(1)}, u32[]{:S(2)}, u32[]{:S(2)}) collective-permute-start(bf16[128,2048]{1,0:T(8,128)(2,1)S(1)} %constant_dynamic-update-slice_fusion.2.refs_1_), channel_id=1, source_target_pairs={{0,2},{1,3},{2,4},{3,5},{4,6},{5,7},{6,0},{7,1},{8,10},{9,11},{10,... | collective-permute-start | bytes 1572872 | tf_op jit(solution)/shard_map/ppermute | solution.py:401
  50.6 13.6 %collective-permute-start.12 = (bf16[128,2048]{1,0:T(8,128)(2,1)S(1)}, bf16[128,2048]{1,0:T(8,128)(2,1)S(1)}, u32[]{:S(2)}, u32[]{:S(2)}) collective-permute-start(bf16[128,2048]{1,0:T(8,128)(2,1)S(1)} %collective-permute-done.8.refs_0_), channel_id=1, source_target_pairs={{0,2},{1,3},{2,4},{3,5},{4,6},{5,7},{6,0},{7,1},{8,10},{9,11},{10,... | collective-permute-start | bytes 1572872 | tf_op jit(solution)/shard_map/ppermute | solution.py:402
  51.8 12.4 %collective-permute-start.13 = (bf16[128,2048]{1,0:T(8,128)(2,1)S(1)}, bf16[128,2048]{1,0:T(8,128)(2,1)S(1)}, u32[]{:S(2)}, u32[]{:S(2)}) collective-permute-start(bf16[128,2048]{1,0:T(8,128)(2,1)S(1)} %collective-permute-done.11.refs_3_), channel_id=1, source_target_pairs={{0,6},{1,7},{2,0},{3,1},{4,2},{5,3},{6,4},{7,5},{8,14},{9,15},{10,... | collective-permute-start | bytes 1572872 | tf_op jit(solution)/shard_map/ppermute | solution.py:402
  58.7 5.5 %copy-start.2 = (f32[8,256]{1,0:T(8,128)}, f32[8,256]{1,0:T(8,128)S(1)}, u32[]{:S(2)}) copy-start(f32[8,256]{1,0:T(8,128)S(1)} %score.3) | copy-start | bytes 24580
  64.2 3.2 %slice-start = ((f32[8,256]{1,0:T(8,128)}), f32[2,256]{1,0:T(2,128)S(1)}, s32[]{:S(2)}) async-start(f32[8,256]{1,0:T(8,128)} %copy-done.2), calls=%async_computation.1 | async-start | bytes 4096 | tf_op jit(solution)/shard_map/slice | solution.py:409
  68.9 15.8 %all-to-all-start = ((f32[128,1,64]{2,1,0:T(1,128)}), f32[128,1,64]{2,1,0:T(1,128)S(1)}, u32[]{:S(2)}, u32[]{:S(2)}) async-start(f32[128,1,64]{2,1,0:T(1,128)} %bitcast.17), calls=%async_computation | async-start | bytes 131072 | tf_op jit(solution)/shard_map/all_to_all | solution.py:413

commit v7 on v6

--- a/solution.py
+++ b/solution.py
@@ -55,11 +55,16 @@
             for source, target in pairs:
                 grown[target].extend(held[source])
         held = grown
-    return np.array(held, np.int32)
+    landing = [*range(12), *range(20, 24), *range(12, 20), *range(24, 32)]
+    return np.array(held, np.int32)[:, landing]
+
+
+def position():
+    xl, c, y, z, xh = [lax.axis_index(axis).astype(jnp.int32) for axis in AXES]
+    return xl, c, xl * 2 + c, (y * 4 + z) * 2 + xh
 
 
 def front_kernel(
-    spot,
     rate,
     offset,
     embedded,
@@ -88,6 +93,7 @@
     step = pl.program_id(0)
     steps, group, width = embedded.shape
     rows = steps * group
+    low_x, core, head_group, batch_group = position()
 
     def contract_last(a, b):
         return lax.dot_general(a, b, (((1,), (1,)), ((), ())), preferred_element_type=F32)
@@ -104,12 +110,12 @@
         for h in range(w_beta.shape[0]):
             b = jnp.broadcast_to(beta_raw[:, h : h + 1], (rows, DV))
             d = jnp.broadcast_to(decay_raw[:, h : h + 1], (rows, DV))
-            at = spot[1] * w_beta.shape[0] + h
+            at = head_group * w_beta.shape[0] + h
             beta_all[h] = jax.nn.sigmoid(b)
             decay_all[h] = jnp.exp(-rate[at] * jax.nn.softplus(d + offset[at]))
         requests = active.shape[1]
         here = lax.broadcasted_iota(jnp.int32, (group, requests), 1) == (
-            spot[0] * group + lax.broadcasted_iota(jnp.int32, (group, requests), 0)
+            batch_group * group + lax.broadcasted_iota(jnp.int32, (group, requests), 0)
         )
         for t in range(steps):
             line = jnp.broadcast_to(active[t : t + 1, :].astype(F32), (group, requests))
@@ -184,14 +190,14 @@
     @pl.when(step == pl.num_programs(0) - 1)
     def _():
         half = rows // 2
-        c = spot[2]
+        c = core
         tokens = embedded[pl.ds(c * (steps // 2), steps // 2)].astype(F32).reshape(half, width)
-        first = jnp.where(spot[3] == 0, 1.0, 0.0)
+        first = jnp.where(low_x == 0, 1.0, 0.0)
         keep[...] = total[pl.ds(pl.multiple_of(c * half, half), half), :] + tokens * first
         give[...] = total[pl.ds(pl.multiple_of((1 - c) * half, half), half), :].astype(BF16)
 
 
-def front(spot, rate, offset, embedded, states, wq, wk, wv, wg, wb, wd, wo, ig, hg, active):
+def front(rate, offset, embedded, states, wq, wk, wv, wg, wb, wd, wo, ig, hg, active):
     steps, group, width = embedded.shape
     rows, heads = steps * group, states.shape[1]
     key_heads = heads // 2
@@ -200,7 +206,7 @@
     return pl.pallas_call(
         front_kernel,
         grid_spec=pltpu.PrefetchScalarGridSpec(
-            num_scalar_prefetch=3,
+            num_scalar_prefetch=2,
             grid=(key_heads,),
             in_specs=[
                 whole(steps, group, width),
@@ -239,39 +245,106 @@
             flops=2 * rows * width * 4096, bytes_accessed=21 << 20, transcendentals=0
         ),
         name="front",
-    )(spot, rate, offset, embedded, states, wq, wk, wv, wg, wb, wd, wo, ig, hg, active)
+    )(rate, offset, embedded, states, wq, wk, wv, wg, wb, wd, wo, ig, hg, active)
 
 
 TILE = 512
 
 
-def score_kernel(count, offset, bases, *refs):
-    parts, (vocabulary, target, stats) = refs[:count], refs[count:]
-    cols = vocabulary.shape[2]
-    pieces = [
-        jnp.concatenate([parts[i][...], parts[i + 1][...]], axis=0) for i in range(0, count, 2)
-    ]
-    size = pieces[0].shape[0]
-    for p, piece in enumerate(pieces):
-        at = slice(p * size, (p + 1) * size)
-        lane = lax.broadcasted_iota(jnp.int32, (size, 128), 1)
-        want = target[:, offset + p * size : offset + (p + 1) * size]
-        want = jnp.broadcast_to(want, (128, size)).T - lane
-        running = jnp.zeros((size, 128), F32)
-        found = jnp.zeros((size, 128), F32)
-        for start in range(0, cols, TILE):
-            for which in range(2):
-                logits = jnp.dot(
-                    piece, vocabulary[which, :, start : start + TILE], preferred_element_type=F32
-                )
-                left = want - (bases[which] + start)
-                for s in range(0, TILE, 128):
-                    part = logits[:, s : s + 128]
-                    running = running + jnp.exp(part)
-                    found = found + jnp.where(left == s, part, 0.0)
-        sums = jnp.sum(running, axis=1, keepdims=True)
-        hits = jnp.sum(found, axis=1, keepdims=True)
-        stats[:, at] = jnp.where(lane == 0, sums, hits).T[:8, :]
+def score_block(parts, vocabulary, target, offset):
+    piece = jnp.concatenate([part[...] for part in parts], axis=0)
+    size, cols = piece.shape[0], vocabulary.shape[2]
+    _, core, head_group, batch_group = position()
+    base = (head_group * GROUPS + batch_group) * cols
+    bases = (base, base + (1 - 2 * core) * GROUPS * cols)
+    lane = lax.broadcasted_iota(jnp.int32, (size, 128), 1)
+    want = jnp.broadcast_to(target[:, offset : offset + size], (128, size)).T - lane
+    running = jnp.zeros((size, 128), F32)
+    found = jnp.zeros((size, 128), F32)
+    for start in range(0, cols, TILE):
+        for which in range(2):
+            logits = jnp.dot(
+                piece, vocabulary[which, :, start : start + TILE], preferred_element_type=F32
+            )
+            left = want - (bases[which] + start)
+            for s in range(0, TILE, 128):
+                part = logits[:, s : s + 128]
+                running = running + jnp.exp(part)
+                found = found + jnp.where(left == s, part, 0.0)
+    sums = jnp.sum(running, axis=1, keepdims=True)
+    hits = jnp.sum(found, axis=1, keepdims=True)
+    return jnp.where(lane == 0, sums, hits).T[:8, :]
+
+
+def score_kernel(offset, one, two, vocabulary, target, stats):
+    stats[...] = score_block((one, two), vocabulary, target, offset)
+
+
+def last_score_kernel(offset, order, one, two, vocabulary, target, *refs):
+    earlier, outgoing = refs[:-1], refs[-1]
+    blocks = [part[...] for part in earlier] + [score_block((one, two), vocabulary, target, offset)]
+    half = outgoing.shape[1] // 2
+    at = 0
+    for block in blocks:
+        for s in range(0, block.shape[1], half):
+            row = jnp.concatenate([block[0:1, s : s + half], block[1:2, s : s + half]], axis=1)
+            for head in range(4):
+                outgoing[pl.ds(order[at] + head * GROUPS, 1), :] = row
+            at += 1
+
+
+def score(parts, vocabulary, target, offset, earlier=(), order=None):
+    size, width = parts[0].shape
+    rows, cols = 2 * size, vocabulary.shape[2]
+    near = pl.BlockSpec(memory_space=pltpu.VMEM)
+    last = order is not None
+    kernel = last_score_kernel if last else score_kernel
+    shape = (DEVICES, 2 * rows * 4 // GROUPS) if last else (8, rows)
+    return pl.pallas_call(
+        functools.partial(kernel, offset),
+        grid_spec=pltpu.PrefetchScalarGridSpec(
+            num_scalar_prefetch=int(last),
+            grid=(),
+            in_specs=[near] * (4 + len(earlier)),
+            out_specs=near,
+        ),
+        out_shape=jax.ShapeDtypeStruct(shape, F32),
+        compiler_params=pltpu.CompilerParams(vmem_limit_bytes=20 << 20),
+        cost_estimate=pl.CostEstimate(
+            flops=4 * rows * width * cols,
+            bytes_accessed=2 * width * (2 * cols + rows),
+            transcendentals=2 * rows * cols,
+        ),
+        name="last_score" if last else "score",
+    )(*([order] if last else []), *parts, vocabulary, target, *earlier)
+
+
+def finish_kernel(incoming, marks, scores):
+    block = GROUPS
+    for core in range(2):
+        total = sum(
+            jnp.sum(incoming[(x * 2 + core) * block : (x * 2 + core + 1) * block, :], axis=0, keepdims=True)
+            for x in range(2)
+        )
+        half = total.shape[1] // 2
+        group = half // 2
+        result = total[:, half:] - jnp.log(total[:, :half])
+        for t in range(2):
+            row = slice(core * 2 + t, core * 2 + t + 1)
+            part = result[:, t * group : (t + 1) * group]
+            scores[row, :] = jnp.where(marks[row, :] > 0, part, 0.0)
+
+
+def finish_scores(incoming, marks):
+    near = pl.BlockSpec(memory_space=pltpu.VMEM)
+    return pl.pallas_call(
+        finish_kernel,
+        in_specs=[near, near],
+        out_specs=near,
+        out_shape=jax.ShapeDtypeStruct(marks.shape, F32),
+        compiler_params=pltpu.CompilerParams(vmem_limit_bytes=4 << 20),
+        name="finish",
+    )(incoming, marks)
 
 
 def gather_kernel(own, other, both, sems):
@@ -298,30 +371,6 @@
         ),
         name="bring_in",
     )(own, other)
-
-
-def score(bases, pieces, vocabulary, target, offset):
-    size, width = pieces[0].shape
-    count, cols = len(pieces), vocabulary.shape[2]
-    rows = size * count
-    near = pl.BlockSpec(memory_space=pltpu.VMEM)
-    return pl.pallas_call(
-        functools.partial(score_kernel, count, offset),
-        grid_spec=pltpu.PrefetchScalarGridSpec(
-            num_scalar_prefetch=1,
-            grid=(),
-            in_specs=[near] * (count + 2),
-            out_specs=near,
-        ),
-        out_shape=jax.ShapeDtypeStruct((8, rows), F32),
-        compiler_params=pltpu.CompilerParams(vmem_limit_bytes=20 << 20),
-        cost_estimate=pl.CostEstimate(
-            flops=4 * rows * width * cols,
-            bytes_accessed=2 * width * (2 * cols + rows),
-            transcendentals=2 * rows * cols,
-        ),
-        name="score",
-    )(bases, *pieces, vocabulary, target)
 
 
 def per_device(
@@ -344,17 +393,13 @@
     active,
 ):
     steps, group, width = embedded.shape
-    cols = lm_head.shape[1]
     me = lax.axis_index(AXES).astype(jnp.int32)
     core = lax.axis_index("c").astype(jnp.int32)
     batch = lax.axis_index(BATCH).astype(jnp.int32)
-    head = lax.axis_index(HEAD).astype(jnp.int32)
     send = functools.partial(lax.ppermute, axis_name=AXES)
     far_head = send(lm_head, perm=OTHER_CORE)
 
-    spot = jnp.stack([batch, head, core, lax.axis_index("xl").astype(jnp.int32)])
     give, keep = front(
-        spot,
         decay_rate,
         decay_bias,
         embedded,
@@ -371,19 +416,15 @@
         active.T,
     )
     block = keep.shape[0]
-    table = sources()
-    order = lax.dynamic_index_in_dim(jnp.asarray(table), me, 0, keepdims=False)
-    inverse = lax.dynamic_index_in_dim(
-        jnp.asarray(np.argsort(table, axis=1).astype(np.int32)), me, 0, keepdims=False
-    )
     pair = (keep + send(give, perm=OTHER_CORE).astype(F32)).astype(BF16)
-    bases = jnp.stack([me * cols, (me ^ GROUPS) * cols])
-    pair, order, inverse, bases = lax.optimization_barrier((pair, order, inverse, bases))
+    pair, me, core, batch = lax.optimization_barrier((pair, me, core, batch))
+    order = lax.dynamic_index_in_dim(jnp.asarray(sources()), me, 0, keepdims=False)
     wanted = lax.dynamic_slice_in_dim(targets.T, core * (steps // 2), steps // 2, 0)
     wanted = jnp.take(wanted.reshape(steps // 2, GROUPS, group), order, axis=1)
     wanted = wanted.transpose(1, 0, 2).reshape(1, GROUPS * block)
+    marks = lax.dynamic_slice_in_dim(active.T, batch * group, group, 1)
     low, corner, high = [send(pair, perm=p) for p in (OTHER_LOW, OTHER_BOTH, OTHER_HIGH)]
-    low, wanted, inverse = lax.optimization_barrier((low, wanted, inverse))
+    low, wanted, order, marks = lax.optimization_barrier((low, wanted, order, marks))
 
     def finish(a, b):
         y = a.astype(F32) + b.astype(F32)
@@ -400,21 +441,14 @@
     forth_one, back_two = send(one, perm=FAR[0]), send(two, perm=FAR[1])
     forth_two, back_one = send(two, perm=FAR[0]), send(one, perm=FAR[1])
     halves = [send(forth_one, perm=FAR[0]), send(back_two, perm=FAR[1])]
-    first = score(bases, [one, two], vocabulary, wanted, 0)
-    wanted, first = lax.optimization_barrier((wanted, first))
-    middle = [forth_one, forth_two, back_one, back_two]
-    middle = score(bases, middle, vocabulary, wanted, 2 * size)
-    wanted, middle = lax.optimization_barrier((wanted, middle))
-    stats = [first, middle, score(bases, halves, vocabulary, wanted, 6 * size)]
-    stats = [part[:2] for part in stats]
-    stats = jnp.concatenate(stats, 1).reshape(2, GROUPS, block).transpose(1, 0, 2)
-    stats = jnp.take(stats.reshape(GROUPS, 2 * block), inverse, axis=0)
-    stats = jnp.broadcast_to(stats[None], (4, GROUPS, 2 * block)).reshape(DEVICES, 2 * block)
-    stats = lax.all_to_all(stats, AXES, 0, 0, tiled=True)
-    stats = jnp.sum(stats.reshape(2, 2, GROUPS, 2, steps // 2, group), axis=(0, 2))
-    total, picked = stats[:, 0].reshape(steps, group), stats[:, 1].reshape(steps, group)
-    marks = lax.dynamic_slice_in_dim(active.T, batch * group, group, 1)
-    return jnp.where(marks > 0, picked - jnp.log(total), 0.0).T
+    stats = []
+    arrivals = ((one, two), (forth_one, back_two), (forth_two, back_one))
+    for i, parts in enumerate(arrivals):
+        stats.append(score(parts, vocabulary, wanted, 2 * size * i))
+        wanted, stats[i] = lax.optimization_barrier((wanted, stats[i]))
+    outgoing = score(halves, vocabulary, wanted, 6 * size, stats, order)
+    incoming = lax.all_to_all(outgoing, AXES, 0, 0, tiled=True)
+    return finish_scores(incoming, marks).T
 
 
 def solution(mesh):

time: 87.4 us -> 84 us (0.961)
  blocking collectives: 0 us -> 16.6 us
  waiting for transfers between devices: 22 us -> 10.5 us
  starting transfers between devices: 28.5 us -> 22.2 us
  local copies, waits for them, and re-layouts: 5.55 us -> 4.55 us
  other arithmetic: 3.87 us -> 2.95 us
    all_to_all x0 -> x1, blocking collectives: none -> 16.6 us  [per_device(): incoming = lax.all_to_all(outgoing, AXES, 0, 0, tiled=True)]
    all_to_all x1 -> x0, waiting for transfers between devices: 9.47 us -> none  [per_device(): stats = lax.all_to_all(stats, AXES, 0, 0, tiled=True)]
    all_to_all x1 -> x0, starting transfers between devices: 6.36 us -> none  [per_device(): stats = lax.all_to_all(stats, AXES, 0, 0, tiled=True)]
    ppermute x3, waiting for transfers between devices: 7.59 us -> 4.62 us  [per_device(): send(pair, perm=p)]
    transpose x1 -> x0, other arithmetic: 1.33 us -> none  [per_device(): return jnp.where(marks > 0, picked - jnp.log(total), 0.0).T]
    ppermute x1, waiting for transfers between devices: 0.28 us -> 1.2 us  [per_device(): pair = (keep + send(give, perm=OTHER_CORE).astype(F32)).astype(BF16)]
    pallas_call x3 -> x5, Pallas kernels: 11.8 us -> 11.7 us  [the longest x4 10.9 us: score(): pl.pallas_call(functools.partial(kernel, offset), grid_spec=pltpu.Prefetc...]
    unnamed x10 -> x8, local copies, waits for them, and re-layouts: 2.23 us -> 2.23 us
  transfers between devices with their start and end apart: 15 -> 14, of which waited for: 7 -> 5; matrix products, arithmetic and copies ran while one was open for 5% -> 6% of each run, Pallas kernels for 27% -> 27%
where the time goes in v7:
time: 84 us; the launch traced here: 83.1 us
  Pallas kernels  26.2 us (31%)
  starting transfers between devices  22.2 us (26%)
  blocking collectives  16.6 us (20%)
  waiting for transfers between devices  10.5 us (12%)
  local copies, waits for them, and re-layouts  4.55 us (5%)
  other arithmetic  2.95 us (4%)
    all_to_all x1, blocking collectives, per_device(): incoming = lax.all_to_all(outgoing, AXES, 0, 0, tiled=True)  16.6 us
    pallas_call x1, Pallas kernels, front(): pl.pallas_call(front_kernel, grid_spec=pltpu.PrefetchScalarGridSpec(num_s...  12.1 us
    pallas_call x4, Pallas kernels, score(): pl.pallas_call(functools.partial(kernel, offset), grid_spec=pltpu.Prefetc...  10.9 us
    ppermute x2, starting transfers between devices, per_device(): forth_one, back_two = (send(one, perm=FAR[0]), send(two, perm=FAR[1]))  5.76 us
    ppermute x3, starting transfers between devices, per_device(): ahead, behind, across = [send(both, perm=p) for p in NEAR]  5.37 us
    ppermute x3, starting transfers between devices, per_device(): send(pair, perm=p)  4.79 us
    ppermute x2, waiting for transfers between devices, per_device(): forth_one, back_two = (send(one, perm=FAR[0]), send(two, perm=FAR[1]))  4.67 us
    ppermute x3, waiting for transfers between devices, per_device(): send(pair, perm=p)  4.62 us
  transfers between devices with their start and end apart: 14, of which 5 were waited for; matrix products, arithmetic and copies ran while one was open for 6% of the time, Pallas kernels for 27%

profile of v7, /device:TPU:0, one launch (start us, length us, event | category | flops | bytes accessed | tf_op | source)
XLA Modules:
  0.0 83.1 jit_solution(97955664992057630)
XLA Ops:
  0.0 12.1 %front.1 = (bf16[32,2048]{1,0:T(8,128)(2,1)}, f32[32,2048]{1,0:T(8,128)}) custom-call(f32[32]{0:T(128)} %rate.1, f32[32]{0:T(128)} %offset.1, bf16[4,16,2048]{2,1,0:T(8,128)(2,1)} %embedded.1, bf16[16,8,128,128]{3,2,1,0:T(8,128)(2,1)} %states.1, bf16[2048,512]{1,0:T(8,128)(2,1)} %w_query.1, bf16[2048,512]{1,0:T(8,128)(2,1)} %w_key.1, ...), custom_call_target="tpu_custom_call" | custom-call | flops 1073741824 | bytes 22020096 | tf_op jit(solution)/shard_map/front/pallas_call | solution.py:206
  12.1 0.5 collective-permute-start
  12.6 1.2 %collective-permute-done = bf16[32,2048]{1,0:T(8,128)(2,1)S(1)} collective-permute-done((bf16[32,2048]{1,0:T(8,128)(2,1)}, bf16[32,2048]{1,0:T(8,128)(2,1)S(1)}, u32[]{:S(2)}, u32[]{:S(2)}) %collective-permute-start) | collective-permute-done | bytes 131104 | tf_op jit(solution)/shard_map/ppermute | solution.py:419
  13.8 1.0 %add_convert_fusion = bf16[32,2048]{1,0:T(8,128)(2,1)S(1)} fusion(f32[32,2048]{1,0:T(8,128)} %get-tuple-element.25, bf16[32,2048]{1,0:T(8,128)(2,1)S(1)} %collective-permute-done), kind=kLoop, calls=%fused_computation.8 | loop fusion | flops 196608 | bytes 524288 | tf_op jit(solution)/shard_map/convert_element_type | solution.py:419
  14.8 1.7 %collective-permute-start.1 = (bf16[32,2048]{1,0:T(8,128)(2,1)S(1)}, bf16[32,2048]{1,0:T(8,128)(2,1)S(1)}, u32[]{:S(2)}, u32[]{:S(2)}) collective-permute-start(bf16[32,2048]{1,0:T(8,128)(2,1)S(1)} %add_convert_fusion), channel_id=1, source_target_pairs={{0,64},{1,65},{2,66},{3,67},{4,68},{5,69},{6,70},{7,71},{8,72},{9,... | collective-permute-start | bytes 393224 | tf_op jit(solution)/shard_map/ppermute | solution.py:426
  16.5 2.7 %collective-permute-start.3 = (bf16[32,2048]{1,0:T(8,128)(2,1)S(1)}, bf16[32,2048]{1,0:T(8,128)(2,1)S(1)}, u32[]{:S(2)}, u32[]{:S(2)}) collective-permute-start(bf16[32,2048]{1,0:T(8,128)(2,1)S(1)} %add_convert_fusion), channel_id=1, source_target_pairs={{0,1},{1,0},{2,3},{3,2},{4,5},{5,4},{6,7},{7,6},{8,9},{9,8},{10,11... | collective-permute-start | bytes 393224 | tf_op jit(solution)/shard_map/ppermute | solution.py:426
  19.2 0.4 collective-permute-start.4
  19.7 0.7 fusion
  20.4 0.6 gather_fusion
  21.0 0.7 compare_and_fusion
  21.9 0.8 dynamic-slice_bitcast_fusion.1.marks
  22.6 0.7 fusion.1.order
  23.6 2.3 %collective-permute-done.3 = bf16[32,2048]{1,0:T(8,128)(2,1)S(1)} collective-permute-done((bf16[32,2048]{1,0:T(8,128)(2,1)S(1)}, bf16[32,2048]{1,0:T(8,128)(2,1)S(1)}, u32[]{:S(2)}, u32[]{:S(2)}) %collective-permute-start.3) | collective-permute-done | bytes 131104 | tf_op jit(solution)/shard_map/ppermute | solution.py:426
  25.8 2.4 %collective-permute-done.4 = bf16[32,2048]{1,0:T(8,128)(2,1)S(1)} collective-permute-done((bf16[32,2048]{1,0:T(8,128)(2,1)S(1)}, bf16[32,2048]{1,0:T(8,128)(2,1)S(1)}, u32[]{:S(2)}, u32[]{:S(2)}) %collective-permute-start.4) | collective-permute-done | bytes 131104 | tf_op jit(solution)/shard_map/ppermute | solution.py:426
  28.5 1.6 %collective-permute-start.5 = (bf16[64,2048]{1,0:T(8,128)(2,1)S(1)}, bf16[64,2048]{1,0:T(8,128)(2,1)S(1)}, u32[]{:S(2)}, u32[]{:S(2)}) collective-permute-start(bf16[64,2048]{1,0:T(8,128)(2,1)S(1)} %pad_maximum_fusion), channel_id=1, source_target_pairs={{0,8},{1,9},{2,10},{3,11},{4,12},{5,13},{6,14},{7,15},{8,16},{9,17... | collective-permute-start | bytes 786440 | tf_op jit(solution)/shard_map/ppermute | solution.py:437
  30.2 1.7 %collective-permute-start.8 = (bf16[64,2048]{1,0:T(8,128)(2,1)S(1)}, bf16[64,2048]{1,0:T(8,128)(2,1)S(1)}, u32[]{:S(2)}, u32[]{:S(2)}) collective-permute-start(bf16[64,2048]{1,0:T(8,128)(2,1)S(1)} %pad_maximum_fusion), channel_id=1, source_target_pairs={{0,24},{1,25},{2,26},{3,27},{4,28},{5,29},{6,30},{7,31},{8,0},{9,1... | collective-permute-start | bytes 786440 | tf_op jit(solution)/shard_map/ppermute | solution.py:437
  31.9 2.1 %collective-permute-start.9 = (bf16[64,2048]{1,0:T(8,128)(2,1)S(1)}, bf16[64,2048]{1,0:T(8,128)(2,1)S(1)}, u32[]{:S(2)}, u32[]{:S(2)}) collective-permute-start(bf16[64,2048]{1,0:T(8,128)(2,1)S(1)} %pad_maximum_fusion), channel_id=1, source_target_pairs={{0,16},{1,17},{2,18},{3,19},{4,20},{5,21},{6,22},{7,23},{8,24},{9,... | collective-permute-start | bytes 786440 | tf_op jit(solution)/shard_map/ppermute | solution.py:437
  33.9 2.2 %copy-done.1 = bf16[2048,1024]{1,0:T(8,128)(2,1)S(1)} copy-done((bf16[2048,1024]{1,0:T(8,128)(2,1)S(1)}, bf16[2048,1024]{1,0:T(8,128)(2,1)}, u32[]{:S(2)}) %copy-start.1) | copy-done | bytes 4194328
  36.1 2.5 %bring_in.1.vocabulary = bf16[2,2048,1024]{2,1,0:T(8,128)(2,1)S(1)} custom-call(bf16[2048,1024]{1,0:T(8,128)(2,1)S(1)} %copy-done.1, bf16[2048,1024]{1,0:T(8,128)(2,1)} %collective-permute-done.2.other), custom_call_target="tpu_custom_call" | custom-call | bytes 8388608 | tf_op jit(solution)/shard_map/bring_in/pallas_call | solution.py:362
  38.6 2.0 %collective-permute-start.6 = (bf16[128,2048]{1,0:T(8,128)(2,1)S(1)}, bf16[128,2048]{1,0:T(8,128)(2,1)S(1)}, u32[]{:S(2)}, u32[]{:S(2)}) collective-permute-start(bf16[128,2048]{1,0:T(8,128)(2,1)S(1)} %constant_dynamic-update-slice_fusion.one), channel_id=1, source_target_pairs={{0,2},{1,3},{2,4},{3,5},{4,6},{5,7},{6,0},{7,1},{8,10},{9,11},{10,... | collective-permute-start | bytes 1572872 | tf_op jit(solution)/shard_map/ppermute | solution.py:441
  40.7 3.8 %collective-permute-start.10 = (bf16[128,2048]{1,0:T(8,128)(2,1)S(1)}, bf16[128,2048]{1,0:T(8,128)(2,1)S(1)}, u32[]{:S(2)}, u32[]{:S(2)}) collective-permute-start(bf16[128,2048]{1,0:T(8,128)(2,1)S(1)} %constant_dynamic-update-slice_fusion.2.two), channel_id=1, source_target_pairs={{0,6},{1,7},{2,0},{3,1},{4,2},{5,3},{6,4},{7,5},{8,14},{9,15},{10,... | collective-permute-start | bytes 1572872 | tf_op jit(solution)/shard_map/ppermute | solution.py:441
  44.5 0.4 collective-permute-start.13
  44.9 1.6 %collective-permute-start.12 = (bf16[128,2048]{1,0:T(8,128)(2,1)S(1)}, bf16[128,2048]{1,0:T(8,128)(2,1)S(1)}, u32[]{:S(2)}, u32[]{:S(2)}) collective-permute-start(bf16[128,2048]{1,0:T(8,128)(2,1)S(1)} %constant_dynamic-update-slice_fusion.2.two), channel_id=1, source_target_pairs={{0,2},{1,3},{2,4},{3,5},{4,6},{5,7},{6,0},{7,1},{8,10},{9,11},{10,... | collective-permute-start | bytes 1572872 | tf_op jit(solution)/shard_map/ppermute | solution.py:442
  46.5 3.4 %collective-permute-done.6.one = bf16[128,2048]{1,0:T(8,128)(2,1)S(1)} collective-permute-done((bf16[128,2048]{1,0:T(8,128)(2,1)S(1)}, bf16[128,2048]{1,0:T(8,128)(2,1)S(1)}, u32[]{:S(2)}, u32[]{:S(2)}) %collective-permute-start.6) | collective-permute-done | bytes 524320 | tf_op jit(solution)/shard_map/ppermute | solution.py:441
  49.9 1.3 %collective-permute-done.10.two = bf16[128,2048]{1,0:T(8,128)(2,1)S(1)} collective-permute-done((bf16[128,2048]{1,0:T(8,128)(2,1)S(1)}, bf16[128,2048]{1,0:T(8,128)(2,1)S(1)}, u32[]{:S(2)}, u32[]{:S(2)}) %collective-permute-start.10) | collective-permute-done | bytes 524320 | tf_op jit(solution)/shard_map/ppermute | solution.py:441
  51.2 3.7 %collective-permute-start.11 = (bf16[128,2048]{1,0:T(8,128)(2,1)S(1)}, bf16[128,2048]{1,0:T(8,128)(2,1)S(1)}, u32[]{:S(2)}, u32[]{:S(2)}) collective-permute-start(bf16[128,2048]{1,0:T(8,128)(2,1)S(1)} %collective-permute-done.10.two), channel_id=1, source_target_pairs={{0,6},{1,7},{2,0},{3,1},{4,2},{5,3},{6,4},{7,5},{8,14},{9,15},{10,... | collective-permute-start | bytes 1572872 | tf_op jit(solution)/shard_map/ppermute | solution.py:443
  54.9 2.6 %score.3.refs_0_ = f32[8,256]{1,0:T(8,128)S(1)} custom-call(bf16[128,2048]{1,0:T(8,128)(2,1)S(1)} %constant_dynamic-update-slice_fusion.one, bf16[128,2048]{1,0:T(8,128)(2,1)S(1)} %constant_dynamic-update-slice_fusion.2.two, bf16[2,2048,1024]{2,1,0:T(8,128)(2,1)S(1)} %bring_in.1.vocabulary, s32[1,1024]{1,0:T(1,128)S(1)} %reshape.60.target), custom_call_target="tpu_custom_call" | custom-call | flops 2147483648 | bytes 9437184 | tf_op jit(solution)/shard_map/score/pallas_call | solution.py:303
  57.4 2.6 %score.4.refs_1_ = f32[8,256]{1,0:T(8,128)S(1)} custom-call(bf16[128,2048]{1,0:T(8,128)(2,1)S(1)} %collective-permute-done.6.one, bf16[128,2048]{1,0:T(8,128)(2,1)S(1)} %collective-permute-done.10.two, bf16[2,2048,1024]{2,1,0:T(8,128)(2,1)S(1)} %bring_in.1.vocabulary, s32[1,1024]{1,0:T(1,128)S(1)} %reshape.60.target), custom_call_target="tpu_custom_call" | custom-call | flops 2147483648 | bytes 9437184 | tf_op jit(solution)/shard_map/score/pallas_call | solution.py:303
  60.0 2.6 %score.5.refs_2_ = f32[8,256]{1,0:T(8,128)S(1)} custom-call(bf16[128,2048]{1,0:T(8,128)(2,1)S(1)} %collective-permute-done.12.one, bf16[128,2048]{1,0:T(8,128)(2,1)S(1)} %collective-permute-done.13.two, bf16[2,2048,1024]{2,1,0:T(8,128)(2,1)S(1)} %bring_in.1.vocabulary, s32[1,1024]{1,0:T(1,128)S(1)} %reshape.60.target), custom_call_target="tpu_custom_call" | custom-call | flops 2147483648 | bytes 9437184 | tf_op jit(solution)/shard_map/score/pallas_call | solution.py:303
  62.6 3.2 %last_score.1 = f32[128,64]{1,0:T(8,128)S(1)} custom-call(s32[32]{0:T(128)S(1)} %fusion.1.order, bf16[128,2048]{1,0:T(8,128)(2,1)S(1)} %collective-permute-done.7.one, bf16[128,2048]{1,0:T(8,128)(2,1)S(1)} %collective-permute-done.11.two, bf16[2,2048,1024]{2,1,0:T(8,128)(2,1)S(1)} %bring_in.1.vocabulary, s32[1,1024]{1,0:T(1,128)S(1)} %reshape.60.target, ...), custom_call_target="tpu_custom_call" | custom-call | flops 2147483648 | bytes 9437184 | tf_op jit(solution)/shard_map/last_score/pallas_call | solution.py:303
  65.8 16.6 %all_to_all.11 = f32[128,1,64]{2,1,0:T(1,128)S(1)} all-to-all(f32[128,1,64]{2,1,0:T(1,128)S(1)} %bitcast.22), channel_id=1, replica_groups=mesh['xl'=2,'c'=2,'y'=4,'z'=4,'xh'=2] {'xl','c','y','z','xh'}, dimensions={0} | all-to-all | bytes 65536 | tf_op jit(solution)/shard_map/all_to_all | solution.py:450
  82.4 0.7 finish.1
  (32 shorter events, 0.9 us)
Async XLA Ops:
  0.0 19.6 %copy-start = (s32[512,4]{0,1:T(4,128)S(1)}, s32[512,4]{0,1:T(4,128)}, u32[]{:S(2)}) copy-start(s32[512,4]{0,1:T(4,128)} %param.33) | copy-start | bytes 24580
  0.0 28.5 %collective-permute-start.2 = (bf16[2048,1024]{1,0:T(8,128)(2,1)}, bf16[2048,1024]{1,0:T(8,128)(2,1)}, u32[]{:S(2)}, u32[]{:S(2)}) collective-permute-start(bf16[2048,1024]{1,0:T(8,128)(2,1)} %own.1), channel_id=1, source_target_pairs={{0,32},{1,33},{2,34},{3,35},{4,36},{5,37},{6,38},{7,39},{8,40},{9,... | collective-permute-start | bytes 12582920 | tf_op jit(solution)/shard_map/ppermute | solution.py:400
  0.0 28.4 %copy-start.2 = (f32[2048]{0:T(1024)S(1)}, f32[2048]{0:T(1024)}, u32[]{:S(2)}) copy-start(f32[2048]{0:T(1024)} %param.31) | copy-start | bytes 24580
  12.1 1.7 %collective-permute-start = (bf16[32,2048]{1,0:T(8,128)(2,1)}, bf16[32,2048]{1,0:T(8,128)(2,1)S(1)}, u32[]{:S(2)}, u32[]{:S(2)}) collective-permute-start(bf16[32,2048]{1,0:T(8,128)(2,1)} %get-tuple-element.26), channel_id=1, source_target_pairs={{0,32},{1,33},{2,34},{3,35},{4,36},{5,37},{6,38},{7,39},{8,40},{9,... | collective-permute-start | bytes 393224 | tf_op jit(solution)/shard_map/ppermute | solution.py:419
  14.8 8.6 %collective-permute-start.1 = (bf16[32,2048]{1,0:T(8,128)(2,1)S(1)}, bf16[32,2048]{1,0:T(8,128)(2,1)S(1)}, u32[]{:S(2)}, u32[]{:S(2)}) collective-permute-start(bf16[32,2048]{1,0:T(8,128)(2,1)S(1)} %add_convert_fusion), channel_id=1, source_target_pairs={{0,64},{1,65},{2,66},{3,67},{4,68},{5,69},{6,70},{7,71},{8,72},{9,... | collective-permute-start | bytes 393224 | tf_op jit(solution)/shard_map/ppermute | solution.py:426
  16.5 9.4 %collective-permute-start.3 = (bf16[32,2048]{1,0:T(8,128)(2,1)S(1)}, bf16[32,2048]{1,0:T(8,128)(2,1)S(1)}, u32[]{:S(2)}, u32[]{:S(2)}) collective-permute-start(bf16[32,2048]{1,0:T(8,128)(2,1)S(1)} %add_convert_fusion), channel_id=1, source_target_pairs={{0,1},{1,0},{2,3},{3,2},{4,5},{5,4},{6,7},{7,6},{8,9},{9,8},{10,11... | collective-permute-start | bytes 393224 | tf_op jit(solution)/shard_map/ppermute | solution.py:426
  19.2 9.0 %collective-permute-start.4 = (bf16[32,2048]{1,0:T(8,128)(2,1)S(1)}, bf16[32,2048]{1,0:T(8,128)(2,1)S(1)}, u32[]{:S(2)}, u32[]{:S(2)}) collective-permute-start(bf16[32,2048]{1,0:T(8,128)(2,1)S(1)} %add_convert_fusion), channel_id=1, source_target_pairs={{0,65},{1,64},{2,67},{3,66},{4,69},{5,68},{6,71},{7,70},{8,73},{9,... | collective-permute-start | bytes 393224 | tf_op jit(solution)/shard_map/ppermute | solution.py:426
  28.5 10.1 %collective-permute-start.5 = (bf16[64,2048]{1,0:T(8,128)(2,1)S(1)}, bf16[64,2048]{1,0:T(8,128)(2,1)S(1)}, u32[]{:S(2)}, u32[]{:S(2)}) collective-permute-start(bf16[64,2048]{1,0:T(8,128)(2,1)S(1)} %pad_maximum_fusion), channel_id=1, source_target_pairs={{0,8},{1,9},{2,10},{3,11},{4,12},{5,13},{6,14},{7,15},{8,16},{9,17... | collective-permute-start | bytes 786440 | tf_op jit(solution)/shard_map/ppermute | solution.py:437
  30.2 10.4 %collective-permute-start.8 = (bf16[64,2048]{1,0:T(8,128)(2,1)S(1)}, bf16[64,2048]{1,0:T(8,128)(2,1)S(1)}, u32[]{:S(2)}, u32[]{:S(2)}) collective-permute-start(bf16[64,2048]{1,0:T(8,128)(2,1)S(1)} %pad_maximum_fusion), channel_id=1, source_target_pairs={{0,24},{1,25},{2,26},{3,27},{4,28},{5,29},{6,30},{7,31},{8,0},{9,1... | collective-permute-start | bytes 786440 | tf_op jit(solution)/shard_map/ppermute | solution.py:437
  31.9 8.8 %collective-permute-start.9 = (bf16[64,2048]{1,0:T(8,128)(2,1)S(1)}, bf16[64,2048]{1,0:T(8,128)(2,1)S(1)}, u32[]{:S(2)}, u32[]{:S(2)}) collective-permute-start(bf16[64,2048]{1,0:T(8,128)(2,1)S(1)} %pad_maximum_fusion), channel_id=1, source_target_pairs={{0,16},{1,17},{2,18},{3,19},{4,20},{5,21},{6,22},{7,23},{8,24},{9,... | collective-permute-start | bytes 786440 | tf_op jit(solution)/shard_map/ppermute | solution.py:437
  33.9 2.2 %copy-start.1 = (bf16[2048,1024]{1,0:T(8,128)(2,1)S(1)}, bf16[2048,1024]{1,0:T(8,128)(2,1)}, u32[]{:S(2)}) copy-start(bf16[2048,1024]{1,0:T(8,128)(2,1)} %own.1) | copy-start | bytes 12582916
  38.6 11.3 %collective-permute-start.6 = (bf16[128,2048]{1,0:T(8,128)(2,1)S(1)}, bf16[128,2048]{1,0:T(8,128)(2,1)S(1)}, u32[]{:S(2)}, u32[]{:S(2)}) collective-permute-start(bf16[128,2048]{1,0:T(8,128)(2,1)S(1)} %constant_dynamic-update-slice_fusion.one), channel_id=1, source_target_pairs={{0,2},{1,3},{2,4},{3,5},{4,6},{5,7},{6,0},{7,1},{8,10},{9,11},{10,... | collective-permute-start | bytes 1572872 | tf_op jit(solution)/shard_map/ppermute | solution.py:441
  40.7 10.5 %collective-permute-start.10 = (bf16[128,2048]{1,0:T(8,128)(2,1)S(1)}, bf16[128,2048]{1,0:T(8,128)(2,1)S(1)}, u32[]{:S(2)}, u32[]{:S(2)}) collective-permute-start(bf16[128,2048]{1,0:T(8,128)(2,1)S(1)} %constant_dynamic-update-slice_fusion.2.two), channel_id=1, source_target_pairs={{0,6},{1,7},{2,0},{3,1},{4,2},{5,3},{6,4},{7,5},{8,14},{9,15},{10,... | collective-permute-start | bytes 1572872 | tf_op jit(solution)/shard_map/ppermute | solution.py:441
  44.5 15.5 %collective-permute-start.13 = (bf16[128,2048]{1,0:T(8,128)(2,1)S(1)}, bf16[128,2048]{1,0:T(8,128)(2,1)S(1)}, u32[]{:S(2)}, u32[]{:S(2)}) collective-permute-start(bf16[128,2048]{1,0:T(8,128)(2,1)S(1)} %constant_dynamic-update-slice_fusion.one), channel_id=1, source_target_pairs={{0,6},{1,7},{2,0},{3,1},{4,2},{5,3},{6,4},{7,5},{8,14},{9,15},{10,... | collective-permute-start | bytes 1572872 | tf_op jit(solution)/shard_map/ppermute | solution.py:442
  44.9 15.1 %collective-permute-start.12 = (bf16[128,2048]{1,0:T(8,128)(2,1)S(1)}, bf16[128,2048]{1,0:T(8,128)(2,1)S(1)}, u32[]{:S(2)}, u32[]{:S(2)}) collective-permute-start(bf16[128,2048]{1,0:T(8,128)(2,1)S(1)} %constant_dynamic-update-slice_fusion.2.two), channel_id=1, source_target_pairs={{0,2},{1,3},{2,4},{3,5},{4,6},{5,7},{6,0},{7,1},{8,10},{9,11},{10,... | collective-permute-start | bytes 1572872 | tf_op jit(solution)/shard_map/ppermute | solution.py:442
  49.9 12.7 %collective-permute-start.7 = (bf16[128,2048]{1,0:T(8,128)(2,1)S(1)}, bf16[128,2048]{1,0:T(8,128)(2,1)S(1)}, u32[]{:S(2)}, u32[]{:S(2)}) collective-permute-start(bf16[128,2048]{1,0:T(8,128)(2,1)S(1)} %collective-permute-done.6.one), channel_id=1, source_target_pairs={{0,2},{1,3},{2,4},{3,5},{4,6},{5,7},{6,0},{7,1},{8,10},{9,11},{10,... | collective-permute-start | bytes 1572872 | tf_op jit(solution)/shard_map/ppermute | solution.py:443
  51.2 11.4 %collective-permute-start.11 = (bf16[128,2048]{1,0:T(8,128)(2,1)S(1)}, bf16[128,2048]{1,0:T(8,128)(2,1)S(1)}, u32[]{:S(2)}, u32[]{:S(2)}) collective-permute-start(bf16[128,2048]{1,0:T(8,128)(2,1)S(1)} %collective-permute-done.10.two), channel_id=1, source_target_pairs={{0,6},{1,7},{2,0},{3,1},{4,2},{5,3},{6,4},{7,5},{8,14},{9,15},{10,... | collective-permute-start | bytes 1572872 | tf_op jit(solution)/shard_map/ppermute | solution.py:443

commit v8 on v7

--- a/solution.py
+++ b/solution.py
@@ -251,9 +251,9 @@
 TILE = 512
 
 
-def score_block(parts, vocabulary, target, offset):
+def score_block(parts, own, other, target, offset):
     piece = jnp.concatenate([part[...] for part in parts], axis=0)
-    size, cols = piece.shape[0], vocabulary.shape[2]
+    size, cols = piece.shape[0], own.shape[1]
     _, core, head_group, batch_group = position()
     base = (head_group * GROUPS + batch_group) * cols
     bases = (base, base + (1 - 2 * core) * GROUPS * cols)
@@ -262,11 +262,9 @@
     running = jnp.zeros((size, 128), F32)
     found = jnp.zeros((size, 128), F32)
     for start in range(0, cols, TILE):
-        for which in range(2):
-            logits = jnp.dot(
-                piece, vocabulary[which, :, start : start + TILE], preferred_element_type=F32
-            )
-            left = want - (bases[which] + start)
+        for base, weight in zip(bases, (own, other)):
+            logits = jnp.dot(piece, weight[:, start : start + TILE], preferred_element_type=F32)
+            left = want - (base + start)
             for s in range(0, TILE, 128):
                 part = logits[:, s : s + 128]
                 running = running + jnp.exp(part)
@@ -276,13 +274,14 @@
     return jnp.where(lane == 0, sums, hits).T[:8, :]
 
 
-def score_kernel(offset, one, two, vocabulary, target, stats):
-    stats[...] = score_block((one, two), vocabulary, target, offset)
-
-
-def last_score_kernel(offset, order, one, two, vocabulary, target, *refs):
+def score_kernel(offset, one, two, own, other, target, stats):
+    stats[...] = score_block((one, two), own, other, target, offset)
+
+
+def last_score_kernel(offset, order, one, two, own, other, target, *refs):
     earlier, outgoing = refs[:-1], refs[-1]
-    blocks = [part[...] for part in earlier] + [score_block((one, two), vocabulary, target, offset)]
+    blocks = [part[...] for part in earlier]
+    blocks.append(score_block((one, two), own, other, target, offset))
     half = outgoing.shape[1] // 2
     at = 0
     for block in blocks:
@@ -293,9 +292,9 @@
             at += 1
 
 
-def score(parts, vocabulary, target, offset, earlier=(), order=None):
+def score(parts, own, other, target, offset, earlier=(), order=None):
     size, width = parts[0].shape
-    rows, cols = 2 * size, vocabulary.shape[2]
+    rows, cols = 2 * size, own.shape[1]
     near = pl.BlockSpec(memory_space=pltpu.VMEM)
     last = order is not None
     kernel = last_score_kernel if last else score_kernel
@@ -305,7 +304,7 @@
         grid_spec=pltpu.PrefetchScalarGridSpec(
             num_scalar_prefetch=int(last),
             grid=(),
-            in_specs=[near] * (4 + len(earlier)),
+            in_specs=[near] * (5 + len(earlier)),
             out_specs=near,
         ),
         out_shape=jax.ShapeDtypeStruct(shape, F32),
@@ -316,7 +315,7 @@
             transcendentals=2 * rows * cols,
         ),
         name="last_score" if last else "score",
-    )(*([order] if last else []), *parts, vocabulary, target, *earlier)
+    )(*([order] if last else []), *parts, own, other, target, *earlier)
 
 
 def finish_kernel(incoming, marks, scores):
@@ -347,30 +346,25 @@
     )(incoming, marks)
 
 
-def gather_kernel(own, other, both, sems):
-    copies = [
-        pltpu.make_async_copy(source, both.at[i], sems.at[i])
-        for i, source in enumerate((own, other))
-    ]
-    for copy in copies:
-        copy.start()
-    for copy in copies:
-        copy.wait()
-
-
-def bring_in(own, other):
+def bring_kernel(source, target, sem):
+    copy = pltpu.make_async_copy(source, target, sem)
+    copy.start()
+    copy.wait()
+
+
+def bring_in(slice_of_head):
     return pl.pallas_call(
-        gather_kernel,
-        in_specs=[pl.BlockSpec(memory_space=pltpu.HBM)] * 2,
+        bring_kernel,
+        in_specs=[pl.BlockSpec(memory_space=pltpu.HBM)],
         out_specs=pl.BlockSpec(memory_space=pltpu.VMEM),
-        scratch_shapes=[pltpu.SemaphoreType.DMA((2,))],
-        out_shape=jax.ShapeDtypeStruct((2, *own.shape), own.dtype),
-        compiler_params=pltpu.CompilerParams(vmem_limit_bytes=12 << 20),
+        scratch_shapes=[pltpu.SemaphoreType.DMA],
+        out_shape=jax.ShapeDtypeStruct(slice_of_head.shape, slice_of_head.dtype),
+        compiler_params=pltpu.CompilerParams(vmem_limit_bytes=8 << 20),
         cost_estimate=pl.CostEstimate(
-            flops=0, bytes_accessed=4 * own.size, transcendentals=0
+            flops=0, bytes_accessed=2 * slice_of_head.size, transcendentals=0
         ),
         name="bring_in",
-    )(own, other)
+    )(slice_of_head)
 
 
 def per_device(
@@ -433,20 +427,21 @@
 
     both = jnp.concatenate([finish(pair, low), finish(high, corner)], 0)
     far_head, both = lax.optimization_barrier((far_head, both))
-    vocabulary = bring_in(lm_head, far_head)
+    far_head = bring_in(far_head)
     ahead, behind, across = [send(both, perm=p) for p in NEAR]
-    ahead, vocabulary = lax.optimization_barrier((ahead, vocabulary))
+    ahead, far_head = lax.optimization_barrier((ahead, far_head))
     one, two = jnp.concatenate([both, ahead], 0), jnp.concatenate([behind, across], 0)
     size = one.shape[0]
     forth_one, back_two = send(one, perm=FAR[0]), send(two, perm=FAR[1])
     forth_two, back_one = send(two, perm=FAR[0]), send(one, perm=FAR[1])
+    own_head = lm_head
     halves = [send(forth_one, perm=FAR[0]), send(back_two, perm=FAR[1])]
     stats = []
     arrivals = ((one, two), (forth_one, back_two), (forth_two, back_one))
     for i, parts in enumerate(arrivals):
-        stats.append(score(parts, vocabulary, wanted, 2 * size * i))
+        stats.append(score(parts, own_head, far_head, wanted, 2 * size * i))
         wanted, stats[i] = lax.optimization_barrier((wanted, stats[i]))
-    outgoing = score(halves, vocabulary, wanted, 6 * size, stats, order)
+    outgoing = score(halves, own_head, far_head, wanted, 6 * size, stats, order)
     incoming = lax.all_to_all(outgoing, AXES, 0, 0, tiled=True)
     return finish_scores(incoming, marks).T
 

time: 84 us -> 84.1 us (level)
  local copies, waits for them, and re-layouts: 4.55 us -> 2.36 us
  starting transfers between devices: 22.2 us -> 24.2 us
  blocking collectives: 16.6 us -> 17.6 us
    unnamed x8, local copies, waits for them, and re-layouts: 2.23 us -> 0.05 us
    ppermute x2, starting transfers between devices: 5.76 us -> 7.86 us  [per_device(): forth_one, back_two = (send(one, perm=FAR[0]), send(two, perm=FAR[1]))]
    ppermute x3, waiting for transfers between devices: 4.62 us -> 2.63 us  [per_device(): send(pair, perm=p)]
    ppermute x3, waiting for transfers between devices: 0.01 us -> 1.42 us  [per_device(): ahead, behind, across = [send(both, perm=p) for p in NEAR]]
    all_to_all x1, blocking collectives: 16.6 us -> 17.6 us  [per_device(): incoming = lax.all_to_all(outgoing, AXES, 0, 0, tiled=True)]
  transfers between devices with their start and end apart: 14 -> 14, of which waited for: 5 -> 6; matrix products, arithmetic and copies ran while one was open for 6% -> 6% of each run, Pallas kernels for 27% -> 27%
where the time goes in v8:
time: 84.1 us; the launch traced here: 83.3 us
  Pallas kernels  26.1 us (31%)
  starting transfers between devices  24.2 us (29%)
  blocking collectives  17.6 us (21%)
  waiting for transfers between devices  9.9 us (12%)
  other arithmetic  2.95 us (4%)
  local copies, waits for them, and re-layouts  2.36 us (3%)
    all_to_all x1, blocking collectives, per_device(): incoming = lax.all_to_all(outgoing, AXES, 0, 0, tiled=True)  17.6 us
    pallas_call x1, Pallas kernels, front(): pl.pallas_call(front_kernel, grid_spec=pltpu.PrefetchScalarGridSpec(num_s...  12.1 us
    pallas_call x4, Pallas kernels, score(): pl.pallas_call(functools.partial(kernel, offset), grid_spec=pltpu.Prefetc...  10.9 us
    ppermute x2, starting transfers between devices, per_device(): forth_one, back_two = (send(one, perm=FAR[0]), send(two, perm=FAR[1]))  7.86 us
    ppermute x3, starting transfers between devices, per_device(): ahead, behind, across = [send(both, perm=p) for p in NEAR]  5.9 us
    ppermute x2, waiting for transfers between devices, per_device(): forth_one, back_two = (send(one, perm=FAR[0]), send(two, perm=FAR[1]))  4.64 us
    ppermute x3, starting transfers between devices, per_device(): send(pair, perm=p)  4.19 us
    ppermute x2, starting transfers between devices, per_device(): halves = [send(forth_one, perm=FAR[0]), send(back_two, perm=FAR[1])]  3.72 us
  transfers between devices with their start and end apart: 14, of which 6 were waited for; matrix products, arithmetic and copies ran while one was open for 6% of the time, Pallas kernels for 27%

profile of v8, /device:TPU:0, one launch (start us, length us, event | category | flops | bytes accessed | tf_op | source)
XLA Modules:
  0.0 83.3 jit_solution(3332595800422378417)
XLA Ops:
  0.0 12.1 %front.1 = (bf16[32,2048]{1,0:T(8,128)(2,1)}, f32[32,2048]{1,0:T(8,128)}) custom-call(f32[32]{0:T(128)} %rate.1, f32[32]{0:T(128)} %offset.1, bf16[4,16,2048]{2,1,0:T(8,128)(2,1)} %embedded.1, bf16[16,8,128,128]{3,2,1,0:T(8,128)(2,1)} %states.1, bf16[2048,512]{1,0:T(8,128)(2,1)} %w_query.1, bf16[2048,512]{1,0:T(8,128)(2,1)} %w_key.1, ...), custom_call_target="tpu_custom_call" | custom-call | flops 1073741824 | bytes 22020096 | tf_op jit(solution)/shard_map/front/pallas_call | solution.py:206
  12.1 0.5 collective-permute-start
  12.6 1.2 %collective-permute-done = bf16[32,2048]{1,0:T(8,128)(2,1)S(1)} collective-permute-done((bf16[32,2048]{1,0:T(8,128)(2,1)}, bf16[32,2048]{1,0:T(8,128)(2,1)S(1)}, u32[]{:S(2)}, u32[]{:S(2)}) %collective-permute-start) | collective-permute-done | bytes 131104 | tf_op jit(solution)/shard_map/ppermute | solution.py:413
  13.8 1.0 %add_convert_fusion = bf16[32,2048]{1,0:T(8,128)(2,1)S(1)} fusion(f32[32,2048]{1,0:T(8,128)} %get-tuple-element.25, bf16[32,2048]{1,0:T(8,128)(2,1)S(1)} %collective-permute-done), kind=kLoop, calls=%fused_computation.8 | loop fusion | flops 196608 | bytes 524288 | tf_op jit(solution)/shard_map/convert_element_type | solution.py:413
  14.8 2.9 %collective-permute-start.4 = (bf16[32,2048]{1,0:T(8,128)(2,1)S(1)}, bf16[32,2048]{1,0:T(8,128)(2,1)S(1)}, u32[]{:S(2)}, u32[]{:S(2)}) collective-permute-start(bf16[32,2048]{1,0:T(8,128)(2,1)S(1)} %add_convert_fusion), channel_id=1, source_target_pairs={{0,65},{1,64},{2,67},{3,66},{4,69},{5,68},{6,71},{7,70},{8,73},{9,... | collective-permute-start | bytes 393224 | tf_op jit(solution)/shard_map/ppermute | solution.py:420
  17.7 0.8 collective-permute-start.3
  18.5 0.5 collective-permute-start.1
  19.1 0.7 fusion
  19.8 0.6 gather_fusion
  20.4 0.7 compare_and_fusion
  21.3 0.8 dynamic-slice_bitcast_fusion.1.marks
  22.0 0.7 fusion.1.order
  22.8 2.5 %collective-permute-done.1 = bf16[32,2048]{1,0:T(8,128)(2,1)S(1)} collective-permute-done((bf16[32,2048]{1,0:T(8,128)(2,1)S(1)}, bf16[32,2048]{1,0:T(8,128)(2,1)S(1)}, u32[]{:S(2)}, u32[]{:S(2)}) %collective-permute-start.1) | collective-permute-done | bytes 131104 | tf_op jit(solution)/shard_map/ppermute | solution.py:420
  25.6 0.2 multiply_reduce_fusion
  25.9 1.6 %collective-permute-start.5 = (bf16[64,2048]{1,0:T(8,128)(2,1)S(1)}, bf16[64,2048]{1,0:T(8,128)(2,1)S(1)}, u32[]{:S(2)}, u32[]{:S(2)}) collective-permute-start(bf16[64,2048]{1,0:T(8,128)(2,1)S(1)} %pad_maximum_fusion), channel_id=1, source_target_pairs={{0,8},{1,9},{2,10},{3,11},{4,12},{5,13},{6,14},{7,15},{8,16},{9,17... | collective-permute-start | bytes 786440 | tf_op jit(solution)/shard_map/ppermute | solution.py:431
  27.6 2.9 %collective-permute-start.9 = (bf16[64,2048]{1,0:T(8,128)(2,1)S(1)}, bf16[64,2048]{1,0:T(8,128)(2,1)S(1)}, u32[]{:S(2)}, u32[]{:S(2)}) collective-permute-start(bf16[64,2048]{1,0:T(8,128)(2,1)S(1)} %pad_maximum_fusion), channel_id=1, source_target_pairs={{0,16},{1,17},{2,18},{3,19},{4,20},{5,21},{6,22},{7,23},{8,24},{9,... | collective-permute-start | bytes 786440 | tf_op jit(solution)/shard_map/ppermute | solution.py:431
  30.5 1.3 %collective-permute-start.8 = (bf16[64,2048]{1,0:T(8,128)(2,1)S(1)}, bf16[64,2048]{1,0:T(8,128)(2,1)S(1)}, u32[]{:S(2)}, u32[]{:S(2)}) collective-permute-start(bf16[64,2048]{1,0:T(8,128)(2,1)S(1)} %pad_maximum_fusion), channel_id=1, source_target_pairs={{0,24},{1,25},{2,26},{3,27},{4,28},{5,29},{6,30},{7,31},{8,0},{9,1... | collective-permute-start | bytes 786440 | tf_op jit(solution)/shard_map/ppermute | solution.py:431
  31.9 2.3 %bring_in.1.other = bf16[2048,1024]{1,0:T(8,128)(2,1)S(1)} custom-call(bf16[2048,1024]{1,0:T(8,128)(2,1)} %collective-permute-done.2.source), custom_call_target="tpu_custom_call" | custom-call | bytes 4194304 | tf_op jit(solution)/shard_map/bring_in/pallas_call | solution.py:356
  34.3 2.0 %collective-permute-start.6 = (bf16[128,2048]{1,0:T(8,128)(2,1)S(1)}, bf16[128,2048]{1,0:T(8,128)(2,1)S(1)}, u32[]{:S(2)}, u32[]{:S(2)}) collective-permute-start(bf16[128,2048]{1,0:T(8,128)(2,1)S(1)} %constant_dynamic-update-slice_fusion.one), channel_id=1, source_target_pairs={{0,2},{1,3},{2,4},{3,5},{4,6},{5,7},{6,0},{7,1},{8,10},{9,11},{10,... | collective-permute-start | bytes 1572872 | tf_op jit(solution)/shard_map/ppermute | solution.py:435
  36.3 1.0 %collective-permute-done.8 = bf16[64,2048]{1,0:T(8,128)(2,1)S(1)} collective-permute-done((bf16[64,2048]{1,0:T(8,128)(2,1)S(1)}, bf16[64,2048]{1,0:T(8,128)(2,1)S(1)}, u32[]{:S(2)}, u32[]{:S(2)}) %collective-permute-start.8) | collective-permute-done | bytes 262176 | tf_op jit(solution)/shard_map/ppermute | solution.py:431
  37.3 0.4 collective-permute-done.9
  37.7 5.9 %collective-permute-start.10 = (bf16[128,2048]{1,0:T(8,128)(2,1)S(1)}, bf16[128,2048]{1,0:T(8,128)(2,1)S(1)}, u32[]{:S(2)}, u32[]{:S(2)}) collective-permute-start(bf16[128,2048]{1,0:T(8,128)(2,1)S(1)} %constant_dynamic-update-slice_fusion.2.two), channel_id=1, source_target_pairs={{0,6},{1,7},{2,0},{3,1},{4,2},{5,3},{6,4},{7,5},{8,14},{9,15},{10,... | collective-permute-start | bytes 1572872 | tf_op jit(solution)/shard_map/ppermute | solution.py:435
  43.6 0.4 collective-permute-start.13
  44.0 1.6 %collective-permute-start.12 = (bf16[128,2048]{1,0:T(8,128)(2,1)S(1)}, bf16[128,2048]{1,0:T(8,128)(2,1)S(1)}, u32[]{:S(2)}, u32[]{:S(2)}) collective-permute-start(bf16[128,2048]{1,0:T(8,128)(2,1)S(1)} %constant_dynamic-update-slice_fusion.2.two), channel_id=1, source_target_pairs={{0,2},{1,3},{2,4},{3,5},{4,6},{5,7},{6,0},{7,1},{8,10},{9,11},{10,... | collective-permute-start | bytes 1572872 | tf_op jit(solution)/shard_map/ppermute | solution.py:436
  45.7 4.6 %collective-permute-done.10.two = bf16[128,2048]{1,0:T(8,128)(2,1)S(1)} collective-permute-done((bf16[128,2048]{1,0:T(8,128)(2,1)S(1)}, bf16[128,2048]{1,0:T(8,128)(2,1)S(1)}, u32[]{:S(2)}, u32[]{:S(2)}) %collective-permute-start.10) | collective-permute-done | bytes 524320 | tf_op jit(solution)/shard_map/ppermute | solution.py:435
  50.3 3.7 %collective-permute-start.11 = (bf16[128,2048]{1,0:T(8,128)(2,1)S(1)}, bf16[128,2048]{1,0:T(8,128)(2,1)S(1)}, u32[]{:S(2)}, u32[]{:S(2)}) collective-permute-start(bf16[128,2048]{1,0:T(8,128)(2,1)S(1)} %collective-permute-done.10.two), channel_id=1, source_target_pairs={{0,6},{1,7},{2,0},{3,1},{4,2},{5,3},{6,4},{7,5},{8,14},{9,15},{10,... | collective-permute-start | bytes 1572872 | tf_op jit(solution)/shard_map/ppermute | solution.py:438
  54.0 2.6 %score.3.refs_0_ = f32[8,256]{1,0:T(8,128)S(1)} custom-call(bf16[128,2048]{1,0:T(8,128)(2,1)S(1)} %constant_dynamic-update-slice_fusion.one, bf16[128,2048]{1,0:T(8,128)(2,1)S(1)} %constant_dynamic-update-slice_fusion.2.two, bf16[2048,1024]{1,0:T(8,128)(2,1)S(1)} %copy-done.1, bf16[2048,1024]{1,0:T(8,128)(2,1)S(1)} %bring_in.1.other, ...), custom_call_target="tpu_custom_call" | custom-call | flops 2147483648 | bytes 9437184 | tf_op jit(solution)/shard_map/score/pallas_call | solution.py:302
  56.6 2.6 %score.4.refs_1_ = f32[8,256]{1,0:T(8,128)S(1)} custom-call(bf16[128,2048]{1,0:T(8,128)(2,1)S(1)} %collective-permute-done.6.one, bf16[128,2048]{1,0:T(8,128)(2,1)S(1)} %collective-permute-done.10.two, bf16[2048,1024]{1,0:T(8,128)(2,1)S(1)} %copy-done.1, bf16[2048,1024]{1,0:T(8,128)(2,1)S(1)} %bring_in.1.other, s32[1,1024]{1,0:T(1,128)S(1)} %reshape.60.target), custom_call_target="tpu_custom_call" | custom-call | flops 2147483648 | bytes 9437184 | tf_op jit(solution)/shard_map/score/pallas_call | solution.py:302
  59.1 2.6 %score.5.refs_2_ = f32[8,256]{1,0:T(8,128)S(1)} custom-call(bf16[128,2048]{1,0:T(8,128)(2,1)S(1)} %collective-permute-done.12.one, bf16[128,2048]{1,0:T(8,128)(2,1)S(1)} %collective-permute-done.13.two, bf16[2048,1024]{1,0:T(8,128)(2,1)S(1)} %copy-done.1, bf16[2048,1024]{1,0:T(8,128)(2,1)S(1)} %bring_in.1.other, s32[1,1024]{1,0:T(1,128)S(1)} %reshape.60.target), custom_call_target="tpu_custom_call" | custom-call | flops 2147483648 | bytes 9437184 | tf_op jit(solution)/shard_map/score/pallas_call | solution.py:302
  61.7 3.2 %last_score.1 = f32[128,64]{1,0:T(8,128)S(1)} custom-call(s32[32]{0:T(128)S(1)} %fusion.1.order, bf16[128,2048]{1,0:T(8,128)(2,1)S(1)} %collective-permute-done.7.one, bf16[128,2048]{1,0:T(8,128)(2,1)S(1)} %collective-permute-done.11.two, bf16[2048,1024]{1,0:T(8,128)(2,1)S(1)} %copy-done.1, bf16[2048,1024]{1,0:T(8,128)(2,1)S(1)} %bring_in.1.other, ...), custom_call_target="tpu_custom_call" | custom-call | flops 2147483648 | bytes 9437184 | tf_op jit(solution)/shard_map/last_score/pallas_call | solution.py:302
  64.9 17.6 %all_to_all.11 = f32[128,1,64]{2,1,0:T(1,128)S(1)} all-to-all(f32[128,1,64]{2,1,0:T(1,128)S(1)} %bitcast.22), channel_id=1, replica_groups=mesh['xl'=2,'c'=2,'y'=4,'z'=4,'xh'=2] {'xl','c','y','z','xh'}, dimensions={0} | all-to-all | bytes 65536 | tf_op jit(solution)/shard_map/all_to_all | solution.py:445
  82.5 0.7 finish.1
  (32 shorter events, 0.9 us)
Async XLA Ops:
  0.0 19.0 %copy-start = (s32[512,4]{0,1:T(4,128)S(1)}, s32[512,4]{0,1:T(4,128)}, u32[]{:S(2)}) copy-start(s32[512,4]{0,1:T(4,128)} %param.33) | copy-start | bytes 24580
  0.0 25.9 %collective-permute-start.2 = (bf16[2048,1024]{1,0:T(8,128)(2,1)}, bf16[2048,1024]{1,0:T(8,128)(2,1)}, u32[]{:S(2)}, u32[]{:S(2)}) collective-permute-start(bf16[2048,1024]{1,0:T(8,128)(2,1)} %own.7), channel_id=1, source_target_pairs={{0,32},{1,33},{2,34},{3,35},{4,36},{5,37},{6,38},{7,39},{8,40},{9,... | collective-permute-start | bytes 12582920 | tf_op jit(solution)/shard_map/ppermute | solution.py:394
  0.0 25.8 %copy-start.2 = (f32[2048]{0:T(1024)S(1)}, f32[2048]{0:T(1024)}, u32[]{:S(2)}) copy-start(f32[2048]{0:T(1024)} %param.31) | copy-start | bytes 24580
  12.1 1.7 %collective-permute-start = (bf16[32,2048]{1,0:T(8,128)(2,1)}, bf16[32,2048]{1,0:T(8,128)(2,1)S(1)}, u32[]{:S(2)}, u32[]{:S(2)}) collective-permute-start(bf16[32,2048]{1,0:T(8,128)(2,1)} %get-tuple-element.26), channel_id=1, source_target_pairs={{0,32},{1,33},{2,34},{3,35},{4,36},{5,37},{6,38},{7,39},{8,40},{9,... | collective-permute-start | bytes 393224 | tf_op jit(solution)/shard_map/ppermute | solution.py:413
  14.8 10.6 %collective-permute-start.4 = (bf16[32,2048]{1,0:T(8,128)(2,1)S(1)}, bf16[32,2048]{1,0:T(8,128)(2,1)S(1)}, u32[]{:S(2)}, u32[]{:S(2)}) collective-permute-start(bf16[32,2048]{1,0:T(8,128)(2,1)S(1)} %add_convert_fusion), channel_id=1, source_target_pairs={{0,65},{1,64},{2,67},{3,66},{4,69},{5,68},{6,71},{7,70},{8,73},{9,... | collective-permute-start | bytes 393224 | tf_op jit(solution)/shard_map/ppermute | solution.py:420
  17.7 7.9 %collective-permute-start.3 = (bf16[32,2048]{1,0:T(8,128)(2,1)S(1)}, bf16[32,2048]{1,0:T(8,128)(2,1)S(1)}, u32[]{:S(2)}, u32[]{:S(2)}) collective-permute-start(bf16[32,2048]{1,0:T(8,128)(2,1)S(1)} %add_convert_fusion), channel_id=1, source_target_pairs={{0,1},{1,0},{2,3},{3,2},{4,5},{5,4},{6,7},{7,6},{8,9},{9,8},{10,11... | collective-permute-start | bytes 393224 | tf_op jit(solution)/shard_map/ppermute | solution.py:420
  18.5 6.8 %collective-permute-start.1 = (bf16[32,2048]{1,0:T(8,128)(2,1)S(1)}, bf16[32,2048]{1,0:T(8,128)(2,1)S(1)}, u32[]{:S(2)}, u32[]{:S(2)}) collective-permute-start(bf16[32,2048]{1,0:T(8,128)(2,1)S(1)} %add_convert_fusion), channel_id=1, source_target_pairs={{0,64},{1,65},{2,66},{3,67},{4,68},{5,69},{6,70},{7,71},{8,72},{9,... | collective-permute-start | bytes 393224 | tf_op jit(solution)/shard_map/ppermute | solution.py:420
  25.9 8.3 %collective-permute-start.5 = (bf16[64,2048]{1,0:T(8,128)(2,1)S(1)}, bf16[64,2048]{1,0:T(8,128)(2,1)S(1)}, u32[]{:S(2)}, u32[]{:S(2)}) collective-permute-start(bf16[64,2048]{1,0:T(8,128)(2,1)S(1)} %pad_maximum_fusion), channel_id=1, source_target_pairs={{0,8},{1,9},{2,10},{3,11},{4,12},{5,13},{6,14},{7,15},{8,16},{9,17... | collective-permute-start | bytes 786440 | tf_op jit(solution)/shard_map/ppermute | solution.py:431
  27.6 10.1 %collective-permute-start.9 = (bf16[64,2048]{1,0:T(8,128)(2,1)S(1)}, bf16[64,2048]{1,0:T(8,128)(2,1)S(1)}, u32[]{:S(2)}, u32[]{:S(2)}) collective-permute-start(bf16[64,2048]{1,0:T(8,128)(2,1)S(1)} %pad_maximum_fusion), channel_id=1, source_target_pairs={{0,16},{1,17},{2,18},{3,19},{4,20},{5,21},{6,22},{7,23},{8,24},{9,... | collective-permute-start | bytes 786440 | tf_op jit(solution)/shard_map/ppermute | solution.py:431
  30.5 6.8 %collective-permute-start.8 = (bf16[64,2048]{1,0:T(8,128)(2,1)S(1)}, bf16[64,2048]{1,0:T(8,128)(2,1)S(1)}, u32[]{:S(2)}, u32[]{:S(2)}) collective-permute-start(bf16[64,2048]{1,0:T(8,128)(2,1)S(1)} %pad_maximum_fusion), channel_id=1, source_target_pairs={{0,24},{1,25},{2,26},{3,27},{4,28},{5,29},{6,30},{7,31},{8,0},{9,1... | collective-permute-start | bytes 786440 | tf_op jit(solution)/shard_map/ppermute | solution.py:431
  31.9 22.1 %copy-start.1 = (bf16[2048,1024]{1,0:T(8,128)(2,1)S(1)}, bf16[2048,1024]{1,0:T(8,128)(2,1)}, u32[]{:S(2)}) copy-start(bf16[2048,1024]{1,0:T(8,128)(2,1)} %own.7) | copy-start | bytes 12582916
  34.3 11.4 %collective-permute-start.6 = (bf16[128,2048]{1,0:T(8,128)(2,1)S(1)}, bf16[128,2048]{1,0:T(8,128)(2,1)S(1)}, u32[]{:S(2)}, u32[]{:S(2)}) collective-permute-start(bf16[128,2048]{1,0:T(8,128)(2,1)S(1)} %constant_dynamic-update-slice_fusion.one), channel_id=1, source_target_pairs={{0,2},{1,3},{2,4},{3,5},{4,6},{5,7},{6,0},{7,1},{8,10},{9,11},{10,... | collective-permute-start | bytes 1572872 | tf_op jit(solution)/shard_map/ppermute | solution.py:435
  37.7 12.6 %collective-permute-start.10 = (bf16[128,2048]{1,0:T(8,128)(2,1)S(1)}, bf16[128,2048]{1,0:T(8,128)(2,1)S(1)}, u32[]{:S(2)}, u32[]{:S(2)}) collective-permute-start(bf16[128,2048]{1,0:T(8,128)(2,1)S(1)} %constant_dynamic-update-slice_fusion.2.two), channel_id=1, source_target_pairs={{0,6},{1,7},{2,0},{3,1},{4,2},{5,3},{6,4},{7,5},{8,14},{9,15},{10,... | collective-permute-start | bytes 1572872 | tf_op jit(solution)/shard_map/ppermute | solution.py:435
  43.6 15.6 %collective-permute-start.13 = (bf16[128,2048]{1,0:T(8,128)(2,1)S(1)}, bf16[128,2048]{1,0:T(8,128)(2,1)S(1)}, u32[]{:S(2)}, u32[]{:S(2)}) collective-permute-start(bf16[128,2048]{1,0:T(8,128)(2,1)S(1)} %constant_dynamic-update-slice_fusion.one), channel_id=1, source_target_pairs={{0,6},{1,7},{2,0},{3,1},{4,2},{5,3},{6,4},{7,5},{8,14},{9,15},{10,... | collective-permute-start | bytes 1572872 | tf_op jit(solution)/shard_map/ppermute | solution.py:436
  44.0 15.1 %collective-permute-start.12 = (bf16[128,2048]{1,0:T(8,128)(2,1)S(1)}, bf16[128,2048]{1,0:T(8,128)(2,1)S(1)}, u32[]{:S(2)}, u32[]{:S(2)}) collective-permute-start(bf16[128,2048]{1,0:T(8,128)(2,1)S(1)} %constant_dynamic-update-slice_fusion.2.two), channel_id=1, source_target_pairs={{0,2},{1,3},{2,4},{3,5},{4,6},{5,7},{6,0},{7,1},{8,10},{9,11},{10,... | collective-permute-start | bytes 1572872 | tf_op jit(solution)/shard_map/ppermute | solution.py:436
  45.6 16.1 %collective-permute-start.7 = (bf16[128,2048]{1,0:T(8,128)(2,1)S(1)}, bf16[128,2048]{1,0:T(8,128)(2,1)S(1)}, u32[]{:S(2)}, u32[]{:S(2)}) collective-permute-start(bf16[128,2048]{1,0:T(8,128)(2,1)S(1)} %collective-permute-done.6.one), channel_id=1, source_target_pairs={{0,2},{1,3},{2,4},{3,5},{4,6},{5,7},{6,0},{7,1},{8,10},{9,11},{10,... | collective-permute-start | bytes 1572872 | tf_op jit(solution)/shard_map/ppermute | solution.py:438
  50.3 11.4 %collective-permute-start.11 = (bf16[128,2048]{1,0:T(8,128)(2,1)S(1)}, bf16[128,2048]{1,0:T(8,128)(2,1)S(1)}, u32[]{:S(2)}, u32[]{:S(2)}) collective-permute-start(bf16[128,2048]{1,0:T(8,128)(2,1)S(1)} %collective-permute-done.10.two), channel_id=1, source_target_pairs={{0,6},{1,7},{2,0},{3,1},{4,2},{5,3},{6,4},{7,5},{8,14},{9,15},{10,... | collective-permute-start | bytes 1572872 | tf_op jit(solution)/shard_map/ppermute | solution.py:438

commit v9 on v8

--- a/solution.py
+++ b/solution.py
@@ -278,12 +278,17 @@
     stats[...] = score_block((one, two), own, other, target, offset)
 
 
-def last_score_kernel(offset, order, one, two, own, other, target, *refs):
+def rows_score_kernel(offset, begun, order, one, two, own, other, target, *refs):
     earlier, outgoing = refs[:-1], refs[-1]
-    blocks = [part[...] for part in earlier]
-    blocks.append(score_block((one, two), own, other, target, offset))
+    mine = score_block((one, two), own, other, target, offset)
+    if begun:
+        outgoing[...] = earlier[0][...]
+        blocks = [mine]
+    else:
+        outgoing[...] = jnp.zeros_like(outgoing)
+        blocks = [*(part[...] for part in earlier), mine]
     half = outgoing.shape[1] // 2
-    at = 0
+    at = begun
     for block in blocks:
         for s in range(0, block.shape[1], half):
             row = jnp.concatenate([block[0:1, s : s + half], block[1:2, s : s + half]], axis=1)
@@ -292,15 +297,17 @@
             at += 1
 
 
-def score(parts, own, other, target, offset, earlier=(), order=None):
+def score(parts, own, other, target, offset, earlier=(), order=None, begun=0):
     size, width = parts[0].shape
     rows, cols = 2 * size, own.shape[1]
     near = pl.BlockSpec(memory_space=pltpu.VMEM)
     last = order is not None
-    kernel = last_score_kernel if last else score_kernel
+    kernel = functools.partial(score_kernel, offset)
+    if last:
+        kernel = functools.partial(rows_score_kernel, offset, begun)
     shape = (DEVICES, 2 * rows * 4 // GROUPS) if last else (8, rows)
     return pl.pallas_call(
-        functools.partial(kernel, offset),
+        kernel,
         grid_spec=pltpu.PrefetchScalarGridSpec(
             num_scalar_prefetch=int(last),
             grid=(),
@@ -314,7 +321,7 @@
             bytes_accessed=2 * width * (2 * cols + rows),
             transcendentals=2 * rows * cols,
         ),
-        name="last_score" if last else "score",
+        name="rows_score" if last else "score",
     )(*([order] if last else []), *parts, own, other, target, *earlier)
 
 
@@ -436,12 +443,17 @@
     forth_two, back_one = send(two, perm=FAR[0]), send(one, perm=FAR[1])
     own_head = lm_head
     halves = [send(forth_one, perm=FAR[0]), send(back_two, perm=FAR[1])]
-    stats = []
-    arrivals = ((one, two), (forth_one, back_two), (forth_two, back_one))
-    for i, parts in enumerate(arrivals):
-        stats.append(score(parts, own_head, far_head, wanted, 2 * size * i))
-        wanted, stats[i] = lax.optimization_barrier((wanted, stats[i]))
-    outgoing = score(halves, own_head, far_head, wanted, 6 * size, stats, order)
+    near = score((one, two), own_head, far_head, wanted, 0)
+    wanted, near = lax.optimization_barrier((wanted, near))
+    side = score((forth_one, back_two), own_head, far_head, wanted, 2 * size)
+    wanted, side = lax.optimization_barrier((wanted, side))
+    outgoing = score(
+        (forth_two, back_one), own_head, far_head, wanted, 4 * size, (near, side), order
+    )
+    begun = 3 * (2 * size // block)
+    outgoing = score(
+        halves, own_head, far_head, wanted, 6 * size, (outgoing,), order, begun
+    )
     incoming = lax.all_to_all(outgoing, AXES, 0, 0, tiled=True)
     return finish_scores(incoming, marks).T
 

time: 84.1 us -> 84.1 us (level)
  no operation moved by 1% of the time
where the time goes in v9:
time: 84.1 us; the launch traced here: 83.3 us
  Pallas kernels  26.8 us (32%)
  starting transfers between devices  24.2 us (29%)
  blocking collectives  16.9 us (20%)
  waiting for transfers between devices  9.91 us (12%)
  other arithmetic  2.95 us (4%)
  local copies, waits for them, and re-layouts  2.36 us (3%)
    all_to_all x1, blocking collectives, per_device(): incoming = lax.all_to_all(outgoing, AXES, 0, 0, tiled=True)  16.9 us
    pallas_call x1, Pallas kernels, front(): pl.pallas_call(front_kernel, grid_spec=pltpu.PrefetchScalarGridSpec(num_s...  12.1 us
    pallas_call x4, Pallas kernels, score(): pl.pallas_call(kernel, grid_spec=pltpu.PrefetchScalarGridSpec(num_scalar_...  11.6 us
    ppermute x2, starting transfers between devices, per_device(): forth_one, back_two = (send(one, perm=FAR[0]), send(two, perm=FAR[1]))  7.86 us
    ppermute x3, starting transfers between devices, per_device(): ahead, behind, across = [send(both, perm=p) for p in NEAR]  5.9 us
    ppermute x2, waiting for transfers between devices, per_device(): forth_one, back_two = (send(one, perm=FAR[0]), send(two, perm=FAR[1]))  4.64 us
    ppermute x3, starting transfers between devices, per_device(): send(pair, perm=p)  4.19 us
    ppermute x2, starting transfers between devices, per_device(): halves = [send(forth_one, perm=FAR[0]), send(back_two, perm=FAR[1])]  3.72 us
  transfers between devices with their start and end apart: 14, of which 6 were waited for; matrix products, arithmetic and copies ran while one was open for 6% of the time, Pallas kernels for 27%

profile of v9, /device:TPU:0, one launch (start us, length us, event | category | flops | bytes accessed | tf_op | source)
XLA Modules:
  0.0 83.3 jit_solution(9126638176574931251)
XLA Ops:
  0.0 12.1 %front.1 = (bf16[32,2048]{1,0:T(8,128)(2,1)}, f32[32,2048]{1,0:T(8,128)}) custom-call(f32[32]{0:T(128)} %rate.1, f32[32]{0:T(128)} %offset.1, bf16[4,16,2048]{2,1,0:T(8,128)(2,1)} %embedded.1, bf16[16,8,128,128]{3,2,1,0:T(8,128)(2,1)} %states.1, bf16[2048,512]{1,0:T(8,128)(2,1)} %w_query.1, bf16[2048,512]{1,0:T(8,128)(2,1)} %w_key.1, ...), custom_call_target="tpu_custom_call" | custom-call | flops 1073741824 | bytes 22020096 | tf_op jit(solution)/shard_map/front/pallas_call | solution.py:206
  12.1 0.5 collective-permute-start
  12.6 1.2 %collective-permute-done = bf16[32,2048]{1,0:T(8,128)(2,1)S(1)} collective-permute-done((bf16[32,2048]{1,0:T(8,128)(2,1)}, bf16[32,2048]{1,0:T(8,128)(2,1)S(1)}, u32[]{:S(2)}, u32[]{:S(2)}) %collective-permute-start) | collective-permute-done | bytes 131104 | tf_op jit(solution)/shard_map/ppermute | solution.py:420
  13.8 1.0 %add_convert_fusion = bf16[32,2048]{1,0:T(8,128)(2,1)S(1)} fusion(f32[32,2048]{1,0:T(8,128)} %get-tuple-element.23, bf16[32,2048]{1,0:T(8,128)(2,1)S(1)} %collective-permute-done), kind=kLoop, calls=%fused_computation.8 | loop fusion | flops 196608 | bytes 524288 | tf_op jit(solution)/shard_map/convert_element_type | solution.py:420
  14.8 2.9 %collective-permute-start.4 = (bf16[32,2048]{1,0:T(8,128)(2,1)S(1)}, bf16[32,2048]{1,0:T(8,128)(2,1)S(1)}, u32[]{:S(2)}, u32[]{:S(2)}) collective-permute-start(bf16[32,2048]{1,0:T(8,128)(2,1)S(1)} %add_convert_fusion), channel_id=1, source_target_pairs={{0,65},{1,64},{2,67},{3,66},{4,69},{5,68},{6,71},{7,70},{8,73},{9,... | collective-permute-start | bytes 393224 | tf_op jit(solution)/shard_map/ppermute | solution.py:427
  17.7 0.8 collective-permute-start.3
  18.5 0.5 collective-permute-start.1
  19.1 0.7 fusion
  19.8 0.6 gather_fusion
  20.4 0.7 compare_and_fusion
  21.3 0.8 dynamic-slice_bitcast_fusion.1.marks
  22.0 0.7 fusion.1.order
  22.8 2.5 %collective-permute-done.1 = bf16[32,2048]{1,0:T(8,128)(2,1)S(1)} collective-permute-done((bf16[32,2048]{1,0:T(8,128)(2,1)S(1)}, bf16[32,2048]{1,0:T(8,128)(2,1)S(1)}, u32[]{:S(2)}, u32[]{:S(2)}) %collective-permute-start.1) | collective-permute-done | bytes 131104 | tf_op jit(solution)/shard_map/ppermute | solution.py:427
  25.6 0.2 multiply_reduce_fusion
  25.9 1.6 %collective-permute-start.5 = (bf16[64,2048]{1,0:T(8,128)(2,1)S(1)}, bf16[64,2048]{1,0:T(8,128)(2,1)S(1)}, u32[]{:S(2)}, u32[]{:S(2)}) collective-permute-start(bf16[64,2048]{1,0:T(8,128)(2,1)S(1)} %pad_maximum_fusion), channel_id=1, source_target_pairs={{0,8},{1,9},{2,10},{3,11},{4,12},{5,13},{6,14},{7,15},{8,16},{9,17... | collective-permute-start | bytes 786440 | tf_op jit(solution)/shard_map/ppermute | solution.py:438
  27.6 2.9 %collective-permute-start.9 = (bf16[64,2048]{1,0:T(8,128)(2,1)S(1)}, bf16[64,2048]{1,0:T(8,128)(2,1)S(1)}, u32[]{:S(2)}, u32[]{:S(2)}) collective-permute-start(bf16[64,2048]{1,0:T(8,128)(2,1)S(1)} %pad_maximum_fusion), channel_id=1, source_target_pairs={{0,16},{1,17},{2,18},{3,19},{4,20},{5,21},{6,22},{7,23},{8,24},{9,... | collective-permute-start | bytes 786440 | tf_op jit(solution)/shard_map/ppermute | solution.py:438
  30.5 1.3 %collective-permute-start.8 = (bf16[64,2048]{1,0:T(8,128)(2,1)S(1)}, bf16[64,2048]{1,0:T(8,128)(2,1)S(1)}, u32[]{:S(2)}, u32[]{:S(2)}) collective-permute-start(bf16[64,2048]{1,0:T(8,128)(2,1)S(1)} %pad_maximum_fusion), channel_id=1, source_target_pairs={{0,24},{1,25},{2,26},{3,27},{4,28},{5,29},{6,30},{7,31},{8,0},{9,1... | collective-permute-start | bytes 786440 | tf_op jit(solution)/shard_map/ppermute | solution.py:438
  31.9 2.3 %bring_in.1.other = bf16[2048,1024]{1,0:T(8,128)(2,1)S(1)} custom-call(bf16[2048,1024]{1,0:T(8,128)(2,1)} %collective-permute-done.2.source), custom_call_target="tpu_custom_call" | custom-call | bytes 4194304 | tf_op jit(solution)/shard_map/bring_in/pallas_call | solution.py:363
  34.3 2.0 %collective-permute-start.6 = (bf16[128,2048]{1,0:T(8,128)(2,1)S(1)}, bf16[128,2048]{1,0:T(8,128)(2,1)S(1)}, u32[]{:S(2)}, u32[]{:S(2)}) collective-permute-start(bf16[128,2048]{1,0:T(8,128)(2,1)S(1)} %constant_dynamic-update-slice_fusion.one), channel_id=1, source_target_pairs={{0,2},{1,3},{2,4},{3,5},{4,6},{5,7},{6,0},{7,1},{8,10},{9,11},{10,... | collective-permute-start | bytes 1572872 | tf_op jit(solution)/shard_map/ppermute | solution.py:442
  36.3 1.0 %collective-permute-done.8 = bf16[64,2048]{1,0:T(8,128)(2,1)S(1)} collective-permute-done((bf16[64,2048]{1,0:T(8,128)(2,1)S(1)}, bf16[64,2048]{1,0:T(8,128)(2,1)S(1)}, u32[]{:S(2)}, u32[]{:S(2)}) %collective-permute-start.8) | collective-permute-done | bytes 262176 | tf_op jit(solution)/shard_map/ppermute | solution.py:438
  37.3 0.4 collective-permute-done.9
  37.7 5.9 %collective-permute-start.10 = (bf16[128,2048]{1,0:T(8,128)(2,1)S(1)}, bf16[128,2048]{1,0:T(8,128)(2,1)S(1)}, u32[]{:S(2)}, u32[]{:S(2)}) collective-permute-start(bf16[128,2048]{1,0:T(8,128)(2,1)S(1)} %constant_dynamic-update-slice_fusion.2.two), channel_id=1, source_target_pairs={{0,6},{1,7},{2,0},{3,1},{4,2},{5,3},{6,4},{7,5},{8,14},{9,15},{10,... | collective-permute-start | bytes 1572872 | tf_op jit(solution)/shard_map/ppermute | solution.py:442
  43.6 0.4 collective-permute-start.13
  44.0 1.6 %collective-permute-start.12 = (bf16[128,2048]{1,0:T(8,128)(2,1)S(1)}, bf16[128,2048]{1,0:T(8,128)(2,1)S(1)}, u32[]{:S(2)}, u32[]{:S(2)}) collective-permute-start(bf16[128,2048]{1,0:T(8,128)(2,1)S(1)} %constant_dynamic-update-slice_fusion.2.two), channel_id=1, source_target_pairs={{0,2},{1,3},{2,4},{3,5},{4,6},{5,7},{6,0},{7,1},{8,10},{9,11},{10,... | collective-permute-start | bytes 1572872 | tf_op jit(solution)/shard_map/ppermute | solution.py:443
  45.7 4.6 %collective-permute-done.10.two = bf16[128,2048]{1,0:T(8,128)(2,1)S(1)} collective-permute-done((bf16[128,2048]{1,0:T(8,128)(2,1)S(1)}, bf16[128,2048]{1,0:T(8,128)(2,1)S(1)}, u32[]{:S(2)}, u32[]{:S(2)}) %collective-permute-start.10) | collective-permute-done | bytes 524320 | tf_op jit(solution)/shard_map/ppermute | solution.py:442
  50.3 3.7 %collective-permute-start.11 = (bf16[128,2048]{1,0:T(8,128)(2,1)S(1)}, bf16[128,2048]{1,0:T(8,128)(2,1)S(1)}, u32[]{:S(2)}, u32[]{:S(2)}) collective-permute-start(bf16[128,2048]{1,0:T(8,128)(2,1)S(1)} %collective-permute-done.10.two), channel_id=1, source_target_pairs={{0,6},{1,7},{2,0},{3,1},{4,2},{5,3},{6,4},{7,5},{8,14},{9,15},{10,... | collective-permute-start | bytes 1572872 | tf_op jit(solution)/shard_map/ppermute | solution.py:445
  54.0 2.6 %score.2.refs_0_ = f32[8,256]{1,0:T(8,128)S(1)} custom-call(bf16[128,2048]{1,0:T(8,128)(2,1)S(1)} %constant_dynamic-update-slice_fusion.one, bf16[128,2048]{1,0:T(8,128)(2,1)S(1)} %constant_dynamic-update-slice_fusion.2.two, bf16[2048,1024]{1,0:T(8,128)(2,1)S(1)} %copy-done.1, bf16[2048,1024]{1,0:T(8,128)(2,1)S(1)} %bring_in.1.other, ...), custom_call_target="tpu_custom_call" | custom-call | flops 2147483648 | bytes 9437184 | tf_op jit(solution)/shard_map/score/pallas_call | solution.py:309
  56.6 2.6 %score.3.refs_1_ = f32[8,256]{1,0:T(8,128)S(1)} custom-call(bf16[128,2048]{1,0:T(8,128)(2,1)S(1)} %collective-permute-done.6.one, bf16[128,2048]{1,0:T(8,128)(2,1)S(1)} %collective-permute-done.10.two, bf16[2048,1024]{1,0:T(8,128)(2,1)S(1)} %copy-done.1, bf16[2048,1024]{1,0:T(8,128)(2,1)S(1)} %bring_in.1.other, s32[1,1024]{1,0:T(1,128)S(1)} %reshape.60.target), custom_call_target="tpu_custom_call" | custom-call | flops 2147483648 | bytes 9437184 | tf_op jit(solution)/shard_map/score/pallas_call | solution.py:309
  59.2 3.2 %rows_score.2.refs_0_ = f32[128,64]{1,0:T(8,128)S(1)} custom-call(s32[32]{0:T(128)S(1)} %fusion.1.order, bf16[128,2048]{1,0:T(8,128)(2,1)S(1)} %collective-permute-done.12.one, bf16[128,2048]{1,0:T(8,128)(2,1)S(1)} %collective-permute-done.13.two, bf16[2048,1024]{1,0:T(8,128)(2,1)S(1)} %copy-done.1, bf16[2048,1024]{1,0:T(8,128)(2,1)S(1)} %bring_in.1.other, ...), custom_call_target="tpu_custom_call" | custom-call | flops 2147483648 | bytes 9437184 | tf_op jit(solution)/shard_map/rows_score/pallas_call | solution.py:309
  62.5 3.2 %rows_score.3 = f32[128,64]{1,0:T(8,128)S(1)} custom-call(s32[32]{0:T(128)S(1)} %fusion.1.order, bf16[128,2048]{1,0:T(8,128)(2,1)S(1)} %collective-permute-done.7.one, bf16[128,2048]{1,0:T(8,128)(2,1)S(1)} %collective-permute-done.11.two, bf16[2048,1024]{1,0:T(8,128)(2,1)S(1)} %copy-done.1, bf16[2048,1024]{1,0:T(8,128)(2,1)S(1)} %bring_in.1.other, ...), custom_call_target="tpu_custom_call" | custom-call | flops 2147483648 | bytes 9437184 | tf_op jit(solution)/shard_map/rows_score/pallas_call | solution.py:309
  65.7 16.9 %all_to_all.11 = f32[128,1,64]{2,1,0:T(1,128)S(1)} all-to-all(f32[128,1,64]{2,1,0:T(1,128)S(1)} %bitcast.22), channel_id=1, replica_groups=mesh['xl'=2,'c'=2,'y'=4,'z'=4,'xh'=2] {'xl','c','y','z','xh'}, dimensions={0} | all-to-all | bytes 65536 | tf_op jit(solution)/shard_map/all_to_all | solution.py:457
  82.6 0.7 finish.1
  (32 shorter events, 0.9 us)
Async XLA Ops:
  0.0 19.0 %copy-start = (s32[512,4]{0,1:T(4,128)S(1)}, s32[512,4]{0,1:T(4,128)}, u32[]{:S(2)}) copy-start(s32[512,4]{0,1:T(4,128)} %param.33) | copy-start | bytes 24580
  0.0 25.9 %collective-permute-start.2 = (bf16[2048,1024]{1,0:T(8,128)(2,1)}, bf16[2048,1024]{1,0:T(8,128)(2,1)}, u32[]{:S(2)}, u32[]{:S(2)}) collective-permute-start(bf16[2048,1024]{1,0:T(8,128)(2,1)} %own.7), channel_id=1, source_target_pairs={{0,32},{1,33},{2,34},{3,35},{4,36},{5,37},{6,38},{7,39},{8,40},{9,... | collective-permute-start | bytes 12582920 | tf_op jit(solution)/shard_map/ppermute | solution.py:401
  0.0 25.8 %copy-start.2 = (f32[2048]{0:T(1024)S(1)}, f32[2048]{0:T(1024)}, u32[]{:S(2)}) copy-start(f32[2048]{0:T(1024)} %param.31) | copy-start | bytes 24580
  12.1 1.7 %collective-permute-start = (bf16[32,2048]{1,0:T(8,128)(2,1)}, bf16[32,2048]{1,0:T(8,128)(2,1)S(1)}, u32[]{:S(2)}, u32[]{:S(2)}) collective-permute-start(bf16[32,2048]{1,0:T(8,128)(2,1)} %get-tuple-element.24), channel_id=1, source_target_pairs={{0,32},{1,33},{2,34},{3,35},{4,36},{5,37},{6,38},{7,39},{8,40},{9,... | collective-permute-start | bytes 393224 | tf_op jit(solution)/shard_map/ppermute | solution.py:420
  14.8 10.6 %collective-permute-start.4 = (bf16[32,2048]{1,0:T(8,128)(2,1)S(1)}, bf16[32,2048]{1,0:T(8,128)(2,1)S(1)}, u32[]{:S(2)}, u32[]{:S(2)}) collective-permute-start(bf16[32,2048]{1,0:T(8,128)(2,1)S(1)} %add_convert_fusion), channel_id=1, source_target_pairs={{0,65},{1,64},{2,67},{3,66},{4,69},{5,68},{6,71},{7,70},{8,73},{9,... | collective-permute-start | bytes 393224 | tf_op jit(solution)/shard_map/ppermute | solution.py:427
  17.7 7.9 %collective-permute-start.3 = (bf16[32,2048]{1,0:T(8,128)(2,1)S(1)}, bf16[32,2048]{1,0:T(8,128)(2,1)S(1)}, u32[]{:S(2)}, u32[]{:S(2)}) collective-permute-start(bf16[32,2048]{1,0:T(8,128)(2,1)S(1)} %add_convert_fusion), channel_id=1, source_target_pairs={{0,1},{1,0},{2,3},{3,2},{4,5},{5,4},{6,7},{7,6},{8,9},{9,8},{10,11... | collective-permute-start | bytes 393224 | tf_op jit(solution)/shard_map/ppermute | solution.py:427
  18.5 6.8 %collective-permute-start.1 = (bf16[32,2048]{1,0:T(8,128)(2,1)S(1)}, bf16[32,2048]{1,0:T(8,128)(2,1)S(1)}, u32[]{:S(2)}, u32[]{:S(2)}) collective-permute-start(bf16[32,2048]{1,0:T(8,128)(2,1)S(1)} %add_convert_fusion), channel_id=1, source_target_pairs={{0,64},{1,65},{2,66},{3,67},{4,68},{5,69},{6,70},{7,71},{8,72},{9,... | collective-permute-start | bytes 393224 | tf_op jit(solution)/shard_map/ppermute | solution.py:427
  25.9 8.3 %collective-permute-start.5 = (bf16[64,2048]{1,0:T(8,128)(2,1)S(1)}, bf16[64,2048]{1,0:T(8,128)(2,1)S(1)}, u32[]{:S(2)}, u32[]{:S(2)}) collective-permute-start(bf16[64,2048]{1,0:T(8,128)(2,1)S(1)} %pad_maximum_fusion), channel_id=1, source_target_pairs={{0,8},{1,9},{2,10},{3,11},{4,12},{5,13},{6,14},{7,15},{8,16},{9,17... | collective-permute-start | bytes 786440 | tf_op jit(solution)/shard_map/ppermute | solution.py:438
  27.6 10.1 %collective-permute-start.9 = (bf16[64,2048]{1,0:T(8,128)(2,1)S(1)}, bf16[64,2048]{1,0:T(8,128)(2,1)S(1)}, u32[]{:S(2)}, u32[]{:S(2)}) collective-permute-start(bf16[64,2048]{1,0:T(8,128)(2,1)S(1)} %pad_maximum_fusion), channel_id=1, source_target_pairs={{0,16},{1,17},{2,18},{3,19},{4,20},{5,21},{6,22},{7,23},{8,24},{9,... | collective-permute-start | bytes 786440 | tf_op jit(solution)/shard_map/ppermute | solution.py:438
  30.5 6.8 %collective-permute-start.8 = (bf16[64,2048]{1,0:T(8,128)(2,1)S(1)}, bf16[64,2048]{1,0:T(8,128)(2,1)S(1)}, u32[]{:S(2)}, u32[]{:S(2)}) collective-permute-start(bf16[64,2048]{1,0:T(8,128)(2,1)S(1)} %pad_maximum_fusion), channel_id=1, source_target_pairs={{0,24},{1,25},{2,26},{3,27},{4,28},{5,29},{6,30},{7,31},{8,0},{9,1... | collective-permute-start | bytes 786440 | tf_op jit(solution)/shard_map/ppermute | solution.py:438
  31.9 22.1 %copy-start.1 = (bf16[2048,1024]{1,0:T(8,128)(2,1)S(1)}, bf16[2048,1024]{1,0:T(8,128)(2,1)}, u32[]{:S(2)}) copy-start(bf16[2048,1024]{1,0:T(8,128)(2,1)} %own.7) | copy-start | bytes 12582916
  34.3 11.4 %collective-permute-start.6 = (bf16[128,2048]{1,0:T(8,128)(2,1)S(1)}, bf16[128,2048]{1,0:T(8,128)(2,1)S(1)}, u32[]{:S(2)}, u32[]{:S(2)}) collective-permute-start(bf16[128,2048]{1,0:T(8,128)(2,1)S(1)} %constant_dynamic-update-slice_fusion.one), channel_id=1, source_target_pairs={{0,2},{1,3},{2,4},{3,5},{4,6},{5,7},{6,0},{7,1},{8,10},{9,11},{10,... | collective-permute-start | bytes 1572872 | tf_op jit(solution)/shard_map/ppermute | solution.py:442
  37.7 12.6 %collective-permute-start.10 = (bf16[128,2048]{1,0:T(8,128)(2,1)S(1)}, bf16[128,2048]{1,0:T(8,128)(2,1)S(1)}, u32[]{:S(2)}, u32[]{:S(2)}) collective-permute-start(bf16[128,2048]{1,0:T(8,128)(2,1)S(1)} %constant_dynamic-update-slice_fusion.2.two), channel_id=1, source_target_pairs={{0,6},{1,7},{2,0},{3,1},{4,2},{5,3},{6,4},{7,5},{8,14},{9,15},{10,... | collective-permute-start | bytes 1572872 | tf_op jit(solution)/shard_map/ppermute | solution.py:442
  43.6 15.6 %collective-permute-start.13 = (bf16[128,2048]{1,0:T(8,128)(2,1)S(1)}, bf16[128,2048]{1,0:T(8,128)(2,1)S(1)}, u32[]{:S(2)}, u32[]{:S(2)}) collective-permute-start(bf16[128,2048]{1,0:T(8,128)(2,1)S(1)} %constant_dynamic-update-slice_fusion.one), channel_id=1, source_target_pairs={{0,6},{1,7},{2,0},{3,1},{4,2},{5,3},{6,4},{7,5},{8,14},{9,15},{10,... | collective-permute-start | bytes 1572872 | tf_op jit(solution)/shard_map/ppermute | solution.py:443
  44.0 15.2 %collective-permute-start.12 = (bf16[128,2048]{1,0:T(8,128)(2,1)S(1)}, bf16[128,2048]{1,0:T(8,128)(2,1)S(1)}, u32[]{:S(2)}, u32[]{:S(2)}) collective-permute-start(bf16[128,2048]{1,0:T(8,128)(2,1)S(1)} %constant_dynamic-update-slice_fusion.2.two), channel_id=1, source_target_pairs={{0,2},{1,3},{2,4},{3,5},{4,6},{5,7},{6,0},{7,1},{8,10},{9,11},{10,... | collective-permute-start | bytes 1572872 | tf_op jit(solution)/shard_map/ppermute | solution.py:443
  45.6 16.8 %collective-permute-start.7 = (bf16[128,2048]{1,0:T(8,128)(2,1)S(1)}, bf16[128,2048]{1,0:T(8,128)(2,1)S(1)}, u32[]{:S(2)}, u32[]{:S(2)}) collective-permute-start(bf16[128,2048]{1,0:T(8,128)(2,1)S(1)} %collective-permute-done.6.one), channel_id=1, source_target_pairs={{0,2},{1,3},{2,4},{3,5},{4,6},{5,7},{6,0},{7,1},{8,10},{9,11},{10,... | collective-permute-start | bytes 1572872 | tf_op jit(solution)/shard_map/ppermute | solution.py:445
  50.3 12.2 %collective-permute-start.11 = (bf16[128,2048]{1,0:T(8,128)(2,1)S(1)}, bf16[128,2048]{1,0:T(8,128)(2,1)S(1)}, u32[]{:S(2)}, u32[]{:S(2)}) collective-permute-start(bf16[128,2048]{1,0:T(8,128)(2,1)S(1)} %collective-permute-done.10.two), channel_id=1, source_target_pairs={{0,6},{1,7},{2,0},{3,1},{4,2},{5,3},{6,4},{7,5},{8,14},{9,15},{10,... | collective-permute-start | bytes 1572872 | tf_op jit(solution)/shard_map/ppermute | solution.py:445
